TPU v7x, 32 devices: a whole 2x2x4 slice. The times are simulated.
32 devices in a mesh: fsdp: 4 (over x, core), seq: 8 (over z, y).
Axes of the slice: x: 2, y: 2, z: 4, core: 2. Of those that a mesh axis runs over, the one named last changes fastest.
Arguments:
- residual: bfloat16 [4, 2048, 1024], P('fsdp', 'seq'), may hold values from -6 to 6
- out_cotangent: bfloat16 [4, 2048, 1024], P('fsdp', 'seq'), may hold values from -6 to 6
- doc_lengths: int32 [4, 8], P('fsdp'), may hold values from 1 to 1024, 2048 in all within a row
- norm_gain: bfloat16 [1024], P('fsdp'), may hold values from 0.5 to 1.5
- input_proj: bfloat16 [1024, 4096], P('fsdp'), may hold values from -0.1875 to 0.1875
- conv_kernel: bfloat16 [4, 2048], P(None, 'fsdp'), may hold values from -3 to 3
- conv_bias: bfloat16 [2048], P('fsdp'), may hold values from -3 to 3
- select_proj: bfloat16 [2048, 96], P('fsdp'), may hold values from -0.125 to 0.125
- step_proj: bfloat16 [64, 2048], P(None, 'fsdp'), may hold values from -0.75 to 0.75
- step_bias: bfloat16 [2048], P('fsdp'), may hold values from -6 to -1
- log_decay: bfloat16 [16, 2048], P(None, 'fsdp'), may hold values from -2 to 2.5
- skip_gain: bfloat16 [2048], P('fsdp'), may hold values from 0.5 to 1.5
- output_proj: bfloat16 [2048, 1024], P('fsdp'), may hold values from -0.25 to 0.25
Outputs:
- layer_output: bfloat16 [4, 2048, 1024], P('fsdp', 'seq')
- residual_grad: float32 [4, 2048, 1024], P('fsdp', 'seq')
- norm_gain_grad: float32 [1024], P('fsdp')
- input_proj_grad: float32 [1024, 4096], P('fsdp')
- conv_kernel_grad: float32 [4, 2048], P(None, 'fsdp')
- conv_bias_grad: float32 [2048], P('fsdp')
- select_proj_grad: float32 [2048, 96], P('fsdp')
- step_proj_grad: float32 [64, 2048], P(None, 'fsdp')
- step_bias_grad: float32 [2048], P('fsdp')
- log_decay_grad: float32 [16, 2048], P(None, 'fsdp')
- skip_gain_grad: float32 [2048], P('fsdp')
- output_proj_grad: float32 [2048, 1024], P('fsdp')
Inputs may be any that keep to these rules, and one draw needn't show every extreme that they name: `doc_lengths`: each row's 8 lengths sum to 2048, and its longest is exactly 1024.
All inputs are finite; a program needn't handle non-finite values.
Results may differ from a plain program's by a relative error of at most 0.012.
The roundings to bfloat16 on the way count: a program that leaves them out, or rounds other values in their place, can miss the bound.
Values may be sent and summed in bfloat16 or wider, within the bound.
A program may use at most 128 MiB of HBM per device.

v0:
```python
from functools import partial

import jax
import jax.numpy as jnp
from jax import lax
from jax.sharding import PartitionSpec as P

BLOCK = 32


EPS = 1e-05


def from_behind(block, axis, distance):
    devices = range(lax.axis_size(axis))
    route = [(i - distance, i) for i in devices if i - distance in devices]
    return lax.ppermute(block, axis, route)


def entering(part, axis, combine, identity, reverse):
    count = lax.axis_size(axis)
    place = lax.axis_index(axis)
    ahead = count - 1 - place if reverse else place
    gathered = jax.tree.map(lambda a: lax.all_gather(a, axis), part)
    state = jax.tree.map(lambda a, e: jnp.zeros_like(a) + jnp.asarray(e, a.dtype), part, identity)

    def one(turn, state):
        source = count - 1 - turn if reverse else turn
        return combine(
            state, jax.tree.map(lambda a: lax.dynamic_index_in_dim(a, source, 0, False), gathered)
        )

    return lax.fori_loop(0, ahead, one, state)


def combine_pairs(first, second):
    return (first[0] * second[0], second[0] * first[1] + second[1])


def doc_marks(lengths, first, count):
    starts = jnp.cumsum(lengths, axis=1) - lengths
    place = first + jnp.arange(count, dtype=jnp.int32)
    ident = jnp.sum((starts[:, None, :] <= place[None, :, None]).astype(jnp.int32), axis=2)
    begin = jnp.any(starts[:, None, :] == place[None, :, None], axis=2).astype(jnp.float32)
    return (ident, begin)


def to_blocks(value, block):
    rows, count = (value.shape[0], value.shape[1])
    return jnp.moveaxis(value.reshape((rows, count // block, block) + value.shape[2:]), 1, 0)


def from_blocks(value):
    blocks, rows, block = (value.shape[0], value.shape[1], value.shape[2])
    return jnp.moveaxis(value, 0, 1).reshape((rows, blocks * block) + value.shape[3:])


def position_first(value):
    return jnp.swapaxes(value, 0, 1)


def rows_inner(left, right):
    return lax.dot_general(
        left, right, (((0,), (0,)), ((), ())), preferred_element_type=jnp.float32
    )


def times_transposed(left, right):
    return lax.dot_general(
        left, right, (((1,), (1,)), ((), ())), preferred_element_type=jnp.float32
    )


def silu_slope(value):
    sig = jax.nn.sigmoid(value)
    return sig * (1.0 + value * (1.0 - sig))


def conv_apply(extended, same, kernel, kbias):
    taps = kernel.shape[0]
    count = extended.shape[1] - taps + 1
    kernel_f = kernel.astype(jnp.float32)
    total = jnp.broadcast_to(
        kbias.astype(jnp.float32), (extended.shape[0], count, extended.shape[2])
    )
    for k in range(taps):
        total = total + kernel_f[k] * extended[:, k : k + count, :].astype(jnp.float32) * same[k]
    return total


def weighted_total(rate, spans, mask, left, right):
    rows, inner = (spans.shape[0], spans.shape[2])

    def add_block(total, item):
        span_b, mask_b, left_b, right_b = item
        weight = jnp.exp(span_b[:, :, None, :] * rate) * mask_b[:, :, None, None]
        return (
            total + jnp.sum(weight * left_b[:, :, :, None] * right_b[:, :, None, :], axis=1),
            None,
        )

    start = jnp.zeros((rows, rate.shape[0], inner), jnp.float32)
    total, unused = lax.scan(
        add_block,
        start,
        (
            to_blocks(spans, BLOCK),
            to_blocks(mask, BLOCK),
            to_blocks(left, BLOCK),
            to_blocks(right, BLOCK),
        ),
    )
    return total


def advance_states(state, step_t, enter_t, mixed_t, keep_t, rate):

    def advance_advance(current, item):
        step_p, enter_p, mixed_p, keep_p = item
        decay = jnp.exp(step_p[:, None, :] * rate) * keep_p[:, None, None]
        current = decay * current + step_p[:, None, :] * enter_p[:, :, None] * mixed_p[:, None, :]
        return (current, current)

    return lax.scan(advance_advance, state, (step_t, enter_t, mixed_t, keep_t))


def block_forward(state, item, rate):
    step_b, enter_b, read_b, mixed_b, keep_b = item
    step_t = position_first(step_b)
    enter_t = position_first(enter_b)
    read_t = position_first(read_b)
    mixed_t = position_first(mixed_b)
    keep_t = position_first(keep_b)

    def block_advance(current, item_p):
        step_p, enter_p, read_p, mixed_p, keep_p = item_p
        decay = jnp.exp(step_p[:, None, :] * rate) * keep_p[:, None, None]
        current = decay * current + step_p[:, None, :] * enter_p[:, :, None] * mixed_p[:, None, :]
        return (current, jnp.sum(read_p[:, :, None] * current, axis=1))

    final, outs = lax.scan(block_advance, state, (step_t, enter_t, read_t, mixed_t, keep_t))
    return (final, (position_first(outs), state))


def block_backward(carry, item, rate):
    later, rate_sum = carry
    start, step_b, enter_b, read_b, mixed_b, keep_b, dout_b = item
    step_t = position_first(step_b)
    enter_t = position_first(enter_b)
    read_t = position_first(read_b)
    mixed_t = position_first(mixed_b)
    keep_t = position_first(keep_b)
    dout_t = position_first(dout_b)
    unused, states = advance_states(start, step_t, enter_t, mixed_t, keep_t, rate)
    before = jnp.concatenate([start[None], states[:-1]], axis=0)

    def retreat(back, item_p):
        passed, total = back
        step_p, enter_p, read_p, mixed_p, keep_p, dout_p, prev_p, cur_p = item_p
        decay = jnp.exp(step_p[:, None, :] * rate) * keep_p[:, None, None]
        adjoint = read_p[:, :, None] * dout_p[:, None, :] + passed
        slope = adjoint * prev_p * decay
        pulled = jnp.sum(adjoint * enter_p[:, :, None], axis=1)
        grad_step = pulled * mixed_p + jnp.sum(slope * rate, axis=1)
        grad_mixed = pulled * step_p
        grad_enter = jnp.sum(adjoint * (step_p * mixed_p)[:, None, :], axis=2)
        grad_read = jnp.sum(cur_p * dout_p[:, None, :], axis=2)
        total = total + jnp.sum(slope * step_p[:, None, :], axis=0)
        return ((decay * adjoint, total), (grad_step, grad_mixed, grad_enter, grad_read))

    (passed, rate_sum), pieces = lax.scan(
        retreat,
        (later, rate_sum),
        (step_t, enter_t, read_t, mixed_t, keep_t, dout_t, before, states),
        reverse=True,
    )
    grad_step, grad_mixed, grad_enter, grad_read = pieces
    return (
        (passed, rate_sum),
        (
            position_first(grad_step),
            position_first(grad_mixed),
            position_first(grad_enter),
            position_first(grad_read),
        ),
    )


def shards(
    residual,
    out_cotangent,
    doc_lengths,
    norm_gain,
    input_proj,
    conv_kernel,
    conv_bias,
    select_proj,
    step_proj,
    step_bias,
    log_decay,
    skip_gain,
    output_proj,
):
    rows_dev, stretch, width = residual.shape
    full = (
        lax.all_gather(norm_gain, "fsdp", axis=0, tiled=True),
        lax.all_gather(input_proj, "fsdp", axis=0, tiled=True),
        lax.all_gather(conv_kernel, "fsdp", axis=1, tiled=True),
        lax.all_gather(conv_bias, "fsdp", axis=0, tiled=True),
        lax.all_gather(select_proj, "fsdp", axis=0, tiled=True),
        lax.all_gather(step_proj, "fsdp", axis=1, tiled=True),
        lax.all_gather(step_bias, "fsdp", axis=0, tiled=True),
        lax.all_gather(log_decay, "fsdp", axis=1, tiled=True),
        lax.all_gather(skip_gain, "fsdp", axis=0, tiled=True),
        lax.all_gather(output_proj, "fsdp", axis=0, tiled=True),
    )
    gain, w_in, kernel, kbias, w_sel, w_step, sbias, logd, skip, w_out = full
    inner = w_in.shape[1] // 2
    rank = w_step.shape[0]
    nstate = logd.shape[0]
    taps = kernel.shape[0]
    tokens = rows_dev * stretch
    flat = residual.reshape(tokens, width).astype(jnp.float32)
    gain_f = gain.astype(jnp.float32)
    scale = lax.rsqrt(jnp.mean(flat * flat, axis=1, keepdims=True) + EPS)
    normed = (flat * scale * gain_f).astype(jnp.bfloat16)
    both = jnp.dot(normed, w_in, preferred_element_type=jnp.float32).astype(jnp.bfloat16)
    inner_in = both[:, :inner].reshape(rows_dev, stretch, inner)
    gate_f = both[:, inner:].astype(jnp.float32)
    edge = from_behind(inner_in[:, stretch - (taps - 1) :, :], "seq", 1)
    extended = jnp.concatenate([edge, inner_in], axis=1)
    anchor = lax.axis_index("seq") * stretch
    ident, begin_ext = doc_marks(doc_lengths, anchor - (taps - 1), stretch + taps - 1)
    begin = begin_ext[:, taps - 1 :]
    keep = 1.0 - begin
    same = [
        (ident[:, k : k + stretch] == ident[:, taps - 1 :]).astype(jnp.float32)[:, :, None]
        for k in range(taps)
    ]
    conv = conv_apply(extended, same, kernel, kbias)
    mixed = jax.nn.silu(conv).astype(jnp.bfloat16).reshape(tokens, inner)
    mixed_f = mixed.astype(jnp.float32).reshape(rows_dev, stretch, inner)
    proj = jnp.dot(mixed, w_sel, preferred_element_type=jnp.float32)
    step_low = proj[:, :rank].astype(jnp.bfloat16)
    enter_coef = proj[:, rank : rank + nstate].reshape(rows_dev, stretch, nstate)
    read_coef = proj[:, rank + nstate :].reshape(rows_dev, stretch, nstate)
    step_pre = jnp.dot(step_low, w_step, preferred_element_type=jnp.float32) + sbias.astype(
        jnp.float32
    )
    step = jax.nn.softplus(step_pre).reshape(rows_dev, stretch, inner)
    rate = -jnp.exp(logd.astype(jnp.float32))
    position = jnp.arange(stretch, dtype=jnp.int32)
    last_start = jnp.max(jnp.where(begin > 0.5, position[None, :], 0), axis=1)
    first_start = jnp.min(jnp.where(begin > 0.5, position[None, :], stretch), axis=1)
    head = jnp.cumsum(step, axis=1)
    tail = jnp.flip(jnp.cumsum(jnp.flip(step, 1), axis=1), 1) - step
    whole = (jnp.max(begin, axis=1) < 0.5).astype(jnp.float32)
    prod_all = jnp.exp(rate[None] * head[:, -1][:, None, :]) * whole[:, None, None]
    after_mask = (position[None, :] >= last_start[:, None]).astype(jnp.float32)
    state_end = weighted_total(rate, tail, after_mask, enter_coef, step * mixed_f)
    carried = entering(
        (prod_all, state_end),
        "seq",
        combine_pairs,
        (jnp.ones_like(prod_all), jnp.zeros_like(state_end)),
        False,
    )
    final, (outs, starts) = lax.scan(
        partial(block_forward, rate=rate),
        carried[1],
        (
            to_blocks(step, BLOCK),
            to_blocks(enter_coef, BLOCK),
            to_blocks(read_coef, BLOCK),
            to_blocks(mixed_f, BLOCK),
            to_blocks(keep, BLOCK),
        ),
    )
    skip_f = skip.astype(jnp.float32)
    y_full = (from_blocks(outs) + skip_f * mixed_f).reshape(tokens, inner)
    gate_act = jax.nn.silu(gate_f)
    gated = (y_full * gate_act).astype(jnp.bfloat16)
    layer_output = (flat + jnp.dot(gated, w_out, preferred_element_type=jnp.float32)).astype(
        jnp.bfloat16
    )
    again = (
        lax.all_gather(norm_gain, "fsdp", axis=0, tiled=True),
        lax.all_gather(input_proj, "fsdp", axis=0, tiled=True),
        lax.all_gather(conv_kernel, "fsdp", axis=1, tiled=True),
        lax.all_gather(conv_bias, "fsdp", axis=0, tiled=True),
        lax.all_gather(select_proj, "fsdp", axis=0, tiled=True),
        lax.all_gather(step_proj, "fsdp", axis=1, tiled=True),
        lax.all_gather(step_bias, "fsdp", axis=0, tiled=True),
        lax.all_gather(log_decay, "fsdp", axis=1, tiled=True),
        lax.all_gather(skip_gain, "fsdp", axis=0, tiled=True),
        lax.all_gather(output_proj, "fsdp", axis=0, tiled=True),
    )
    gain_b, w_in_b, kernel_b, kbias_b, w_sel_b, w_step_b, sbias_b, logd_b, skip_b, w_out_b = again
    cotangent = out_cotangent.reshape(tokens, width)
    output_grad = rows_inner(gated, cotangent)
    d_gated = times_transposed(cotangent, w_out_b).astype(jnp.bfloat16).astype(jnp.float32)
    d_y = d_gated * gate_act
    d_gate = d_gated * y_full * silu_slope(gate_f)
    mixed_flat = mixed_f.reshape(tokens, inner)
    skip_grad = jnp.sum(d_y * mixed_flat, axis=0)
    d_y_rows = d_y.reshape(rows_dev, stretch, inner)
    before_mask = (position[None, :] < first_start[:, None]).astype(jnp.float32)
    adjoint_local = weighted_total(rate, head, before_mask, read_coef, d_y_rows)
    incoming = entering(
        (prod_all, adjoint_local),
        "seq",
        combine_pairs,
        (jnp.ones_like(prod_all), jnp.zeros_like(adjoint_local)),
        True,
    )
    carry_end, pieces = lax.scan(
        partial(block_backward, rate=rate),
        (incoming[1], jnp.zeros_like(rate)),
        (
            starts,
            to_blocks(step, BLOCK),
            to_blocks(enter_coef, BLOCK),
            to_blocks(read_coef, BLOCK),
            to_blocks(mixed_f, BLOCK),
            to_blocks(keep, BLOCK),
            to_blocks(d_y_rows, BLOCK),
        ),
        reverse=True,
    )
    rate_total = carry_end[1]
    log_decay_grad = rate_total * rate
    grad_step = from_blocks(pieces[0]).reshape(tokens, inner)
    grad_mixed = from_blocks(pieces[1]).reshape(tokens, inner)
    grad_enter = from_blocks(pieces[2]).reshape(tokens, nstate)
    grad_read = from_blocks(pieces[3]).reshape(tokens, nstate)
    d_pre = grad_step * jax.nn.sigmoid(step_pre)
    step_bias_grad = jnp.sum(d_pre, axis=0)
    d_lin = d_pre.astype(jnp.bfloat16)
    step_grad = rows_inner(step_low, d_lin)
    d_step_low = times_transposed(d_lin, w_step_b)
    d_proj = jnp.concatenate([d_step_low, grad_enter, grad_read], axis=1).astype(jnp.bfloat16)
    select_grad = rows_inner(mixed, d_proj)
    d_mixed = grad_mixed + d_y * skip_b.astype(jnp.float32) + times_transposed(d_proj, w_sel_b)
    d_conv = (d_mixed * silu_slope(conv.reshape(tokens, inner))).reshape(rows_dev, stretch, inner)
    conv_bias_grad = jnp.sum(d_conv, axis=(0, 1))
    kernel_f = kernel_b.astype(jnp.float32)
    kernel_rows = []
    d_ext = jnp.zeros((rows_dev, stretch + taps - 1, inner), jnp.float32)
    for k in range(taps):
        masked = d_conv * same[k]
        kernel_rows.append(
            jnp.sum(masked * extended[:, k : k + stretch, :].astype(jnp.float32), axis=(0, 1))
        )
        d_ext = d_ext + jnp.pad(kernel_f[k] * masked, ((0, 0), (k, taps - 1 - k), (0, 0)))
    kernel_grad = jnp.stack(kernel_rows, axis=0)
    back_edge = from_behind(d_ext[:, : taps - 1, :], "seq", -1)
    d_inner = d_ext[:, taps - 1 :, :] + jnp.pad(
        back_edge, ((0, 0), (stretch - (taps - 1), 0), (0, 0))
    )
    d_both = jnp.concatenate([d_inner.reshape(tokens, inner), d_gate], axis=1).astype(jnp.bfloat16)
    input_grad = rows_inner(normed, d_both)
    d_normed = times_transposed(d_both, w_in_b)
    hat = flat * scale
    gain_grad = jnp.sum(d_normed * hat, axis=0)
    d_hat = d_normed * gain_b.astype(jnp.float32)
    d_flat = scale * (d_hat - hat * jnp.mean(d_hat * hat, axis=1, keepdims=True))
    residual_grad = (cotangent.astype(jnp.float32) + d_flat).reshape(rows_dev, stretch, width)
    shares = (
        lax.psum_scatter(gain_grad, "fsdp", scatter_dimension=0, tiled=True),
        lax.psum_scatter(input_grad, "fsdp", scatter_dimension=0, tiled=True),
        lax.psum_scatter(kernel_grad, "fsdp", scatter_dimension=1, tiled=True),
        lax.psum_scatter(conv_bias_grad, "fsdp", scatter_dimension=0, tiled=True),
        lax.psum_scatter(select_grad, "fsdp", scatter_dimension=0, tiled=True),
        lax.psum_scatter(step_grad, "fsdp", scatter_dimension=1, tiled=True),
        lax.psum_scatter(step_bias_grad, "fsdp", scatter_dimension=0, tiled=True),
        lax.psum_scatter(log_decay_grad, "fsdp", scatter_dimension=1, tiled=True),
        lax.psum_scatter(skip_grad, "fsdp", scatter_dimension=0, tiled=True),
        lax.psum_scatter(output_grad, "fsdp", scatter_dimension=0, tiled=True),
    )
    summed = lax.psum(
        (
            shares[0],
            shares[1],
            shares[2],
            shares[3],
            shares[4],
            shares[5],
            shares[6],
            shares[7],
            shares[8],
            shares[9],
        ),
        "seq",
    )
    return (
        layer_output.reshape(rows_dev, stretch, width),
        residual_grad,
        summed[0],
        summed[1],
        summed[2],
        summed[3],
        summed[4],
        summed[5],
        summed[6],
        summed[7],
        summed[8],
        summed[9],
    )


def solution(mesh):
    in_specs = (
        P("fsdp", "seq", None),
        P("fsdp", "seq", None),
        P("fsdp", None),
        P("fsdp"),
        P("fsdp", None),
        P(None, "fsdp"),
        P("fsdp"),
        P("fsdp", None),
        P(None, "fsdp"),
        P("fsdp"),
        P(None, "fsdp"),
        P("fsdp"),
        P("fsdp", None),
    )
    out_specs = (
        P("fsdp", "seq", None),
        P("fsdp", "seq", None),
        P("fsdp"),
        P("fsdp", None),
        P(None, "fsdp"),
        P("fsdp"),
        P("fsdp", None),
        P(None, "fsdp"),
        P("fsdp"),
        P(None, "fsdp"),
        P("fsdp"),
        P("fsdp", None),
    )
    return jax.shard_map(shards, mesh=mesh, in_specs=in_specs, out_specs=out_specs, check_vma=False)
```

profile of v0, /device:TPU:0, one launch (start us, length us, event | category | flops | bytes accessed | tf_op | source)
XLA Modules:
  0.0 2991.4 jit_solution(16714517798567430962)
XLA Ops:
  8.8 6.0 all-gather.4
  15.2 5.5 all_gather.59
  20.7 7.3 all_gather.63
  31.4 9.9 all_gather.62
  41.5 32.7 %all-gather.13.cloned.1.call-done = bf16[1024,4096]{1,0:T(8,128)(2,1)} async-done(((bf16[256,4096]{1,0:T(8,128)(2,1)}), bf16[1024,4096]{1,0:T(8,128)(2,1)}) %all-gather.13.cloned.1.call-update) | async-done | bytes 8388624 | tf_op jit(solution)/shard_map/all_gather | solution.py:207
  74.2 5.8 convolution_convert_fusion
  81.2 3.4 collective-permute-start
  84.6 6.1 all_gather.57
  90.7 5.2 all-gather.3
  95.9 5.4 all-gather.5
  101.9 8.7 all-gather.15.cloned.1.call-done
  110.8 8.2 fusion.36
  119.5 3.5 convert_multiply_fusion.5
  123.0 10.5 reverse.3
  133.4 3.2 fusion.51
  144.2 3.2 bitcast_add_fusion.7
  147.3 16.6 rev.8
  168.0 4.8 bitcast_subtract_fusion
  173.4 66.2 %while.193 = (s32[]{:T(128)}, f32[1,16,2048]{2,1,0:T(8,128)}, f32[8,1,32,2048]{3,2,1,0:T(8,128)}, f32[16,2048]{1,0:T(8,128)S(1)}, f32[8,1,32]{2,1,0:T(1,128)}, /...) while((s32[]{:T(128)}, f32[1,16,2048]{2,1,0:T(8,128)}, ...), condition=%wide.region_12.13_spmd.clone, body=%wide.region_10.12_spmd.clone.sunk | while | flops 5275651 | bytes 2238963 | solution.py:103
  242.6 66.1 %while.194 = (s32[]{:T(128)}, f32[1,16,2048]{2,1,0:T(8,128)}, f32[8,1,32,2048]{3,2,1,0:T(8,128)}, f32[16,2048]{1,0:T(8,128)S(1)}, f32[8,1,32]{2,1,0:T(1,128)}, /...) while((s32[]{:T(128)}, f32[1,16,2048]{2,1,0:T(8,128)}, ...), condition=%wide.region_23.24_spmd.clone, body=%wide.region_21.23_spmd.clone.sunk | while | flops 5275651 | bytes 2238963 | solution.py:103
  315.2 6.4 all-gather.17.cloned.1.call-done
  323.2 399.4 %while.188 = (s32[]{:T(128)}, f32[1,16,2048]{2,1,0:T(8,128)S(1)}, f32[8,1,32,2048]{3,2,0,1:T(8,128)}, f32[8,1,16,2048]{3,2,1,0:T(8,128)}, f32[8,1,32,2048]{3,0,2...) while((s32[]{:T(128)}, f32[1,16,2048]{2,1,0:T(8,128)S(1)}, ...), condition=%wide.region_19.20_spmd, body=%wide.region_15.19_spmd.sunk | while | flops 260100 | bytes 2836450 | solution.py:268
  326.6 45.1 %while.195 = (s32[]{:T(128)}, f32[1,16,2048]{2,1,0:T(8,128)S(1)}, f32[32,1,2048]{2,1,0:T(1,128)S(1)}, f32[32,1,2048]{2,1,0:T(1,128)S(1)}, f32[16,2048]{1,0:T(8,1...) while((s32[]{:T(128)}, f32[1,16,2048]{2,1,0:T(8,128)S(1)}, ...), condition=%wide.region_18.18_spmd, body=%wide.region_16.17_spmd.sunk | while | flops 260098 | bytes 467457 | solution.py:141
  376.5 45.1 %while.195 = (s32[]{:T(128)}, f32[1,16,2048]{2,1,0:T(8,128)S(1)}, f32[32,1,2048]{2,1,0:T(1,128)S(1)}, f32[32,1,2048]{2,1,0:T(1,128)S(1)}, f32[16,2048]{1,0:T(8,1...) while((s32[]{:T(128)}, f32[1,16,2048]{2,1,0:T(8,128)S(1)}, ...), condition=%wide.region_18.18_spmd, body=%wide.region_16.17_spmd.sunk | while | flops 260098 | bytes 467457 | solution.py:141
  426.4 45.1 %while.195 = (s32[]{:T(128)}, f32[1,16,2048]{2,1,0:T(8,128)S(1)}, f32[32,1,2048]{2,1,0:T(1,128)S(1)}, f32[32,1,2048]{2,1,0:T(1,128)S(1)}, f32[16,2048]{1,0:T(8,1...) while((s32[]{:T(128)}, f32[1,16,2048]{2,1,0:T(8,128)S(1)}, ...), condition=%wide.region_18.18_spmd, body=%wide.region_16.17_spmd.sunk | while | flops 260098 | bytes 467457 | solution.py:141
  476.4 45.1 %while.195 = (s32[]{:T(128)}, f32[1,16,2048]{2,1,0:T(8,128)S(1)}, f32[32,1,2048]{2,1,0:T(1,128)S(1)}, f32[32,1,2048]{2,1,0:T(1,128)S(1)}, f32[16,2048]{1,0:T(8,1...) while((s32[]{:T(128)}, f32[1,16,2048]{2,1,0:T(8,128)S(1)}, ...), condition=%wide.region_18.18_spmd, body=%wide.region_16.17_spmd.sunk | while | flops 260098 | bytes 467457 | solution.py:141
  526.3 45.1 %while.195 = (s32[]{:T(128)}, f32[1,16,2048]{2,1,0:T(8,128)S(1)}, f32[32,1,2048]{2,1,0:T(1,128)S(1)}, f32[32,1,2048]{2,1,0:T(1,128)S(1)}, f32[16,2048]{1,0:T(8,1...) while((s32[]{:T(128)}, f32[1,16,2048]{2,1,0:T(8,128)S(1)}, ...), condition=%wide.region_18.18_spmd, body=%wide.region_16.17_spmd.sunk | while | flops 260098 | bytes 467457 | solution.py:141
  576.2 45.1 %while.195 = (s32[]{:T(128)}, f32[1,16,2048]{2,1,0:T(8,128)S(1)}, f32[32,1,2048]{2,1,0:T(1,128)S(1)}, f32[32,1,2048]{2,1,0:T(1,128)S(1)}, f32[16,2048]{1,0:T(8,1...) while((s32[]{:T(128)}, f32[1,16,2048]{2,1,0:T(8,128)S(1)}, ...), condition=%wide.region_18.18_spmd, body=%wide.region_16.17_spmd.sunk | while | flops 260098 | bytes 467457 | solution.py:141
  626.2 45.1 %while.195 = (s32[]{:T(128)}, f32[1,16,2048]{2,1,0:T(8,128)S(1)}, f32[32,1,2048]{2,1,0:T(1,128)S(1)}, f32[32,1,2048]{2,1,0:T(1,128)S(1)}, f32[16,2048]{1,0:T(8,1...) while((s32[]{:T(128)}, f32[1,16,2048]{2,1,0:T(8,128)S(1)}, ...), condition=%wide.region_18.18_spmd, body=%wide.region_16.17_spmd.sunk | while | flops 260098 | bytes 467457 | solution.py:141
  676.1 45.1 %while.195 = (s32[]{:T(128)}, f32[1,16,2048]{2,1,0:T(8,128)S(1)}, f32[32,1,2048]{2,1,0:T(1,128)S(1)}, f32[32,1,2048]{2,1,0:T(1,128)S(1)}, f32[16,2048]{1,0:T(8,1...) while((s32[]{:T(128)}, f32[1,16,2048]{2,1,0:T(8,128)S(1)}, ...), condition=%wide.region_18.18_spmd, body=%wide.region_16.17_spmd.sunk | while | flops 260098 | bytes 467457 | solution.py:141
  722.7 7.4 while.189
  733.4 1708.4 %while.192 = (s32[]{:T(128)}, f32[1,16,2048]{2,1,0:T(8,128)S(1)}, f32[16,2048]{1,0:T(8,128)S(1)}, f32[8,1,32,2048]{3,2,0,1:T(8,128)}, f32[8,1,32,2048]{3,2,0,1:T...) while((s32[]{:T(128)}, f32[1,16,2048]{2,1,0:T(8,128)S(1)}, ...), condition=%wide.region_35.36_spmd, body=%wide.region_26.35_spmd.sunk | while | flops 2002920 | bytes 23094080 | solution.py:316
  738.6 63.2 %while.196 = (s32[]{:T(128)}, f32[1,16,2048]{2,1,0:T(8,128)S(1)}, f32[32,1,16,2048]{3,2,1,0:T(8,128)}, f32[32,1,2048]{2,1,0:T(1,128)S(1)}, f32[16,2048]{1,0:T(8,...) while((s32[]{:T(128)}, f32[1,16,2048]{2,1,0:T(8,128)S(1)}, ...), condition=%wide.region_28.28_spmd, body=%wide.region_27.27_spmd.sunk | while | flops 196610 | bytes 574769 | solution.py:124
  809.0 136.9 %while.197 = (s32[]{:T(128)}, f32[1,16,2048]{2,1,0:T(8,128)S(1)}, f32[16,2048]{1,0:T(8,128)S(1)}, f32[32,1,2048]{2,1,0:T(1,128)S(1)}, f32[32,1,2048]{2,1,0:T(1,1...) while((s32[]{:T(128)}, f32[1,16,2048]{2,1,0:T(8,128)S(1)}, ...), condition=%wide.region_34.34_spmd, body=%wide.region_29.33_spmd.sunk | while | flops 757731 | bytes 1731361 | solution.py:171
  952.2 63.2 %while.196 = (s32[]{:T(128)}, f32[1,16,2048]{2,1,0:T(8,128)S(1)}, f32[32,1,16,2048]{3,2,1,0:T(8,128)}, f32[32,1,2048]{2,1,0:T(1,128)S(1)}, f32[16,2048]{1,0:T(8,...) while((s32[]{:T(128)}, f32[1,16,2048]{2,1,0:T(8,128)S(1)}, ...), condition=%wide.region_28.28_spmd, body=%wide.region_27.27_spmd.sunk | while | flops 196610 | bytes 574769 | solution.py:124
  1022.6 136.9 %while.197 = (s32[]{:T(128)}, f32[1,16,2048]{2,1,0:T(8,128)S(1)}, f32[16,2048]{1,0:T(8,128)S(1)}, f32[32,1,2048]{2,1,0:T(1,128)S(1)}, f32[32,1,2048]{2,1,0:T(1,1...) while((s32[]{:T(128)}, f32[1,16,2048]{2,1,0:T(8,128)S(1)}, ...), condition=%wide.region_34.34_spmd, body=%wide.region_29.33_spmd.sunk | while | flops 757731 | bytes 1731361 | solution.py:171
  1165.7 63.2 %while.196 = (s32[]{:T(128)}, f32[1,16,2048]{2,1,0:T(8,128)S(1)}, f32[32,1,16,2048]{3,2,1,0:T(8,128)}, f32[32,1,2048]{2,1,0:T(1,128)S(1)}, f32[16,2048]{1,0:T(8,...) while((s32[]{:T(128)}, f32[1,16,2048]{2,1,0:T(8,128)S(1)}, ...), condition=%wide.region_28.28_spmd, body=%wide.region_27.27_spmd.sunk | while | flops 196610 | bytes 574769 | solution.py:124
  1236.2 136.9 %while.197 = (s32[]{:T(128)}, f32[1,16,2048]{2,1,0:T(8,128)S(1)}, f32[16,2048]{1,0:T(8,128)S(1)}, f32[32,1,2048]{2,1,0:T(1,128)S(1)}, f32[32,1,2048]{2,1,0:T(1,1...) while((s32[]{:T(128)}, f32[1,16,2048]{2,1,0:T(8,128)S(1)}, ...), condition=%wide.region_34.34_spmd, body=%wide.region_29.33_spmd.sunk | while | flops 757731 | bytes 1731361 | solution.py:171
  1379.3 63.2 %while.196 = (s32[]{:T(128)}, f32[1,16,2048]{2,1,0:T(8,128)S(1)}, f32[32,1,16,2048]{3,2,1,0:T(8,128)}, f32[32,1,2048]{2,1,0:T(1,128)S(1)}, f32[16,2048]{1,0:T(8,...) while((s32[]{:T(128)}, f32[1,16,2048]{2,1,0:T(8,128)S(1)}, ...), condition=%wide.region_28.28_spmd, body=%wide.region_27.27_spmd.sunk | while | flops 196610 | bytes 574769 | solution.py:124
  1449.7 136.9 %while.197 = (s32[]{:T(128)}, f32[1,16,2048]{2,1,0:T(8,128)S(1)}, f32[16,2048]{1,0:T(8,128)S(1)}, f32[32,1,2048]{2,1,0:T(1,128)S(1)}, f32[32,1,2048]{2,1,0:T(1,1...) while((s32[]{:T(128)}, f32[1,16,2048]{2,1,0:T(8,128)S(1)}, ...), condition=%wide.region_34.34_spmd, body=%wide.region_29.33_spmd.sunk | while | flops 757731 | bytes 1731361 | solution.py:171
  1592.8 63.2 %while.196 = (s32[]{:T(128)}, f32[1,16,2048]{2,1,0:T(8,128)S(1)}, f32[32,1,16,2048]{3,2,1,0:T(8,128)}, f32[32,1,2048]{2,1,0:T(1,128)S(1)}, f32[16,2048]{1,0:T(8,...) while((s32[]{:T(128)}, f32[1,16,2048]{2,1,0:T(8,128)S(1)}, ...), condition=%wide.region_28.28_spmd, body=%wide.region_27.27_spmd.sunk | while | flops 196610 | bytes 574769 | solution.py:124
  1663.3 136.9 %while.197 = (s32[]{:T(128)}, f32[1,16,2048]{2,1,0:T(8,128)S(1)}, f32[16,2048]{1,0:T(8,128)S(1)}, f32[32,1,2048]{2,1,0:T(1,128)S(1)}, f32[32,1,2048]{2,1,0:T(1,1...) while((s32[]{:T(128)}, f32[1,16,2048]{2,1,0:T(8,128)S(1)}, ...), condition=%wide.region_34.34_spmd, body=%wide.region_29.33_spmd.sunk | while | flops 757731 | bytes 1731361 | solution.py:171
  1806.4 63.2 %while.196 = (s32[]{:T(128)}, f32[1,16,2048]{2,1,0:T(8,128)S(1)}, f32[32,1,16,2048]{3,2,1,0:T(8,128)}, f32[32,1,2048]{2,1,0:T(1,128)S(1)}, f32[16,2048]{1,0:T(8,...) while((s32[]{:T(128)}, f32[1,16,2048]{2,1,0:T(8,128)S(1)}, ...), condition=%wide.region_28.28_spmd, body=%wide.region_27.27_spmd.sunk | while | flops 196610 | bytes 574769 | solution.py:124
  1876.8 136.9 %while.197 = (s32[]{:T(128)}, f32[1,16,2048]{2,1,0:T(8,128)S(1)}, f32[16,2048]{1,0:T(8,128)S(1)}, f32[32,1,2048]{2,1,0:T(1,128)S(1)}, f32[32,1,2048]{2,1,0:T(1,1...) while((s32[]{:T(128)}, f32[1,16,2048]{2,1,0:T(8,128)S(1)}, ...), condition=%wide.region_34.34_spmd, body=%wide.region_29.33_spmd.sunk | while | flops 757731 | bytes 1731361 | solution.py:171
  2019.9 63.2 %while.196 = (s32[]{:T(128)}, f32[1,16,2048]{2,1,0:T(8,128)S(1)}, f32[32,1,16,2048]{3,2,1,0:T(8,128)}, f32[32,1,2048]{2,1,0:T(1,128)S(1)}, f32[16,2048]{1,0:T(8,...) while((s32[]{:T(128)}, f32[1,16,2048]{2,1,0:T(8,128)S(1)}, ...), condition=%wide.region_28.28_spmd, body=%wide.region_27.27_spmd.sunk | while | flops 196610 | bytes 574769 | solution.py:124
  2090.3 136.9 %while.197 = (s32[]{:T(128)}, f32[1,16,2048]{2,1,0:T(8,128)S(1)}, f32[16,2048]{1,0:T(8,128)S(1)}, f32[32,1,2048]{2,1,0:T(1,128)S(1)}, f32[32,1,2048]{2,1,0:T(1,1...) while((s32[]{:T(128)}, f32[1,16,2048]{2,1,0:T(8,128)S(1)}, ...), condition=%wide.region_34.34_spmd, body=%wide.region_29.33_spmd.sunk | while | flops 757731 | bytes 1731361 | solution.py:171
  2233.4 63.2 %while.196 = (s32[]{:T(128)}, f32[1,16,2048]{2,1,0:T(8,128)S(1)}, f32[32,1,16,2048]{3,2,1,0:T(8,128)}, f32[32,1,2048]{2,1,0:T(1,128)S(1)}, f32[16,2048]{1,0:T(8,...) while((s32[]{:T(128)}, f32[1,16,2048]{2,1,0:T(8,128)S(1)}, ...), condition=%wide.region_28.28_spmd, body=%wide.region_27.27_spmd.sunk | while | flops 196610 | bytes 574769 | solution.py:124
  2303.9 136.9 %while.197 = (s32[]{:T(128)}, f32[1,16,2048]{2,1,0:T(8,128)S(1)}, f32[16,2048]{1,0:T(8,128)S(1)}, f32[32,1,2048]{2,1,0:T(1,128)S(1)}, f32[32,1,2048]{2,1,0:T(1,1...) while((s32[]{:T(128)}, f32[1,16,2048]{2,1,0:T(8,128)S(1)}, ...), condition=%wide.region_34.34_spmd, body=%wide.region_29.33_spmd.sunk | while | flops 757731 | bytes 1731361 | solution.py:171
  2441.8 2.9 fusion.98
  2446.9 5.2 all-gather.6
  2461.1 4.0 fusion.94
  2466.1 4.5 fusion.78
  2474.6 3.2 collective-permute-done.1
  2478.1 8.2 fusion.59
  2488.8 4.5 reduce-scatter.11.cloned.1.call-done
  2493.4 74.3 %reduce-scatter.17.cloned.1.call-done = f32[512,1024]{1,0:T(8,128)} async-done(((f32[2048,1024]{1,0:T(8,128)}), f32[512,1024]{1,0:T(8,128)}) %reduce-scatter.17.cloned.1.call-update) | async-done | bytes 2097168 | tf_op jit(solution)/shard_map/reduce_scatter | solution.py:378
  2567.7 129.0 %reduce-scatter.9.cloned.1.call-done = f32[256,4096]{1,0:T(8,128)} async-done(((f32[1024,4096]{1,0:T(8,128)}), f32[256,4096]{1,0:T(8,128)}) %reduce-scatter.9.cloned.1.call-update) | async-done | bytes 4194320 | tf_op jit(solution)/shard_map/reduce_scatter | solution.py:370
  2699.2 4.3 fusion.62
  2703.6 7.2 fusion.71
  2710.7 10.9 all-reduce.11
  2725.8 21.8 reduce-scatter.15.cloned.1.call-done
  2747.6 40.3 %all-reduce.9 = (f32[256]{0:T(256)}, f32[4,512]{1,0:T(4,128)}, f32[512]{0:T(512)}, f32[512]{0:T(512)}, f32[16,512]{1,0:T(8,128)}, /*index=5*/f32[512]{0:T(512)}) all-reduce(f32[256]{0:T(256)S(1)} %dynamic-slice.1, f32[4,512]{1,0:T(4,128)S(1)} %copy.144, f32[512]{0:T(512)S(1)} %dynamic-slice.3, ...), channel_id=1, replica_groups=mesh['fsdp'=4,'seq'=8] {'seq'}, use_global_device_ids=true, to_apply=%region_39.40 | all-reduce | flops 12032 | bytes 96256 | tf_op jit(solution)/shard_map/psum | solution.py:380
  2787.8 189.1 %all-reduce.14.cloned.1.call-done = (f32[256,4096]{1,0:T(8,128)}, f32[512,96]{0,1:T(8,128)}, f32[64,512]{1,0:T(8,128)}, f32[512,1024]{1,0:T(8,128)}) async-done(((f32[256,4096]{1,0:T(8,128)}, f32[512,96]{0,1:T(8,128)}, f32[64,512]{1,0:T(8,128)}, f32[512,1024]{1,0:T(8,128)}), (f32[256,4096]{1,0:T(8,128)}, f32[512,96]{0,1:T(8,128)}, f32[64,512]{1,0:T(8,128)}, ...) | async-done | bytes 6619152 | tf_op jit(solution)/shard_map/psum | solution.py:380
  2976.9 4.8 copy.311
  (5154 shorter events, 2281.7 us)
Async XLA Ops:
  7.2 7.6 copy-start.59
  7.2 8.0 copy-start.52
  7.2 13.5 copy-start.35
  7.2 24.0 copy-start.9
  7.2 24.2 copy-start.34
  7.2 66.9 %all-gather.13.cloned.1.call-start = ((), (), s32[]{:S(2)}) async-start(), calls=%async_computation.6 | async-start | bytes 10485760 | tf_op jit(solution)/shard_map/all_gather | solution.py:207
  8.0 102.7 %all-gather.15.cloned.1.call-start = ((), (), s32[]{:S(2)}) async-start(), calls=%async_computation.7 | async-start | bytes 5242880 | tf_op jit(solution)/shard_map/all_gather | solution.py:215
  8.7 306.4 %all-gather.19.cloned.1.call-start = ((), (), s32[]{:S(2)}) async-start(), calls=%async_computation.14 | async-start | bytes 1179648 | tf_op jit(solution)/shard_map/all_gather | solution.py:24
  28.0 91.5 %copy-start.15 = (bf16[64,2048]{1,0:T(8,128)(2,1)}, bf16[64,2048]{1,0:T(8,128)(2,1)S(1)}, u32[]{:S(2)}) copy-start(bf16[64,2048]{1,0:T(8,128)(2,1)S(1)} %all_gather.63) | copy-start | bytes 786436
  41.4 69.3 %copy-start.46 = (f32[1,256]{1,0:T(1,128)}, f32[1,256]{1,0:T(1,128)S(1)}, u32[]{:S(2)}) copy-start(f32[1,256]{1,0:T(1,128)S(1)} %get-tuple-element.1530) | copy-start | bytes 3076
  41.4 69.3 %copy-start.48 = (f32[1,256]{1,0:T(1,128)}, f32[1,256]{1,0:T(1,128)S(1)}, u32[]{:S(2)}) copy-start(f32[1,256]{1,0:T(1,128)S(1)} %get-tuple-element.1531) | copy-start | bytes 3076
  41.4 69.3 %copy-start.50 = (f32[1,256]{1,0:T(1,128)}, f32[1,256]{1,0:T(1,128)S(1)}, u32[]{:S(2)}) copy-start(f32[1,256]{1,0:T(1,128)S(1)} %get-tuple-element.1532) | copy-start | bytes 3076
  41.5 69.2 %copy-start.36 = (f32[1,2048]{1,0:T(1,128)}, f32[1,2048]{1,0:T(1,128)S(1)}, u32[]{:S(2)}) copy-start(f32[1,2048]{1,0:T(1,128)S(1)} %get-tuple-element.1526) | copy-start | bytes 24580
  41.5 69.2 %copy-start.38 = (f32[1,2048]{1,0:T(1,128)}, f32[1,2048]{1,0:T(1,128)S(1)}, u32[]{:S(2)}) copy-start(f32[1,2048]{1,0:T(1,128)S(1)} %get-tuple-element.1527) | copy-start | bytes 24580
  41.5 69.2 %copy-start.40 = (f32[1,2048]{1,0:T(1,128)}, f32[1,2048]{1,0:T(1,128)S(1)}, u32[]{:S(2)}) copy-start(f32[1,2048]{1,0:T(1,128)S(1)} %get-tuple-element.1528) | copy-start | bytes 24580
  41.5 69.2 %copy-start.42 = (f32[1,2048]{1,0:T(1,128)}, f32[1,2048]{1,0:T(1,128)S(1)}, u32[]{:S(2)}) copy-start(f32[1,2048]{1,0:T(1,128)S(1)} %get-tuple-element.1529) | copy-start | bytes 24580
  80.0 39.0 %copy-start.11 = (bf16[256,4096]{1,0:T(8,128)(2,1)}, bf16[256,4096]{1,0:T(8,128)(2,1)S(1)}, u32[]{:S(2)}) copy-start(bf16[256,4096]{1,0:T(8,128)(2,1)S(1)} %convolution_convert_fusion) | copy-start | bytes 6291460
  80.0 4.7 copy-start.44
  80.0 10.7 copy-start.53
  80.0 15.9 copy-start.54
  81.2 29.4 collective-permute-start
  110.7 8.3 copy-start.56
  110.7 8.3 copy-start.19
  119.5 24.0 copy-start.24
  168.0 4.8 copy-start.26
  239.7 81.9 %all-gather.17.cloned.1.call-start = ((), (), s32[]{:S(2)}) async-start(), calls=%async_computation.13 | async-start | bytes 1179648 | tf_op jit(solution)/shard_map/all_gather | solution.py:24
  242.6 480.1 %all-gather.21.cloned.1.call-start = ((), (), s32[]{:S(2)}) async-start(), calls=%async_computation.15 | async-start | bytes 1179648 | tf_op jit(solution)/shard_map/all_gather | solution.py:24
  315.1 2173.7 %reduce-scatter.13.cloned.1.call-start = ((), (), s32[]{:S(2)}) async-start(), calls=%async_computation.10 | async-start | bytes 655360 | tf_op jit(solution)/shard_map/reduce_scatter | solution.py:374
  2441.8 2.9 copy-start.28
  2441.8 2.9 copy-start.30
  2441.8 3.9 copy-start.25
  2445.7 6.4 copy-start.29
  2445.7 6.4 copy-start.31
  2446.8 46.6 %reduce-scatter.11.cloned.1.call-start = ((), (), s32[]{:S(2)}) async-start(), calls=%async_computation.9 | async-start | bytes 983040 | tf_op jit(solution)/shard_map/reduce_scatter | solution.py:373
  2452.0 3.8 copy-start.3
  2455.4 112.4 %reduce-scatter.17.cloned.1.call-start = ((), (), s32[]{:S(2)}) async-start(), calls=%async_computation.12 | async-start | bytes 10485760 | tf_op jit(solution)/shard_map/reduce_scatter | solution.py:378
  2455.8 2.2 copy-start.20
  2455.8 2.2 copy-start.22
  2455.9 2.7 copy-start.61
  2458.6 2.2 copy-start.5
  2458.6 2.2 copy-start.12
  2458.6 2.5 copy-start.23
  2458.6 2.5 copy-start.37
  2458.6 2.5 copy-start.39
  2458.6 2.5 copy-start.41
  2458.6 2.5 copy-start.43
  2461.1 5.0 copy-start.17
  2470.6 226.0 %reduce-scatter.9.cloned.1.call-start = ((), (), s32[]{:S(2)}) async-start(), calls=%async_computation.8 | async-start | bytes 20971520 | tf_op jit(solution)/shard_map/reduce_scatter | solution.py:370
  2470.7 2.7 copy-start
  2470.7 2.7 copy-start.1
  2470.7 2.9 copy-start.2
  2471.8 6.1 collective-permute-start.1
  2474.6 3.5 copy-start.10
  2474.6 3.5 copy-start.13
  2486.4 238.4 %reduce-scatter.19.cloned.1.call-start = ((), (), s32[]{:S(2)}) async-start(), calls=%async_computation.16 | async-start | bytes 1310720
  2487.8 259.7 %reduce-scatter.15.cloned.1.call-start = ((), (), s32[]{:S(2)}) async-start(), calls=%async_computation.11 | async-start | bytes 163840 | tf_op jit(solution)/shard_map/reduce_scatter | solution.py:376
  2488.6 488.3 %all-reduce.14.cloned.1.call-start = ((), (), s32[]{:S(2)}) async-start(), calls=%async_computation.17 | async-start | bytes 13238272 | tf_op jit(solution)/shard_map/psum | solution.py:380
  2696.7 2.5 copy-start.8
  2699.2 4.3 copy-start.14
  2703.5 7.2 copy-start.45
  2703.6 18.4 copy-start.18
  2976.9 4.8 copy-start.32
  2976.9 5.5 copy-start.33
  2976.9 6.1 copy-start.16
  (12 other events, 19.0 us)
Sparse Core Ops, SparseCore 0:
  9.6 64.4 all-gather.12
  75.7 34.9 all-gather.14
  239.8 40.1 all-gather.18
  282.6 38.9 all-gather.16
  324.1 38.9 all-gather.20
  2446.9 20.4 reduce-scatter.12
  2470.1 23.2 reduce-scatter.10
  2495.9 71.7 reduce-scatter.16
  2570.5 126.1 reduce-scatter.8
  2699.6 25.0 reduce-scatter.18
  2727.9 19.6 reduce-scatter.14
  2751.9 225.0 all-reduce.13
where the time goes:
time: 3020 us; the launch traced here: 2990 us
  other arithmetic  1600 us (53%)
  local copies, waits for them, and re-layouts  725 us (24%)
  waiting for transfers between devices  472 us (16%)
  blocking collectives  102 us (3%)
  matrix products  48.5 us (2%)
    reduce_sum x256, other arithmetic, retreat(): grad_enter = jnp.sum(adjoint * (step_p * mixed_p)[:, None, :], axis=2)  479 us
    dynamic_slice x1280, local copies, waits for them, and re-layouts, block_forward(): lax.scan(block_advance, state, (step_t, enter_t, read_t, mixed_t, keep_t))  452 us
    add x256, other arithmetic, retreat(): total = total + jnp.sum(slope * step_p[:, None, :], axis=0)  426 us
    dynamic_update_slice x256, other arithmetic, advance_states(): return lax.scan(advance_advance, state, (step_t, enter_t, mixed_t, keep_t))  356 us
    reduce_sum x256, other arithmetic, block_advance(): return (current, jnp.sum(read_p[:, :, None] * current, axis=1))  192 us
    psum x1, waiting for transfers between devices, shards(): lax.psum((shares[0], shares[1], shares[2], shares[3], shares[4], shares[5...  189 us
    reduce_scatter x1, waiting for transfers between devices, shards(): lax.psum_scatter(input_grad, 'fsdp', scatter_dimension=0, tiled=True)  129 us
    reduce_scatter x1, waiting for transfers between devices, shards(): lax.psum_scatter(output_grad, 'fsdp', scatter_dimension=0, tiled=True)  74.3 us

commit v1 on v0

v1 whole, which is shorter than its diff:
```python
import functools
import math

import jax
import jax.numpy as jnp
from jax import lax
from jax.experimental import pallas as pl
from jax.experimental.pallas import tpu as pltpu
from jax.sharding import PartitionSpec as P

EPS = 1e-05
MESH = pl.DeviceIdType.MESH
LOG2E = math.log2(math.e)
LN2 = math.log(2.0)
BF16 = jnp.bfloat16
F32 = jnp.float32
ANY = pl.BlockSpec(memory_space=pl.ANY)
VMEM = pl.BlockSpec(memory_space=pltpu.VMEM)
RESET = 1e30
HALO = 16


def here():
    return lax.axis_index("fsdp"), lax.axis_index("seq")


def greet(peers):
    barrier = pltpu.get_barrier_semaphore()
    count = 0
    for ok, device in peers:
        if ok is None:
            pl.semaphore_signal(barrier, inc=1, device_id=device, device_id_type=MESH)
            count = count + 1
        else:

            @pl.when(ok)
            def _():
                pl.semaphore_signal(barrier, inc=1, device_id=device, device_id_type=MESH)

            count = count + ok.astype(jnp.int32)
    pl.semaphore_wait(barrier, count)


def remote(src, dst, send, recv, device):
    return pltpu.make_async_remote_copy(
        src_ref=src, dst_ref=dst, send_sem=send, recv_sem=recv, device_id=device, device_id_type=MESH
    )


def comm_params(cid, vmem=None):
    return pltpu.CompilerParams(collective_id=cid, has_side_effects=True, vmem_limit_bytes=vmem)


def enter_kernel(nf, ns, ch, inner, x, ct, w, sm, xg, cg, wi, wg, sg, hal, ssem, rsem, lsem):
    f, s = here()
    core = lax.bitwise_xor(f, 1)
    up, down = s + 1, s - 1
    has_up, has_down = up < ns, down >= 0
    peers = [(None, (lax.bitwise_xor(f, i), s)) for i in range(1, nf)]
    for i in range(nf):
        peers.append((has_up, (lax.bitwise_xor(f, i), up)))
        peers.append((has_down, (lax.bitwise_xor(f, i), down)))
    greet(peers)
    stretch = x.shape[1]
    tail = x.at[:, pl.ds(stretch - HALO, HALO), :]

    def cols(block, base):
        return w.at[:, pl.ds(pl.multiple_of(base + block * ch, 128), ch)]

    def make(kind, i, src, dst, device):
        return remote(src, dst, ssem.at[kind, i], rsem.at[kind, i], device)

    first, later, halos = [], [], []
    for i in range(1, nf):
        other = lax.bitwise_xor(f, i)
        device = (other, s)
        first.append(make(0, i, sm, sg.at[f], device))
        first.append(make(1, i, cols(other, 0), wi.at[f], device))
        later.append(make(2, i, cols(other, inner), wg.at[f], device))
    xcopies = [make(3, i, x, xg.at[f], (lax.bitwise_xor(f, i), s)) for i in [1] + list(range(2, nf, 2))]
    ccopies = [make(4, i, ct, cg.at[f], (lax.bitwise_xor(f, i), s)) for i in [1] + list(range(2, nf, 2))]
    for i in range(nf):
        halos.append(make(5, i, tail, hal.at[f], (lax.bitwise_xor(f, i), up)))
    for c in xcopies + first:
        c.start()

    @pl.when(has_up)
    def _():
        for c in halos:
            c.start()

    for c in ccopies + later:
        c.start()
    local = [
        pltpu.make_async_copy(x, xg.at[f], lsem.at[0]),
        pltpu.make_async_copy(ct, cg.at[f], lsem.at[1]),
        pltpu.make_async_copy(cols(f, 0), wi.at[f], lsem.at[2]),
        pltpu.make_async_copy(cols(f, inner), wg.at[f], lsem.at[3]),
        pltpu.make_async_copy(sm, sg.at[f], lsem.at[4]),
    ]
    for c in local:
        c.start()
    forwards = []
    for n, i in enumerate(range(2, nf, 2)):
        xcopies[1 + n].wait_recv()
        src = lax.bitwise_xor(f, i)
        c = make(3, i + 1, xg.at[src], xg.at[src], (core, s))
        c.start()
        forwards.append(c)
    for n, i in enumerate(range(2, nf, 2)):
        ccopies[1 + n].wait_recv()
        src = lax.bitwise_xor(f, i)
        c = make(4, i + 1, cg.at[src], cg.at[src], (core, s))
        c.start()
        forwards.append(c)
    xcopies[0].wait_recv()
    ccopies[0].wait_recv()
    for c in xcopies + ccopies:
        c.wait_send()
    for c in first + later + forwards + local:
        c.wait()

    @pl.when(has_up)
    def _():
        for c in halos:
            c.wait_send()

    @pl.when(has_down)
    def _():
        for c in halos:
            c.wait_recv()


def enter_all(nf, ns, x, ct, w, sm):
    rd, stretch, width = x.shape
    rows, both = w.shape
    inner = both // 2
    ch = inner // nf
    shape = jax.ShapeDtypeStruct
    return pl.pallas_call(
        functools.partial(enter_kernel, nf, ns, ch, inner),
        out_shape=(
            shape((nf, rd, stretch, width), BF16),
            shape((nf, rd, stretch, width), BF16),
            shape((nf, rows, ch), BF16),
            shape((nf, rows, ch), BF16),
            shape((nf, 8, 128), F32),
            shape((nf, rd, HALO, width), BF16),
        ),
        in_specs=[ANY] * 4,
        out_specs=[ANY] * 6,
        scratch_shapes=[
            pltpu.SemaphoreType.DMA((6, nf)),
            pltpu.SemaphoreType.DMA((6, nf)),
            pltpu.SemaphoreType.DMA((5,)),
        ],
        compiler_params=comm_params(0),
        name="enter_all",
    )(x, ct, w, sm)


def total_kernel(nf, part, out, got, mid, far, ssem, rsem):
    f, s = here()
    c = lax.rem(f, 2)
    half = part.shape[0] // 2
    core = (lax.bitwise_xor(f, 1), s)
    chips = list(range(2, nf, 2))
    greet([(None, core)] + [(None, (lax.bitwise_xor(f, i), s)) for i in chips])
    mine = pl.ds(pl.multiple_of(c * half, 8), half)
    other = pl.ds(pl.multiple_of((1 - c) * half, 8), half)
    one = remote(part.at[other], got, ssem.at[0], rsem.at[0], core)
    one.start()
    one.wait()
    mid[...] = part[mine, :] + got[...]
    two = []
    for n, i in enumerate(chips):
        cp = remote(mid, far.at[n], ssem.at[1 + n], rsem.at[1 + n], (lax.bitwise_xor(f, i), s))
        cp.start()
        two.append(cp)
    for cp in two:
        cp.wait()
    acc = mid[...]
    for n in range(len(chips)):
        acc = acc + far[n]
    out[mine, :] = acc
    last = len(chips) + 1
    three = remote(out.at[mine], out.at[mine], ssem.at[last], rsem.at[last], core)
    three.start()
    three.wait()


def total_over_fsdp(nf, cid, part):
    tokens, lanes = part.shape
    chips = nf // 2 - 1
    return pl.pallas_call(
        functools.partial(total_kernel, nf),
        out_shape=jax.ShapeDtypeStruct(part.shape, F32),
        in_specs=[VMEM],
        out_specs=VMEM,
        scratch_shapes=[
            pltpu.VMEM((tokens // 2, lanes), F32),
            pltpu.VMEM((tokens // 2, lanes), F32),
            pltpu.VMEM((chips, tokens // 2, lanes), F32),
            pltpu.SemaphoreType.DMA((chips + 2,)),
            pltpu.SemaphoreType.DMA((chips + 2,)),
        ],
        compiler_params=comm_params(cid, 40 << 20),
        name="total_over_fsdp",
    )(part)


def share_kernel(nf, part, out, got, mid, far, ssem, rsem):
    f, s = here()
    c = lax.rem(f, 2)
    core = (lax.bitwise_xor(f, 1), s)
    chips = list(range(2, nf, 2))
    greet([(None, core)] + [(None, (lax.bitwise_xor(f, i), s)) for i in chips])
    near = []
    for n, i in enumerate([0] + chips):
        dest = lax.bitwise_xor(lax.bitwise_xor(f, 1), i)
        cp = remote(part.at[dest], got.at[n], ssem.at[n], rsem.at[n], core)
        cp.start()
        near.append(cp)
    two = []
    for n, i in list(enumerate([0] + chips))[::-1]:
        near[n].wait()
        dest = lax.bitwise_xor(f, i)
        both = part[dest].astype(F32) + got[n].astype(F32)
        if i == 0:
            acc = both
        else:
            mid[n - 1] = both.astype(BF16)
            k = len(chips) + n
            cp = remote(mid.at[n - 1], far.at[n - 1], ssem.at[k], rsem.at[k], (dest, s))
            cp.start()
            two.append(cp)
    for cp in two:
        cp.wait()
    for n in range(len(chips)):
        acc = acc + far[n].astype(F32)
    out[...] = acc


def share_over_fsdp(nf, cid, part):
    block = part.shape[1:]
    chips = nf // 2 - 1
    return pl.pallas_call(
        functools.partial(share_kernel, nf),
        out_shape=jax.ShapeDtypeStruct(block, F32),
        in_specs=[VMEM],
        out_specs=VMEM,
        scratch_shapes=[
            pltpu.VMEM((chips + 1,) + block, BF16),
            pltpu.VMEM((chips,) + block, BF16),
            pltpu.VMEM((chips,) + block, BF16),
            pltpu.SemaphoreType.DMA((2 * chips + 1,)),
            pltpu.SemaphoreType.DMA((2 * chips + 1,)),
        ],
        compiler_params=comm_params(cid, 48 << 20),
        name="share_over_fsdp",
    )(part)


def swap_kernel(nf, part, out, ssem, rsem, lsem):
    f, s = here()
    greet([(None, (lax.bitwise_xor(f, i), s)) for i in range(1, nf)])
    copies = []
    for i in range(1, nf):
        other = lax.bitwise_xor(f, i)
        copies.append(remote(part.at[other], out.at[f], ssem.at[i], rsem.at[i], (other, s)))
    for cp in copies:
        cp.start()
    own = pltpu.make_async_copy(part.at[f], out.at[f], lsem)
    own.start()
    for cp in copies + [own]:
        cp.wait()


def swap_over_fsdp(nf, cid, part):
    return pl.pallas_call(
        functools.partial(swap_kernel, nf),
        out_shape=jax.ShapeDtypeStruct(part.shape, part.dtype),
        in_specs=[ANY],
        out_specs=ANY,
        scratch_shapes=[
            pltpu.SemaphoreType.DMA((nf,)),
            pltpu.SemaphoreType.DMA((nf,)),
            pltpu.SemaphoreType.DMA,
        ],
        compiler_params=comm_params(cid),
        name="swap_over_fsdp",
    )(part)


def carry_kernel(reach, ns, b, g, t, bf, gb, tf, tb, ssem, rsem):
    f, s = here()
    peers = []
    for j in range(1, reach + 1):
        peers.append((s + j < ns, (f, s + j)))
        peers.append((s - j >= 0, (f, s - j)))
    greet(peers)

    def copies(j):
        ahead, back = (f, s + j), (f, s - j)
        k = j - 1
        fwd = [
            remote(b, bf.at[k], ssem.at[0, k], rsem.at[0, k], ahead),
            remote(t, tf.at[k], ssem.at[1, k], rsem.at[1, k], ahead),
        ]
        bwd = [
            remote(g, gb.at[k], ssem.at[2, k], rsem.at[2, k], back),
            remote(t, tb.at[k], ssem.at[3, k], rsem.at[3, k], back),
        ]
        return fwd, bwd

    every = [copies(j) for j in range(1, reach + 1)]
    for j in range(1, reach + 1):
        fwd, bwd = every[j - 1]

        @pl.when(s + j < ns)
        def _():
            for cp in fwd:
                cp.start()

        @pl.when(s - j >= 0)
        def _():
            for cp in bwd:
                cp.start()

    for j in range(1, reach + 1):
        fwd, bwd = every[j - 1]

        @pl.when(s + j < ns)
        def _():
            for cp in fwd:
                cp.wait_send()
            for cp in bwd:
                cp.wait_recv()

        @pl.when(s - j >= 0)
        def _():
            for cp in bwd:
                cp.wait_send()
            for cp in fwd:
                cp.wait_recv()


def carry_over_seq(reach, ns, cid, b, g, t):
    shape = jax.ShapeDtypeStruct
    return pl.pallas_call(
        functools.partial(carry_kernel, reach, ns),
        out_shape=(
            shape((reach,) + b.shape, b.dtype),
            shape((reach,) + g.shape, g.dtype),
            shape((reach,) + t.shape, t.dtype),
            shape((reach,) + t.shape, t.dtype),
        ),
        in_specs=[VMEM] * 3,
        out_specs=[VMEM] * 4,
        scratch_shapes=[
            pltpu.SemaphoreType.DMA((4, reach)),
            pltpu.SemaphoreType.DMA((4, reach)),
        ],
        compiler_params=comm_params(cid, 32 << 20),
        name="carry_over_seq",
    )(b, g, t)


def back_kernel(ns, e, out, ssem, rsem):
    f, s = here()
    greet([(s + 1 < ns, (f, s + 1)), (s >= 1, (f, s - 1))])
    cp = remote(e, out, ssem, rsem, (f, s - 1))

    @pl.when(s >= 1)
    def _():
        cp.start()
        cp.wait_send()

    @pl.when(s + 1 < ns)
    def _():
        cp.wait_recv()


def back_over_seq(ns, cid, e):
    return pl.pallas_call(
        functools.partial(back_kernel, ns),
        out_shape=jax.ShapeDtypeStruct(e.shape, e.dtype),
        in_specs=[VMEM],
        out_specs=VMEM,
        scratch_shapes=[pltpu.SemaphoreType.DMA, pltpu.SemaphoreType.DMA],
        compiler_params=comm_params(cid),
        name="back_over_seq",
    )(e)


BLOCK_TOKENS = 1024


def at(t):
    return pl.ds(pl.multiple_of(t * 8, 8), 8)


def cut(d):
    return slice(d * 128, (d + 1) * 128)


def pieces(v, count):
    out = []
    for _ in range(count):
        top = v.astype(BF16)
        out.append(top)
        v = v - top.astype(F32)
    return out


def coef_pieces(proj, rank, nstate):
    parts = pieces(proj[:, rank : rank + 2 * nstate], 3)
    return jnp.pad(jnp.concatenate(parts, axis=1), ((0, 0), (0, 128 - 6 * nstate)))


def spread_coefs(packed, cscr, first, count, nstate):
    wide = 2 * count * 128
    source = lax.broadcasted_iota(jnp.int32, (128, wide), 0)
    block = lax.broadcasted_iota(jnp.int32, (128, wide), 1) // 128
    want = jnp.where(block < count, block, nstate - count + block) + first
    pick = jnp.where(
        jnp.logical_and(source % (2 * nstate) == want, source < 6 * nstate), 1.0, 0.0
    ).astype(BF16)
    cscr[...] = jnp.dot(packed[...], pick, preferred_element_type=F32)


ENDS_UNROLL = 4
SCAN_UNROLL = 4


def ends_kernel(count, groups, rank, nstate, step, u, dy, proj, rate, b, p, g, cscr):
    j = pl.program_id(2)
    steps = step.shape[0] // 8
    spread_coefs(proj, cscr, j * count, count, nstate)
    keys = [(d, i) for d in range(groups) for i in range(count)]
    rates = [jnp.broadcast_to(rate[0, i : i + 1, cut(d)], (8, 128)) for d, i in keys]

    def one(t, carry):
        bs, ps, gs = carry
        nb, np_, ng = [], [], []
        enter = [cscr[at(t), cut(i)] for i in range(count)]
        read = [cscr[at(t), cut(count + i)] for i in range(count)]
        for d in range(groups):
            st, ut, dt = step[at(t), cut(d)], u[at(t), cut(d)], dy[at(t), cut(d)]
            for i in range(count):
                k = d * count + i
                a = jnp.exp2(st * rates[k])
                prod = ps[k] * a
                nb.append(bs[k] * a + enter[i] * ut)
                np_.append(prod)
                ng.append(gs[k] + prod * (read[i] * dt))
        return tuple(nb), tuple(np_), tuple(ng)

    size = count * groups
    zero = jnp.zeros((8, 128), F32)
    init = ((zero,) * size, (zero + 1.0,) * size, (zero,) * size)
    bs, ps, gs = lax.fori_loop(0, steps, one, init, unroll=ENDS_UNROLL)
    for k, (d, i) in enumerate(keys):
        b[0, i, :, cut(d)] = bs[k]
        p[0, i, :, cut(d)] = ps[k]
        g[0, i, :, cut(d)] = gs[k]


def scan_ends(step, u, dy, proj, rate, rank, count):
    tokens, ch = step.shape
    nstate = rate.shape[0]
    blocks = tokens // BLOCK_TOKENS
    width = min(ch, 512)
    groups = width // 128
    tok = pl.BlockSpec((BLOCK_TOKENS, width), lambda n, c, j: (n, c))
    state = pl.BlockSpec((1, count, 8, width), lambda n, c, j: (n, j, 0, c))
    shape = jax.ShapeDtypeStruct((blocks, nstate, 8, ch), F32)
    return pl.pallas_call(
        functools.partial(ends_kernel, count, groups, rank, nstate),
        out_shape=(shape,) * 3,
        grid=(blocks, ch // width, nstate // count),
        in_specs=[
            tok,
            tok,
            tok,
            pl.BlockSpec((BLOCK_TOKENS, 128), lambda n, c, j: (n, 0)),
            pl.BlockSpec((1, count, width), lambda n, c, j: (j, 0, c)),
        ],
        out_specs=[state] * 3,
        scratch_shapes=[pltpu.VMEM((BLOCK_TOKENS, 2 * count * 128), F32)],
        compiler_params=pltpu.CompilerParams(vmem_limit_bytes=32 << 20),
        cost_estimate=pl.CostEstimate(
            flops=8 * tokens * nstate * ch, bytes_accessed=12 * tokens * ch, transcendentals=tokens * nstate * ch
        ),
        name="scan_ends",
    )(step, u, dy, proj, rate.reshape(nstate // count, count, ch))


def scan_kernel(
    count, groups, rank, nstate, step, u, dy, proj, rate, hin, lin, y, pulled, gs, coef, tot, ascr, hscr, cscr, seen_scr
):
    c, j = pl.program_id(1), pl.program_id(2)
    steps = step.shape[0] // 8
    size = count * groups
    keys = [(d, i) for d in range(groups) for i in range(count)]
    rates = [jnp.broadcast_to(rate[0, i : i + 1, cut(d)], (8, 128)) for d, i in keys]
    spread_coefs(proj, cscr, j * count, count, nstate)

    @pl.when(j == 0)
    def _():
        y[...] = jnp.zeros_like(y)
        pulled[...] = jnp.zeros_like(pulled)
        gs[...] = jnp.zeros_like(gs)

    @pl.when(jnp.logical_and(j == 0, c == 0))
    def _():
        coef[...] = jnp.zeros_like(coef)

    def forward(t, state):
        enter = [cscr[at(t), cut(i)] for i in range(count)]
        read = [cscr[at(t), cut(count + i)] for i in range(count)]
        new = []
        seen = [None] * count
        for d in range(groups):
            st, ut, dt = step[at(t), cut(d)], u[at(t), cut(d)], dy[at(t), cut(d)]
            out = None
            for i in range(count):
                k = d * count + i
                a = jnp.exp2(st * rates[k])
                ascr[t, k] = a
                hscr[t, k] = state[k]
                h = state[k] * a + enter[i] * ut
                new.append(h)
                out = read[i] * h if out is None else out + read[i] * h
                term = h * dt
                seen[i] = term if seen[i] is None else seen[i] + term
            y[at(t), cut(d)] += out
        for i in range(count):
            seen_scr[at(t), cut(count + i)] = seen[i]
        return tuple(new)

    lax.fori_loop(0, steps, forward, tuple(hin[0, i, :, cut(d)] for d, i in keys), unroll=SCAN_UNROLL)

    def backward(k0, carry):
        t = steps - 1 - k0
        passed, sums = carry
        enter = [cscr[at(t), cut(i)] for i in range(count)]
        read = [cscr[at(t), cut(count + i)] for i in range(count)]
        new, news = [], []
        seen = [None] * count
        for d in range(groups):
            st, ut, dt = step[at(t), cut(d)], u[at(t), cut(d)], dy[at(t), cut(d)]
            pull, slope_sum = None, None
            for i in range(count):
                k = d * count + i
                adj = passed[k] + read[i] * dt
                pull = adj * enter[i] if pull is None else pull + adj * enter[i]
                back = adj * ascr[t, k]
                slope = back * hscr[t, k]
                slope_sum = slope * rates[k] if slope_sum is None else slope_sum + slope * rates[k]
                new.append(back)
                news.append(sums[k] + slope * st)
                term = adj * ut
                seen[i] = term if seen[i] is None else seen[i] + term
            pulled[at(t), cut(d)] += pull
            gs[at(t), cut(d)] += slope_sum
        for i in range(count):
            seen_scr[at(t), cut(i)] = seen[i]
        return tuple(new), tuple(news)

    zero = jnp.zeros((8, 128), F32)
    init = (tuple(lin[0, i, :, cut(d)] for d, i in keys), (zero,) * size)
    passed, sums = lax.fori_loop(0, steps, backward, init, unroll=SCAN_UNROLL)
    for n, (d, i) in enumerate(keys):
        tot[0, i, :, cut(d)] = sums[n]

    wide = 2 * count * 128
    block = lax.broadcasted_iota(jnp.int32, (wide, 128), 0) // 128
    column = lax.broadcasted_iota(jnp.int32, (wide, 128), 1)
    want = jnp.where(block < count, block, nstate - count + block) + j * count + rank
    ones = jnp.where(column == want, 1.0, 0.0).astype(BF16)
    for part in pieces(seen_scr[...], 2):
        coef[...] += jnp.dot(part, ones, preferred_element_type=F32)


def scan_all(step, u, dy, proj, rate, hin, lin, rank, count):
    tokens, ch = step.shape
    nstate = rate.shape[0]
    blocks = tokens // BLOCK_TOKENS
    width = min(ch, 512)
    groups = width // 128
    steps = BLOCK_TOKENS // 8
    tok = pl.BlockSpec((BLOCK_TOKENS, width), lambda n, c, j: (n, c))
    narrow = pl.BlockSpec((BLOCK_TOKENS, 128), lambda n, c, j: (n, 0))
    state = pl.BlockSpec((1, count, 8, width), lambda n, c, j: (n, j, 0, c))
    shape = jax.ShapeDtypeStruct
    return pl.pallas_call(
        functools.partial(scan_kernel, count, groups, rank, nstate),
        out_shape=(
            shape((tokens, ch), F32),
            shape((tokens, ch), F32),
            shape((tokens, ch), F32),
            shape((tokens, 128), F32),
            shape((blocks, nstate, 8, ch), F32),
        ),
        grid=(blocks, ch // width, nstate // count),
        in_specs=[
            tok,
            tok,
            tok,
            narrow,
            pl.BlockSpec((1, count, width), lambda n, c, j: (j, 0, c)),
            state,
            state,
        ],
        out_specs=[tok, tok, tok, narrow, state],
        scratch_shapes=[
            pltpu.VMEM((steps, count * groups, 8, 128), F32),
            pltpu.VMEM((steps, count * groups, 8, 128), F32),
            pltpu.VMEM((BLOCK_TOKENS, 2 * count * 128), F32),
            pltpu.VMEM((BLOCK_TOKENS, 2 * count * 128), F32),
        ],
        compiler_params=pltpu.CompilerParams(vmem_limit_bytes=60 << 20),
        cost_estimate=pl.CostEstimate(
            flops=20 * tokens * nstate * ch, bytes_accessed=24 * tokens * ch, transcendentals=tokens * nstate * ch
        ),
        name="scan_all",
    )(step, u, dy, proj, rate.reshape(nstate // count, count, ch), hin, lin)


def rows_inner(left, right):
    return lax.dot_general(left, right, (((0,), (0,)), ((), ())), preferred_element_type=F32)


def times_transposed(left, right):
    return lax.dot_general(left, right, (((1,), (1,)), ((), ())), preferred_element_type=F32)


def silu_slope(value):
    sig = jax.nn.sigmoid(value)
    return sig * (1.0 + value * (1.0 - sig))


def shards(
    nf,
    ns,
    residual,
    out_cotangent,
    doc_lengths,
    norm_gain,
    input_proj,
    conv_kernel,
    conv_bias,
    select_proj,
    step_proj,
    step_bias,
    log_decay,
    skip_gain,
    output_proj,
):
    rd, stretch, width = residual.shape
    rows = nf * rd
    docs = doc_lengths.shape[1]
    ch = conv_bias.shape[0]
    rank = step_proj.shape[0]
    nstate = log_decay.shape[0]
    taps = conv_kernel.shape[0]
    edge = taps - 1
    tokens = rows * stretch
    half = stretch // 2
    blocks = rows // 4
    f, s = here()
    reach = -(-(stretch * ns // 2 - 1) // stretch)
    count = 4

    small = jnp.zeros((8, 128), F32)
    small = small.at[:rd, :docs].set(doc_lengths.astype(F32))
    grows = norm_gain.shape[0]
    gl = min(grows, 128)
    small = small.at[4 : 4 + grows // gl, :gl].set(norm_gain.astype(F32).reshape(-1, gl))
    xg, cg, wi, wg, sg, hal = enter_all(nf, ns, residual, out_cotangent, input_proj, small)
    lengths = sg[:, :rd, :docs].reshape(rows, docs).astype(jnp.int32)
    gain = sg[:, 4 : 4 + grows // gl, :gl].reshape(1, width)
    w_inner = wi.reshape(width, ch)
    w_gate = wg.reshape(width, ch)

    def to_tokens(v):
        v = v.reshape((blocks, 4, 2, half) + v.shape[2:])
        return jnp.moveaxis(v, 3, 1).reshape((tokens,) + v.shape[4:])

    def from_tokens(v):
        v = v.reshape((blocks, half, 4, 2) + v.shape[1:])
        return jnp.moveaxis(v, 1, 3).reshape((rows, stretch) + v.shape[4:])

    def stacked(v):
        return v.reshape((blocks, half, 8) + v.shape[1:])

    def norm(v):
        v = v.astype(F32)
        scale = lax.rsqrt(jnp.mean(v * v, axis=-1, keepdims=True) + EPS)
        return (v * scale * gain).astype(BF16)

    normed = norm(to_tokens(xg.reshape(rows, stretch, width)))
    cot = to_tokens(cg.reshape(rows, stretch, width))
    before = jnp.where(s > 0, hal.reshape(rows * HALO, width), 0)

    starts = jnp.cumsum(lengths, axis=1) - lengths
    place = s * stretch - edge + jnp.arange(stretch + edge, dtype=jnp.int32)
    ident = jnp.sum((starts[:, None, :] <= place[None, :, None]).astype(jnp.int32), axis=2)
    begin = jnp.any(starts[:, None, :] == place[None, edge:, None], axis=2)
    same = [to_tokens(ident[:, k : k + stretch] == ident[:, edge:])[:, None] for k in range(taps)]
    begin = to_tokens(begin)[:, None]

    inner = jnp.dot(normed, w_inner, preferred_element_type=F32).astype(BF16)
    inner_before = jnp.dot(norm(before), w_inner, preferred_element_type=F32).astype(BF16)
    gate = jnp.dot(normed, w_gate, preferred_element_type=F32).astype(BF16).astype(F32)
    kern = conv_kernel.astype(F32)
    inner_s = stacked(inner)
    lead = inner_before.reshape(blocks, 4, HALO, ch)[:, :, HALO - edge :, :]
    lead = jnp.moveaxis(lead, 2, 1)[:, :, :, None, :]
    own_lead = inner_s[:, half - edge :].reshape(blocks, edge, 4, 2, ch)[:, :, :, :1, :]
    lead = jnp.concatenate([lead, own_lead], axis=3).reshape(blocks, edge, 8, ch)
    extended = jnp.concatenate([lead, inner_s], axis=1)
    taps_in = [extended[:, k : k + half].reshape(tokens, ch).astype(F32) for k in range(taps)]
    conv = conv_bias.astype(F32)[None, :]
    for k in range(taps):
        conv = conv + kern[k][None, :] * jnp.where(same[k], taps_in[k], 0.0)
    mixed = jax.nn.silu(conv).astype(BF16)
    mixed_f = mixed.astype(F32)
    w_sel = jnp.pad(select_proj, ((0, 0), (0, 128 - select_proj.shape[1])))
    proj = total_over_fsdp(nf, 1, jnp.dot(mixed, w_sel, preferred_element_type=F32))
    step_low = proj[:, :rank].astype(BF16)
    step_pre = jnp.dot(step_low, step_proj, preferred_element_type=F32) + step_bias.astype(F32)[None, :]
    step = jax.nn.softplus(step_pre)
    u = step * mixed_f
    stepd = jnp.where(begin, RESET, step)
    rate = -jnp.exp(log_decay.astype(F32))
    rate2 = rate * LOG2E
    gate_act = jax.nn.silu(gate)
    d_gated = times_transposed(cot, output_proj).astype(BF16).astype(F32)
    d_y = d_gated * gate_act

    coefs = coef_pieces(proj, rank, nstate)
    b, p, g = scan_ends(stepd, u, d_y, coefs, rate2, rank, count)
    run = jnp.sum(stacked(stepd), axis=1)

    def halves(v):
        v = v.reshape(v.shape[:-2] + (4, 2, ch))
        return v[..., 0, :], v[..., 1, :]

    b0, b1 = halves(b)
    p0, p1 = halves(p)
    g0, g1 = halves(g)
    r0, r1 = halves(run)
    flat = (blocks * nstate * 4, ch)
    bf, gb, tf, tb = carry_over_seq(
        reach,
        ns,
        2,
        (p1 * b0 + b1).astype(BF16).reshape(flat),
        (g0 + p0 * g1).astype(BF16).reshape(flat),
        (r0 + r1).reshape(blocks * 4, ch),
    )
    state_shape = (blocks, nstate, 4, ch)

    def gathered(ends, sums, valid):
        state = jnp.zeros(state_shape, F32)
        for j in range(reach - 1, -1, -1):
            decay = jnp.exp2(rate2[None, :, None, :] * sums[j].reshape(blocks, 1, 4, ch))
            new = decay * state + ends[j].reshape(state_shape).astype(F32)
            state = jnp.where(valid(j + 1), new, 0.0)
        return state

    h_first = gathered(bf, tf, lambda j: s - j >= 0)
    l_last = gathered(gb, tb, lambda j: s + j < ns)
    hin = jnp.stack([h_first, p0 * h_first + b0], axis=3).reshape(blocks, nstate, 8, ch)
    lin = jnp.stack([g1 + p1 * l_last, l_last], axis=3).reshape(blocks, nstate, 8, ch)

    y, pulled, slopes, coef, tot = scan_all(stepd, u, d_y, coefs, rate2, hin, lin, rank, count)
    log_decay_grad = rate * jnp.sum(tot, axis=(0, 2))
    d_step = mixed_f * pulled + slopes * LN2
    d_pre = d_step * jax.nn.sigmoid(step_pre)
    step_bias_grad = jnp.sum(d_pre, axis=0)
    d_lin = d_pre.astype(BF16)
    wide = jnp.pad(step_proj, ((0, 128 - rank), (0, 0)))
    part = times_transposed(d_lin, wide) + coef
    d_proj = total_over_fsdp(nf, 3, part).astype(BF16)

    skip = skip_gain.astype(F32)[None, :]
    y_full = y + skip * mixed_f
    gated = (y_full * gate_act).astype(BF16)
    out_part = jnp.dot(from_tokens(gated).reshape(tokens, ch), output_proj, preferred_element_type=F32)
    out_sum = share_over_fsdp(nf, 4, out_part.astype(BF16).reshape(nf, rd * stretch, width))
    own = residual.reshape(rd * stretch, width).astype(F32)
    layer_output = (own + out_sum).astype(BF16).reshape(rd, stretch, width)
    output_grad = rows_inner(gated, cot)
    d_gate = (d_gated * y_full * silu_slope(gate)).astype(BF16)
    gate_grad = rows_inner(normed, d_gate).astype(BF16)
    gate_grad = swap_over_fsdp(nf, 5, gate_grad.reshape(nf, width // nf, ch))
    skip_grad = jnp.sum(d_y * mixed_f, axis=0)
    step_grad = rows_inner(step_low, d_lin)

    w_sel_t = w_sel
    select_grad = rows_inner(mixed, d_proj)[:, : select_proj.shape[1]]
    d_mixed = step * pulled + d_y * skip + times_transposed(d_proj, w_sel_t)
    d_conv = d_mixed * silu_slope(conv)
    conv_bias_grad = jnp.sum(d_conv, axis=0)
    masked = [jnp.where(same[k], d_conv, 0.0) for k in range(taps)]
    kernel_grad = jnp.stack([jnp.sum(masked[k] * jnp.where(same[k], taps_in[k], 0.0), axis=0) for k in range(taps)])
    tilted = [stacked(masked[k])[:, :edge] * kern[k][None, None, None, :] for k in range(taps)]
    over = []
    for j in range(edge):
        over.append(sum(tilted[k][:, j - k] for k in range(j + 1)))
    over = jnp.stack(over, axis=1)
    behind = back_over_seq(ns, 6, over.reshape(blocks * edge * 8, ch)).reshape(blocks, edge, 4, 2, ch)
    behind = jnp.where(s + 1 < ns, behind[:, :, :, :1], 0.0)
    back = jnp.concatenate([over.reshape(blocks, edge, 4, 2, ch)[:, :, :, 1:], behind], axis=3)
    back = back.reshape(blocks, edge, 8, ch)
    d_inner = jnp.zeros((blocks, half, 8, ch), F32)
    for k in range(taps):
        ahead = edge - k
        d_inner = d_inner + jnp.pad(
            stacked(masked[k])[:, ahead:] * kern[k][None, None, None, :], ((0, 0), (0, ahead), (0, 0), (0, 0))
        )
    d_inner = d_inner + jnp.pad(back, ((0, 0), (half - edge, 0), (0, 0), (0, 0)))
    d_inner = d_inner.reshape(tokens, ch).astype(BF16)
    inner_grad = rows_inner(normed, d_inner).astype(BF16)
    inner_grad = swap_over_fsdp(nf, 7, inner_grad.reshape(nf, width // nf, ch))
    d_norm_part = times_transposed(from_tokens(d_inner).reshape(tokens, ch), w_inner) + times_transposed(
        from_tokens(d_gate).reshape(tokens, ch), w_gate
    )
    d_normed = share_over_fsdp(nf, 8, d_norm_part.astype(BF16).reshape(nf, rd * stretch, width))
    scale = lax.rsqrt(jnp.mean(own * own, axis=1, keepdims=True) + EPS)
    hat = own * scale
    gain_grad = jnp.sum(d_normed * hat, axis=0)
    d_hat = d_normed * gain
    d_flat = scale * (d_hat - hat * jnp.mean(d_hat * hat, axis=1, keepdims=True))
    own_cot = out_cotangent.reshape(rd * stretch, width).astype(F32)
    residual_grad = (own_cot + d_flat).reshape(rd, stretch, width)

    def sides(v):
        return jnp.moveaxis(v, 0, 1).reshape(width // nf, nf * ch)

    early = lax.psum((output_grad.astype(BF16), sides(gate_grad)), "seq")
    late = lax.psum(sides(inner_grad), "seq")
    tiny = lax.psum((select_grad, step_grad, kernel_grad, conv_bias_grad, step_bias_grad, log_decay_grad, skip_grad), "seq")
    gains = lax.psum_scatter(lax.psum(gain_grad, "seq"), "fsdp", scatter_dimension=0, tiled=True)
    input_grad = jnp.concatenate([late, early[1]], axis=1).astype(F32)
    return (
        layer_output,
        residual_grad,
        gains,
        input_grad,
        tiny[2],
        tiny[3],
        tiny[0],
        tiny[1],
        tiny[4],
        tiny[5],
        tiny[6],
        early[0].astype(F32),
    )


def solution(mesh):
    nf, ns = mesh.shape["fsdp"], mesh.shape["seq"]
    in_specs = (
        P("fsdp", "seq", None),
        P("fsdp", "seq", None),
        P("fsdp", None),
        P("fsdp"),
        P("fsdp", None),
        P(None, "fsdp"),
        P("fsdp"),
        P("fsdp", None),
        P(None, "fsdp"),
        P("fsdp"),
        P(None, "fsdp"),
        P("fsdp"),
        P("fsdp", None),
    )
    out_specs = (
        P("fsdp", "seq", None),
        P("fsdp", "seq", None),
        P("fsdp"),
        P("fsdp", None),
        P(None, "fsdp"),
        P("fsdp"),
        P("fsdp", None),
        P(None, "fsdp"),
        P("fsdp"),
        P(None, "fsdp"),
        P("fsdp"),
        P("fsdp", None),
    )
    return jax.shard_map(
        functools.partial(shards, nf, ns), mesh=mesh, in_specs=in_specs, out_specs=out_specs, check_vma=False
    )
```

time: 3020 us -> 521 us (0.17)
  other arithmetic: 1600 us -> 48 us
  local copies, waits for them, and re-layouts: 725 us -> 60.3 us
  waiting for transfers between devices: 472 us -> 94.9 us
  Pallas kernels: 0 us -> 217 us
  blocking collectives: 102 us -> 41.9 us
    reduce_sum x532 -> x7, other arithmetic: 721 us -> 6.56 us  [the longest x2 3.63 us: norm(): scale = lax.rsqrt(jnp.mean(v * v, axis=-1, keepdims=True) + EPS)]
    dynamic_slice x1344 -> x0, local copies, waits for them, and re-layouts: 483 us -> none  [the longest x1280 452 us: block_forward(): lax.scan(block_advance, state, (step_t, enter_t, read_t, mixed_t, keep_t))]
    add x282 -> x5, other arithmetic: 463 us -> 0.57 us  [the longest x1 0.28 us: shards(): p0 * h_first + b0]
    dynamic_update_slice x512 -> x0, other arithmetic: 364 us -> none  [the longest x256 356 us: advance_states(): return lax.scan(advance_advance, state, (step_t, enter_t, mixed_t, keep_t))]
    reduce_scatter x5 -> x0, waiting for transfers between devices: 230 us -> none  [the longest x1 129 us: shards(): lax.psum_scatter(input_grad, 'fsdp', scatter_dimension=0, tiled=True)]
    pallas_call x0 -> x11, Pallas kernels: none -> 217 us  [the longest x1 53.3 us: enter_all(): pl.pallas_call(functools.partial(enter_kernel, nf, ns, ch, inner), out_sh...]
    psum x1 -> x2, waiting for transfers between devices: 189 us -> 94.9 us  [the longest x1 63.4 us: shards(): lax.psum((select_grad, step_grad, kernel_grad, conv_bias_grad, step_bias_...]
    mul x816 -> x2, local copies, waits for them, and re-layouts: 55 us -> 0.01 us  [gathered(): rate2[None, :, None, :] * sums[j].reshape(blocks, 1, 4, ch)]
where the time goes in v1:
time: 521 us; the launch traced here: 516 us
  Pallas kernels  217 us (42%)
  waiting for transfers between devices  94.9 us (18%)
  local copies, waits for them, and re-layouts  60.3 us (12%)
  other arithmetic  48 us (9%)
  blocking collectives  41.9 us (8%)
  matrix products  37.8 us (7%)
  between operations  15.9 us (3%)
    psum x1, waiting for transfers between devices, shards(): lax.psum((select_grad, step_grad, kernel_grad, conv_bias_grad, step_bias_...  63.4 us
    pallas_call x1, Pallas kernels, enter_all(): pl.pallas_call(functools.partial(enter_kernel, nf, ns, ch, inner), out_sh...  53.3 us
    pallas_call x1, Pallas kernels, scan_all(): pl.pallas_call(functools.partial(scan_kernel, count, groups, rank, nstate...  41 us
    psum x1, blocking collectives, shards(): lax.psum(gain_grad, 'seq')  35.7 us
    pallas_call x2, Pallas kernels, share_over_fsdp(): pl.pallas_call(functools.partial(share_kernel, nf), out_shape=jax.ShapeDt...  34.1 us
    psum x1, waiting for transfers between devices, shards(): early = lax.psum((output_grad.astype(BF16), sides(gate_grad)), 'seq')  31.5 us
    pallas_call x2, Pallas kernels, swap_over_fsdp(): pl.pallas_call(functools.partial(swap_kernel, nf), out_shape=jax.ShapeDty...  28.4 us
    pallas_call x2, Pallas kernels, total_over_fsdp(): pl.pallas_call(functools.partial(total_kernel, nf), out_shape=jax.ShapeDt...  22.7 us
  transfers between devices with their start and end apart: 2, of which 2 were waited for; matrix products, arithmetic and copies ran while one was open for 6% of the time, Pallas kernels for 7%

profile of v1, /device:TPU:0, one launch (start us, length us, event | category | flops | bytes accessed | tf_op | source)
XLA Modules:
  0.0 515.5 jit_solution(9553802539222926046)
XLA Ops:
  9.2 53.3 %enter_all.1 = (bf16[4,1,256,1024]{3,2,1,0:T(8,128)(2,1)}, bf16[4,1,256,1024]{3,2,1,0:T(8,128)(2,1)}, bf16[4,256,512]{2,1,0:T(8,128)(2,1)}, bf16[4,256,512]{2,1,...) custom-call(bf16[1,256,1024]{2,1,0:T(8,128)(2,1)} %x.17, bf16[1,256,1024]{2,1,0:T(8,128)(2,1)} %ct.1, ...), custom_call_target="tpu_custom_call" | custom-call | tf_op jit(solution)/shard_map/enter_all/pallas_call | solution.py:140
  64.2 1.5 convolution_convert_fusion.6
  65.7 2.0 convert.29
  67.8 3.5 multiply_reduce_fusion
  71.4 3.6 multiply_convert_fusion.1
  75.0 2.3 convert_element_type.378
  77.3 3.3 convolution_convert_fusion.5
  80.6 1.0 copy-done.15
  84.5 3.5 copy.165
  88.0 2.8 reshape.810
  90.9 1.3 convolution_convert_fusion.4
  92.8 1.1 copy-done.20
  94.2 5.4 %fusion.12 = (f32[512]{0:T(512)}, f32[1024,512]{1,0:T(8,128)}, bf16[1024,512]{1,0:T(8,128)(2,1)S(1)}, f32[1024,512]{1,0:T(8,128)}, bf16[1024,512]{1,0:T(8,128)(2,1)}) fusion(bf16[1024,512]{1,0:T(8,128)(2,1)S(1)} %convolution_convert_fusion.4, bf16[1024,512]{1,0:T(8,128)(2,1)S(1)} %copy-done.16, f32[512]{0:T(512)S(1)} %bitcast.233, ...), kind=kOutput, calls=%fused_computation.29 | convolution fusion | flops 1091567104 | bytes 12622848 | tf_op jit(solution)/shard_map/dot_general | solution.py:716
  100.0 11.3 %total_over_fsdp.2 = f32[1024,128]{1,0:T(8,128)S(1)} custom-call(f32[1024,128]{1,0:T(8,128)S(1)} %fusion.65.part), custom_call_target="tpu_custom_call" | custom-call | tf_op jit(solution)/shard_map/total_over_fsdp/pallas_call | solution.py:195
  111.8 1.0 subtract_convert_fusion
  112.8 3.4 bitcast_reduce_fusion
  116.2 4.2 convert_multiply_fusion.3.u
  120.5 1.3 fusion.61.proj
  121.7 1.7 copy-done.1
  123.4 1.6 copy-done.4
  125.0 1.6 copy-done.5
  126.6 15.0 %scan_ends.1 = (f32[1,16,8,512]{3,2,1,0:T(8,128)S(1)}, f32[1,16,8,512]{3,2,1,0:T(8,128)S(1)}, f32[1,16,8,512]{3,2,1,0:T(8,128)S(1)}) custom-call(f32[1024,512]{1,0:T(8,128)S(1)} %copy-done.4, f32[1024,512]{1,0:T(8,128)S(1)} %copy-done.1, f32[1024,512]{1,0:T(8,128)S(1)} %copy-done.5, bf16[1024,128]{1,0:T(8,128)(2,1)S(1)} %fusion.61.proj, ...), custom_call_target="tpu_custom_call" | custom-call | flops 67108864 | bytes 6291456 | tf_op jit(solution)/shard_map/scan_ends/pallas_call | solution.py:478
  142.9 16.7 %carry_over_seq.1 = (bf16[4,64,512]{2,1,0:T(8,128)(2,1)S(1)}, bf16[4,64,512]{2,1,0:T(8,128)(2,1)S(1)}, f32[4,4,512]{2,1,0:T(4,128)S(1)}, f32[4,4,512]{2,1,0:T(4,128)S(1)}) custom-call(bf16[64,512]{1,0:T(8,128)(2,1)S(1)} %convert_element_type.401.b, bf16[64,512]{1,0:T(8,128)(2,1)S(1)} %convert_element_type.403.g, f32[4,512]{1,0:T(4,128)S(1)} %fusion.75.t), custom_call_target="tpu_custom_call" | custom-call | tf_op jit(solution)/shard_map/carry_over_seq/pallas_call | solution.py:350
  163.1 41.0 %scan_all.1 = (f32[1024,512]{1,0:T(8,128)}, f32[1024,512]{1,0:T(8,128)}, f32[1024,512]{1,0:T(8,128)}, f32[1024,128]{1,0:T(8,128)}, f32[1,16,8,512]{3,2,1,0:T(8,128)}) custom-call(f32[1024,512]{1,0:T(8,128)} %get-tuple-element.149.step, f32[1024,512]{1,0:T(8,128)} %convert_multiply_fusion.3.u, f32[1024,512]{1,0:T(8,128)} %get-tuple-element.139.dy, ...), custom_call_target="tpu_custom_call" | custom-call | flops 167772160 | bytes 12582912 | tf_op jit(solution)/shard_map/scan_all/pallas_call | solution.py:597
  204.1 6.2 %fusion.3 = (bf16[1024,512]{1,0:T(8,128)(2,1)}, bf16[1024,512]{1,0:T(8,128)(2,1)}, f32[512]{0:T(512)S(1)}, bf16[1024,512]{1,0:T(8,128)(2,1)S(1)}) fusion(bf16[1024,512]{1,0:T(8,128)(2,1)} %copy-done.24, bf16[1024,512]{1,0:T(8,128)(2,1)} %get-tuple-element.196, f32[1024,512]{1,0:T(8,128)} %get-tuple-element.67, bf16[1024,512]{1,0:T(8,128)(2,1)S(1)} %copy-done.8, ...), kind=kLoop, calls=%fused_computation.20 | loop fusion | flops 14679552 | bytes 14686208 | tf_op jit(solution)/shard_map/convert_element_type | solution.py:797
  210.4 0.9 copy-done.9
  211.8 11.3 %total_over_fsdp.3 = f32[1024,128]{1,0:T(8,128)S(1)} custom-call(f32[1024,128]{1,0:T(8,128)S(1)} %convolution_add_fusion.part), custom_call_target="tpu_custom_call" | custom-call | tf_op jit(solution)/shard_map/total_over_fsdp/pallas_call | solution.py:195
  223.2 2.2 multiply_multiply_fusion
  225.5 2.2 fusion.25
  227.7 1.6 slice_multiply_fusion.2
  229.2 1.6 slice_multiply_fusion
  230.8 1.6 slice_multiply_fusion.1
  233.3 5.8 %copy.164 = f32[1,4,2,128,1024]{4,2,1,3,0:T(2,128)} copy(bf16[1,4,2,128,1024]{4,3,2,1,0:T(8,128)(2,1)} %bitcast.194) | data formatting | bytes 6291456 | tf_op jit(solution)/shard_map/convert_element_type | solution.py:699
  239.1 5.5 %back_over_seq.1 = f32[24,512]{1,0:T(8,128)} custom-call(f32[24,512]{1,0:T(8,128)} %maximum_bitcast_fusion.e), custom_call_target="tpu_custom_call" | custom-call | tf_op jit(solution)/shard_map/back_over_seq/pallas_call | solution.py:385
  245.6 4.6 fusion.28
  250.3 2.2 convolution_convert_fusion.2
  252.5 14.2 %swap_over_fsdp.2 = bf16[4,256,512]{2,1,0:T(8,128)(2,1)} custom-call(bf16[4,256,512]{2,1,0:T(8,128)(2,1)} %bitcast.210), custom_call_target="tpu_custom_call" | custom-call | tf_op jit(solution)/shard_map/swap_over_fsdp/pallas_call | solution.py:280
  266.7 2.5 copy.128
  269.2 6.1 %reshape.851 = f32[1024,1024]{1,0:T(8,128)} reshape(f32[1,128,4,2,1024]{4,3,2,1,0:T(2,128)} %bitcast.192) | data formatting | bytes 8388608 | tf_op jit(solution)/shard_map/convert_element_type | solution.py:699
  275.3 4.8 fusion.31
  280.1 14.2 %swap_over_fsdp.3 = bf16[4,256,512]{2,1,0:T(8,128)(2,1)} custom-call(bf16[4,256,512]{2,1,0:T(8,128)(2,1)} %bitcast.209), custom_call_target="tpu_custom_call" | custom-call | tf_op jit(solution)/shard_map/swap_over_fsdp/pallas_call | solution.py:280
  294.3 2.3 copy.129
  296.5 4.2 convolution_convert_fusion.1
  300.8 1.0 fusion.62
  301.8 2.2 fusion.53
  304.0 2.7 copy.126
  306.7 2.2 reshape.830
  309.1 1.2 reshape.820
  310.4 2.9 fusion.92
  314.5 1.3 add_convert_fusion
  315.8 17.1 %share_over_fsdp.3 = f32[256,1024]{1,0:T(8,128)S(1)} custom-call(bf16[4,256,1024]{2,1,0:T(8,128)(2,1)S(1)} %bitcast.190), custom_call_target="tpu_custom_call" | custom-call | tf_op jit(solution)/shard_map/share_over_fsdp/pallas_call | solution.py:247
  333.3 6.2 %all-reduce.8 = f32[1024]{0:T(1024)S(1)} all-reduce(f32[1024]{0:T(1024)S(1)} %get-tuple-element.125), channel_id=2, replica_groups=mesh['fsdp'=4,'seq'=8] {'fsdp'}, use_global_device_ids=true, to_apply=%region_10.11.clone | all-reduce | flops 1024 | bytes 8192
  339.6 1.5 copy.125
  341.1 1.3 convolution_convert_fusion
  342.4 17.1 %share_over_fsdp.2 = f32[256,1024]{1,0:T(8,128)S(1)} custom-call(bf16[4,256,1024]{2,1,0:T(8,128)(2,1)S(1)} %bitcast.191), custom_call_target="tpu_custom_call" | custom-call | tf_op jit(solution)/shard_map/share_over_fsdp/pallas_call | solution.py:247
  360.8 2.8 fusion.39
  363.6 35.7 %all-reduce.9 = (f32[256]{0:T(256)}, f32[4,512]{1,0:T(4,128)}, f32[512]{0:T(512)}, f32[512]{0:T(512)}, f32[16,512]{1,0:T(8,128)}, /*index=5*/f32[512]{0:T(512)}) all-reduce(f32[256]{0:T(256)S(1)} %dynamic-slice.15, f32[4,512]{1,0:T(4,128)S(1)} %pad_maximum_fusion.6, ...), channel_id=1, replica_groups=mesh['fsdp'=4,'seq'=8] {'seq'}, use_global_device_ids=true, to_apply=%region_9.10 | all-reduce | flops 12032 | bytes 96256 | tf_op jit(solution)/shard_map/psum | solution.py:847
  399.3 31.5 %all-reduce.17.cloned.1.call-done = (bf16[256,2048]{0,1:T(8,128)(2,1)}, bf16[256,2048]{0,1:T(8,128)(2,1)}, bf16[512,1024]{1,0:T(8,128)(2,1)}) async-done(((bf16[256,2048]{0,1:T(8,128)(2,1)}, bf16[256,2048]{0,1:T(8,128)(2,1)}, bf16[512,1024]{1,0:T(8,128)(2,1)}), (bf16[256,2048]{0,1:T(8,128)(2,1)}, bf16[256,2048]{0,1:T(8,128)(2,1)}, bf16[512,1024]{1,0:T(8,128)(2,1)})) %all-reduce.17.cloned.1.call-update) | async-done | bytes 3145744 | tf_op jit(solution)/shard_map/psum | solution.py:844
  430.8 3.8 maximum_convert_fusion
  434.6 5.7 %copy.130 = f32[256,4096]{1,0:T(8,128)} copy(f32[256,4096]{0,1:T(8,128)} %maximum_convert_fusion) | data formatting | bytes 8388608
  440.3 1.6 convert_element_type.440
  441.9 63.4 %all-reduce.15.cloned.1.call-done = (f32[512,96]{0,1:T(8,128)}, f32[64,512]{1,0:T(8,128)}) async-done(((f32[512,96]{0,1:T(8,128)}, f32[64,512]{1,0:T(8,128)}), (f32[512,96]{0,1:T(8,128)}, f32[64,512]{1,0:T(8,128)})) %all-reduce.15.cloned.1.call-update) | async-done | bytes 327696 | tf_op jit(solution)/shard_map/psum | solution.py:846
  505.3 1.6 copy.172
  506.9 1.6 copy.173
  (179 shorter events, 18.3 us)
Async XLA Ops:
  7.2 83.7 %copy-start = (bf16[512,1024]{1,0:T(8,128)(2,1)S(1)}, bf16[512,1024]{1,0:T(8,128)(2,1)}, u32[]{:S(2)}) copy-start(bf16[512,1024]{1,0:T(8,128)(2,1)} %param.29) | copy-start | bytes 3145732
  7.2 423.6 %all-reduce.17.cloned.1.call-start = ((), (), s32[]{:S(2)}) async-start(), calls=%async_computation.1 | async-start | bytes 6291456 | tf_op jit(solution)/shard_map/psum | solution.py:844
  8.7 0.6 copy-start.35
  77.3 7.2 %copy-start.22 = (bf16[4,1,256,1024]{3,2,1,0:T(8,128)(2,1)S(1)}, bf16[4,1,256,1024]{3,2,1,0:T(8,128)(2,1)}, u32[]{:S(2)}) copy-start(bf16[4,1,256,1024]{3,2,1,0:T(8,128)(2,1)} %get-tuple-element.58) | copy-start | bytes 6291460
  80.5 1.0 copy-start.15
  88.0 2.8 copy-start.36
  88.0 2.8 copy-start.38
  90.8 1.4 copy-start.12
  90.9 1.9 copy-start.16
  90.9 3.0 copy-start.20
  90.9 3.2 copy-start.26
  92.2 7.3 %copy-start.24 = (bf16[1024,512]{1,0:T(8,128)(2,1)}, bf16[1024,512]{1,0:T(8,128)(2,1)S(1)}, u32[]{:S(2)}) copy-start(bf16[1024,512]{1,0:T(8,128)(2,1)S(1)} %convolution_convert_fusion.4) | copy-start | bytes 3145732
  94.2 5.4 %copy-start.30 = (bf16[512,96]{0,1:T(8,128)(2,1)S(1)}, bf16[512,96]{0,1:T(8,128)(2,1)}, u32[]{:S(2)}) copy-start(bf16[512,96]{0,1:T(8,128)(2,1)} %param.24) | copy-start | bytes 294916
  99.5 16.7 %copy-start.7 = (bf16[1024,512]{1,0:T(8,128)(2,1)}, bf16[1024,512]{1,0:T(8,128)(2,1)S(1)}, u32[]{:S(2)}) copy-start(bf16[1024,512]{1,0:T(8,128)(2,1)S(1)} %get-tuple-element.140) | copy-start | bytes 3145732
  99.5 12.3 %copy-start.39 = (bf16[512]{0:T(512)(128)(2,1)S(1)}, bf16[512]{0:T(512)(128)(2,1)}, u32[]{:S(2)}) copy-start(bf16[512]{0:T(512)(128)(2,1)} %param.26) | copy-start | bytes 3076
  99.5 13.2 %copy-start.32 = (bf16[64,512]{1,0:T(8,128)(2,1)S(1)}, bf16[64,512]{1,0:T(8,128)(2,1)}, u32[]{:S(2)}) copy-start(bf16[64,512]{1,0:T(8,128)(2,1)} %param.25) | copy-start | bytes 196612
  116.2 4.2 copy-start.34
  120.4 21.1 %copy-start.3 = (f32[4,4,512]{2,1,0:T(4,128)}, f32[4,4,512]{2,1,0:T(4,128)S(1)}, u32[]{:S(2)}) copy-start(f32[4,4,512]{2,1,0:T(4,128)S(1)} %reshape.812.rate) | copy-start | bytes 98308
  121.7 19.9 %copy-start.2 = (bf16[1024,128]{1,0:T(8,128)(2,1)}, bf16[1024,128]{1,0:T(8,128)(2,1)S(1)}, u32[]{:S(2)}) copy-start(bf16[1024,128]{1,0:T(8,128)(2,1)S(1)} %fusion.61.proj) | copy-start | bytes 786436
  121.7 1.7 copy-start.1
  123.4 1.6 copy-start.4
  125.0 1.6 copy-start.5
  161.4 1.7 copy-start.40
  163.1 41.0 %copy-start.8 = (bf16[1024,512]{1,0:T(8,128)(2,1)S(1)}, bf16[1024,512]{1,0:T(8,128)(2,1)}, u32[]{:S(2)}) copy-start(bf16[1024,512]{1,0:T(8,128)(2,1)} %copy-done.7) | copy-start | bytes 3145732
  204.1 7.3 %copy-start.28 = (f32[1024,128]{1,0:T(8,128)S(1)}, f32[1024,128]{1,0:T(8,128)}, u32[]{:S(2)}) copy-start(f32[1024,128]{1,0:T(8,128)} %get-tuple-element.70) | copy-start | bytes 1572868
  204.1 7.2 %copy-start.33 = (bf16[64,512]{1,0:T(8,128)(2,1)S(1)}, bf16[64,512]{1,0:T(8,128)(2,1)}, u32[]{:S(2)}) copy-start(bf16[64,512]{1,0:T(8,128)(2,1)} %param.25) | copy-start | bytes 196612
  204.1 19.0 %copy-start.13 = (f32[1024,512]{1,0:T(8,128)S(1)}, f32[1024,512]{1,0:T(8,128)}, u32[]{:S(2)}) copy-start(f32[1024,512]{1,0:T(8,128)} %get-tuple-element.197) | copy-start | bytes 6291460
  204.1 19.0 %copy-start.23 = (f32[1024,512]{1,0:T(8,128)S(1)}, f32[1024,512]{1,0:T(8,128)}, u32[]{:S(2)}) copy-start(f32[1024,512]{1,0:T(8,128)} %get-tuple-element.68) | copy-start | bytes 6291460
  204.1 19.0 %copy-start.42 = (f32[1024,512]{1,0:T(8,128)S(1)}, f32[1024,512]{1,0:T(8,128)}, u32[]{:S(2)}) copy-start(f32[1024,512]{1,0:T(8,128)} %get-tuple-element.141) | copy-start | bytes 6291460
  210.4 1.0 copy-start.9
  210.4 12.8 %copy-start.6 = (f32[1024,512]{1,0:T(8,128)S(1)}, f32[1024,512]{1,0:T(8,128)}, u32[]{:S(2)}) copy-start(f32[1024,512]{1,0:T(8,128)} %get-tuple-element.139.dy) | copy-start | bytes 6291460
  210.4 12.8 %copy-start.31 = (bf16[512,96]{0,1:T(8,128)(2,1)S(1)}, bf16[512,96]{0,1:T(8,128)(2,1)}, u32[]{:S(2)}) copy-start(bf16[512,96]{0,1:T(8,128)(2,1)} %param.24) | copy-start | bytes 294916
  223.2 2.3 copy-start.17
  225.5 2.2 copy-start.11
  245.6 4.6 copy-start.21
  250.3 2.3 copy-start.18
  300.7 204.6 %all-reduce.15.cloned.1.call-start = ((), (), s32[]{:S(2)}) async-start(), calls=%async_computation | async-start | bytes 655360 | tf_op jit(solution)/shard_map/psum | solution.py:846
  304.0 4.9 copy-start.14
  304.0 5.1 copy-start.10
  310.4 2.9 copy-start.19
  313.3 1.2 copy-start.27
  315.8 23.7 %copy-start.29 = (f32[1,16,8,512]{3,2,1,0:T(8,128)S(1)}, f32[1,16,8,512]{3,2,1,0:T(8,128)}, u32[]{:S(2)}) copy-start(f32[1,16,8,512]{3,2,1,0:T(8,128)} %get-tuple-element.71) | copy-start | bytes 786436
  342.4 17.1 %copy-start.41 = (u32[32]{0:T(128)S(1)}, u32[32]{0:T(128)}, u32[]{:S(2)}) copy-start(u32[32]{0:T(128)} %constant.139) | copy-start | bytes 388
  360.8 2.8 copy-start.37
  434.6 5.7 %copy-start.25 = (bf16[512,1024]{1,0:T(8,128)(2,1)S(1)}, bf16[512,1024]{1,0:T(8,128)(2,1)}, u32[]{:S(2)}) copy-start(bf16[512,1024]{1,0:T(8,128)(2,1)} %get-tuple-element.137) | copy-start | bytes 3145732
Sparse Core Ops, SparseCore 0:
  300.9 129.8 all-reduce.16
  435.2 70.1 all-reduce.14

commit v2 on v1

v2 whole, which is shorter than its diff:
```python
import functools
import math

import jax
import jax.numpy as jnp
from jax import lax
from jax.experimental import pallas as pl
from jax.experimental.pallas import tpu as pltpu
from jax.sharding import PartitionSpec as P

EPS = 1e-05
MESH = pl.DeviceIdType.MESH
LOG2E = math.log2(math.e)
LN2 = math.log(2.0)
BF16 = jnp.bfloat16
F32 = jnp.float32
ANY = pl.BlockSpec(memory_space=pl.ANY)
VMEM = pl.BlockSpec(memory_space=pltpu.VMEM)
RESET = 1e30
HALO = 16
DOCS = 8


def here():
    return lax.axis_index("fsdp"), lax.axis_index("seq")


def greet(peers):
    barrier = pltpu.get_barrier_semaphore()
    count = 0
    for ok, device in peers:
        if ok is None:
            pl.semaphore_signal(barrier, inc=1, device_id=device, device_id_type=MESH)
            count = count + 1
        else:

            @pl.when(ok)
            def _():
                pl.semaphore_signal(barrier, inc=1, device_id=device, device_id_type=MESH)

            count = count + ok.astype(jnp.int32)
    pl.semaphore_wait(barrier, count)


def remote(src, dst, send, recv, device):
    return pltpu.make_async_remote_copy(
        src_ref=src, dst_ref=dst, send_sem=send, recv_sem=recv, device_id=device, device_id_type=MESH
    )


def comm_params(cid, vmem=None):
    return pltpu.CompilerParams(collective_id=cid, has_side_effects=True, vmem_limit_bytes=vmem)


class Wire:
    def __init__(self, ssem, rsem):
        self.ssem, self.rsem, self.copies, self.done = ssem, rsem, [], []

    def send(self, src, dst, device):
        k = len(self.copies)
        cp = remote(src, dst, self.ssem.at[k], self.rsem.at[k], device)
        self.copies.append(cp)
        cp.start()
        return cp

    def sent(self, cp):
        cp.wait_send()
        self.done.append(cp)

    def drain(self):
        for cp in self.copies:
            if all(cp is not other for other in self.done):
                cp.wait_send()


LEAD = 24


def rows_at(base, size, unit=8):
    return pl.ds(pl.multiple_of(base, unit), size)


def split_at(i, n):
    return lax.div(i, n), lax.rem(i, n)


def front_kernel(nf, ns, rd, rank, nstate, sems, *refs):
    (x, ct, w, sm, vecs, w_sel, w_step, w_out) = refs[:8]
    (normed_o, cg_o, ext_o, slope_o, mix_o, dy_o, ga_o, dgs_o, step_o, beg_o, proj_o, packed_o, wi_o, wg_o, gain_o) = refs[8:23]
    (xg, cg, wi, wg, sg, hal, hres, vbuf, gbuf, ext, slope, mix, mixb, dy, ga, dgs, step, beg, part, got, mid, far, proj, packed) = refs[
        23:47
    ]
    ssem, rsem, hsem, hrem, lsem, osem = refs[47:]
    f, s = here()
    core, b = lax.rem(f, 2), lax.rem(s, 2)
    stretch = x.shape[1]
    half = stretch // 2
    dmodel = xg.shape[1]
    ch = wi.shape[1]
    groups = ch // 128
    rows = nf * rd
    blocks = rows // 4
    tokens = rows * stretch
    drow = w.shape[0]
    inner_all = w.shape[1] // 2
    chips = list(range(2, nf, 2))
    peer = (lax.bitwise_xor(f, 1), s)
    beside = (f, lax.bitwise_xor(s, 1))
    up, down = s + 1, s - 1
    has_up, has_down = up < ns, down >= 0

    def fdev(i):
        return (lax.bitwise_xor(f, i), s)

    greeted = [(None, fdev(i)) for i in range(1, nf)] + [(None, beside)]
    for i in range(nf):
        greeted.append((has_up, (lax.bitwise_xor(f, i), up)))
        greeted.append((has_down, (lax.bitwise_xor(f, i), down)))
    greet(greeted)
    wire = Wire(ssem, rsem)

    def act_rows(who):
        return rows_at(who * (rd * stretch), rd * stretch, 16)

    def wcols(who, base, start, size):
        return w.at[pl.ds(start, size), pl.ds(pl.multiple_of(base + who * ch, 128), ch)]

    def wrows(who, start, size):
        return pl.ds(pl.multiple_of(who * drow + start, 16), size)

    half_rows = drow // 2
    mine = pl.multiple_of(b * half_rows, 16)

    locals_ = []

    def local(src, dst):
        cp = pltpu.make_async_copy(src, dst, lsem.at[len(locals_)])
        locals_.append(cp)
        cp.start()
        return cp

    x2 = [x.at[q] for q in range(rd)]
    smalls = [wire.send(sm, sg.at[f], fdev(i)) for i in range(1, nf)]
    own_x = [local(x2[q], xg.at[rows_at((f * rd + q) * stretch, stretch, 16)]) for q in range(rd)]
    own_s = local(sm, sg.at[f])

    def send_rows(src, dst):
        if rd == 1:
            return [wire.send(src.at[0], dst.at[act_rows(f)], fdev(i)) for i in [1] + chips]
        return [wire.send(src, dst.at[act_rows(f)], fdev(i)) for i in [1] + chips]

    def send_weight(base, dst):
        out = [wire.send(wcols(peer[0], base, 0, drow), dst.at[wrows(f, 0, drow)], peer)]
        for i in range(2, nf):
            out.append(
                wire.send(wcols(lax.bitwise_xor(f, i), base, mine, half_rows), dst.at[wrows(f, mine, half_rows)], fdev(i))
            )
        return out

    xs = send_rows(x, xg)
    wis = send_weight(0, wi)
    halos = [
        remote(
            x.at[:, pl.ds(stretch - HALO, HALO), :],
            hal.at[pl.ds(f * rd, rd)],
            hsem.at[i],
            hrem.at[i],
            (lax.bitwise_xor(f, i), up),
        )
        for i in range(nf)
    ]

    @pl.when(has_up)
    def _():
        for cp in halos:
            cp.start()

    own_wi = local(wcols(f, 0, 0, drow), wi.at[wrows(f, 0, drow)])
    cs = send_rows(ct, cg)
    wgs = send_weight(inner_all, wg)
    own_c = [local(ct.at[q], cg.at[rows_at((f * rd + q) * stretch, stretch, 16)]) for q in range(rd)]
    own_wg = local(wcols(f, inner_all, 0, drow), wg.at[wrows(f, 0, drow)])

    own_s.wait()
    for cp in smalls:
        cp.wait_recv()
    table = sg[0]
    for k in range(1, nf):
        table = table + sg[k]
    gain = jnp.concatenate([table[q : q + 1, :] for q in range(dmodel // 128)], axis=1)
    gain_o[...] = table
    sub = lax.broadcasted_iota(jnp.int32, (8, 128), 0)
    for n in range(blocks):
        lens = jnp.zeros((8, 128), F32)
        for q in range(4):
            r = n * 4 + q
            line = sg[r // rd, 8 + r % rd : 9 + r % rd, :]
            lens = jnp.where(sub // 2 == q, jnp.broadcast_to(line, (8, 128)), lens)
        starts = [jnp.zeros((8, 128), F32)]
        for j in range(DOCS - 1):
            starts.append(starts[-1] + jnp.broadcast_to(lens[:, j : j + 1], (8, 128)))
        first = (s * stretch + (sub % 2) * half).astype(F32)

        def mark(t, carry, n=n, starts=starts, first=first):
            place = first + (t - 2).astype(F32)
            hit = starts[0] == place
            for j in range(1, DOCS):
                hit = jnp.logical_or(hit, starts[j] == place)
            beg[rows_at(n * (half + 2) * 8 + t * 8, 8), :] = jnp.where(hit, RESET, 0.0)
            return carry

        lax.fori_loop(0, half + 2, mark, 0)

    def norm_rows(ref, start, size):
        def one(i, carry):
            at_ = rows_at(start + i * 32, 32, 16)
            v = ref[at_, :].astype(F32)
            scale = lax.rsqrt(jnp.sum(v * v, axis=1, keepdims=True) * (1.0 / dmodel) + EPS)
            ref[at_, :] = (v * scale * gain).astype(BF16)
            return carry

        lax.fori_loop(0, size // 32, one, 0)

    span = rd * stretch
    for cp in own_x:
        cp.wait()
    norm_rows(xg, f * span, span)
    xs[0].wait_recv()
    norm_rows(xg, peer[0] * span, span)
    xf = []
    for n, i in enumerate(chips):
        xs[1 + n].wait_recv()
        block = act_rows(lax.bitwise_xor(f, i))
        xf.append(wire.send(xg.at[block], xg.at[block], peer))
    for n, i in enumerate(chips):
        xf[n].wait_recv()
        norm_rows(xg, lax.bitwise_xor(f, i + 1) * span, span)
        wire.sent(xf[n])
        norm_rows(xg, lax.bitwise_xor(f, i) * span, span)
    wif = []
    for n, i in enumerate(range(2, nf)):
        wis[1 + n].wait_recv()
        block = wrows(lax.bitwise_xor(f, i), mine, half_rows)
        wif.append(wire.send(wi.at[block], wi.at[block], beside))

    @pl.when(has_down)
    def _():
        for cp in halos:
            cp.wait_recv()

    hal_rows = rows * HALO
    hflat = vbuf
    for r in range(rows):
        v = hal[r].astype(F32)
        scale = lax.rsqrt(jnp.sum(v * v, axis=1, keepdims=True) * (1.0 / dmodel) + EPS)
        hflat[r * HALO : (r + 1) * HALO, :] = jnp.where(s > 0, v * scale * gain, 0.0).astype(BF16)
    own_wi.wait()
    wis[0].wait_recv()
    for cp in wif:
        cp.wait_recv()
    out_copies = []

    def put(src, dst):
        cp = pltpu.make_async_copy(src, dst, osem.at[len(out_copies)])
        out_copies.append(cp)
        cp.start()

    put(xg, normed_o)
    put(beg, beg_o)
    put(wi, wi_o)

    def inner_row(r, carry):
        v = jnp.dot(xg[rows_at(r * stretch, stretch, 16), :], wi[...], preferred_element_type=F32)
        v = v.astype(BF16).astype(F32)
        n, q = split_at(r, 4)
        base = n * (half * 8 + LEAD) + LEAD + q * 2
        for g in range(2):
            for d in range(groups):
                ext[d, pl.ds(base + g, half, stride=8), :] = v[g * half : (g + 1) * half, cut(d)]
        return carry

    lax.fori_loop(0, rows, inner_row, 0)
    hv = jnp.dot(hflat[...], wi[...], preferred_element_type=F32).astype(BF16).astype(F32)
    for d in range(groups):
        hres[d] = hv[:, cut(d)]
    for n in range(blocks):
        base = n * (half * 8 + LEAD)
        for d in range(groups):
            for j in range(3):
                before = hres[d, pl.ds(n * 4 * HALO + HALO - 3 + j, 4, stride=HALO), :]
                ext[d, pl.ds(base + j * 8, 4, stride=2), :] = before
                own = ext[d, pl.ds(base + LEAD + (half - 3 + j) * 8, 4, stride=2), :]
                ext[d, pl.ds(base + j * 8 + 1, 4, stride=2), :] = own
    put(ext, ext_o)

    span_t = half * 8
    chunk = 64
    per = span_t // chunk

    def conv_chunk(idx, carry):
        nd, c = split_at(idx, per)
        n, d = split_at(nd, groups)
        base = n * (span_t + LEAD) + c * chunk
        bb = n * (span_t + 16) + c * chunk
        same2 = jnp.where(beg[rows_at(bb + 16, chunk), :] > 0.0, 0.0, 1.0)
        same1 = jnp.where(beg[rows_at(bb + 8, chunk), :] > 0.0, 0.0, same2)
        same0 = jnp.where(beg[rows_at(bb, chunk), :] > 0.0, 0.0, same1)
        tap = [ext[d, rows_at(base + k * 8, chunk), :] for k in range(4)]
        v = vecs[d, 4:5, :] + vecs[d, 0:1, :] * (tap[0] * same0)
        v = v + vecs[d, 1:2, :] * (tap[1] * same1) + vecs[d, 2:3, :] * (tap[2] * same2) + vecs[d, 3:4, :] * tap[3]
        sig = jax.nn.sigmoid(v)
        m = (v * sig).astype(BF16)
        at_ = rows_at(n * span_t + c * chunk, chunk)
        slope[d, at_, :] = sig * (1.0 + v * (1.0 - sig))
        mixb[d, rows_at(n * span_t + c * chunk, chunk, 16), :] = m
        mix[d, at_, :] = m.astype(F32)
        return carry

    lax.fori_loop(0, blocks * groups * per, conv_chunk, 0)
    put(slope, slope_o)
    put(mix, mix_o)

    hs = tokens // 2
    other = (1 - core) * hs
    keep = core * hs

    def project(start):
        total = None
        for d in range(groups):
            term = jnp.dot(mixb[d, rows_at(start, hs, 16), :], w_sel[d * 128 : (d + 1) * 128, :], preferred_element_type=F32)
            total = term if total is None else total + term
        part[rows_at(start, hs), :] = total

    project(other)
    one = wire.send(part.at[rows_at(other, hs)], got, peer)
    project(keep)
    one.wait_recv()
    mid[...] = part[rows_at(keep, hs), :] + got[...]
    two = [wire.send(mid, far.at[n], fdev(i)) for n, i in enumerate(chips)]

    cf = []
    for n, i in enumerate(chips):
        cs[1 + n].wait_recv()
        block = act_rows(lax.bitwise_xor(f, i))
        cf.append(wire.send(cg.at[block], cg.at[block], peer))
    wgf = []
    for n, i in enumerate(range(2, nf)):
        wgs[1 + n].wait_recv()
        block = wrows(lax.bitwise_xor(f, i), mine, half_rows)
        wgf.append(wire.send(wg.at[block], wg.at[block], beside))
    for cp in own_c + [own_wg]:
        cp.wait()
    for cp in [cs[0], wgs[0]] + cf + wgf:
        cp.wait_recv()
    put(cg, cg_o)
    put(wg, wg_o)

    def gate_row(r, carry):
        at_ = rows_at(r * stretch, stretch, 16)
        gbuf[0] = jnp.dot(xg[at_, :], wg[...], preferred_element_type=F32).astype(BF16).astype(F32)
        gbuf[1] = times_transposed(cg[at_, :], w_out[...]).astype(BF16).astype(F32)
        n, q = split_at(r, 4)
        base = n * span_t + q * 2
        for g in range(2):
            for d in range(groups):
                def some(i, carry2, g=g, d=d):
                    src = rows_at(g * half + i * 32, 32)
                    v, dg = gbuf[0, src, cut(d)], gbuf[1, src, cut(d)]
                    sig = jax.nn.sigmoid(v)
                    act = v * sig
                    dst = rows_at(r * stretch + g * half + i * 32, 32)
                    ga[dst, cut(d)] = act
                    dgs[dst, cut(d)] = dg * (sig * (1.0 + v * (1.0 - sig)))
                    dy[d, pl.ds(base + g + i * 256, 32, stride=8), :] = dg * act
                    return carry2

                lax.fori_loop(0, half // 32, some, 0)
        return carry

    lax.fori_loop(0, rows, gate_row, 0)
    put(dy, dy_o)
    put(ga, ga_o)
    put(dgs, dgs_o)

    for cp in two:
        cp.wait_recv()
    acc = mid[...]
    for n in range(len(chips)):
        acc = acc + far[n]
    proj[rows_at(keep, hs), :] = acc
    three = wire.send(proj.at[rows_at(keep, hs)], proj.at[rows_at(keep, hs)], peer)

    lane = lax.broadcasted_iota(jnp.int32, (256, 128), 1)

    def step_rows(i, carry):
        at_ = rows_at(carry + i * 256, 256)
        p = proj[at_, :]
        pre = jnp.dot(p[:, :rank].astype(BF16), w_step[...], preferred_element_type=F32)
        for d in range(groups):
            v = pre[:, cut(d)] + vecs[d, 5:6, :]
            step[d, at_, :] = jnp.maximum(v, 0.0) + jnp.log1p(jnp.exp(-jnp.abs(v)))
        top = p.astype(BF16)
        rest = p - top.astype(F32)
        second = rest.astype(BF16)
        third = (rest - second.astype(F32)).astype(BF16).astype(F32)
        width = 2 * nstate
        out = pltpu.roll(top.astype(F32), 128 - rank, 1)
        out = jnp.where(lane < width, out, pltpu.roll(second.astype(F32), (128 - rank + width) % 128, 1))
        out = jnp.where(lane < 2 * width, out, pltpu.roll(third, (128 - rank + 2 * width) % 128, 1))
        packed[rows_at(carry + i * 256, 256, 16), :] = jnp.where(lane < 3 * width, out, 0.0).astype(BF16)
        return carry

    lax.fori_loop(0, hs // 256, step_rows, keep)
    three.wait_recv()
    lax.fori_loop(0, hs // 256, step_rows, other)
    put(step, step_o)
    put(proj, proj_o)
    put(packed, packed_o)
    for cp in out_copies:
        cp.wait()
    wire.drain()

    @pl.when(has_up)
    def _():
        for cp in halos:
            cp.wait_send()

    assert len(wire.copies) == sems


def front(nf, ns, x, ct, w, sm, vecs, w_sel, w_step, w_out, rank, nstate):
    rd, stretch, width = x.shape
    drow = w.shape[0]
    ch = w_step.shape[1]
    groups = ch // 128
    rows = nf * rd
    blocks = rows // 4
    tokens = rows * stretch
    half = stretch // 2
    chips = nf // 2 - 1
    ext_rows = blocks * (half * 8 + LEAD)
    beg_rows = blocks * (half + 2) * 8
    sems = 0
    sems += nf - 1
    sems += 2 * (1 + chips)
    sems += 2 * (nf - 1)
    sems += 2 * chips + 2 * (nf - 2)
    sems += 2 + chips
    shape = jax.ShapeDtypeStruct
    wide = (groups, tokens, 128)
    out_shape = (
        shape((tokens, width), BF16),
        shape((tokens, width), BF16),
        shape((groups, ext_rows, 128), F32),
        shape(wide, F32),
        shape(wide, F32),
        shape(wide, F32),
        shape((tokens, ch), F32),
        shape((tokens, ch), F32),
        shape(wide, F32),
        shape((beg_rows, 128), F32),
        shape((tokens, 128), F32),
        shape((tokens, 128), BF16),
        shape((width, ch), BF16),
        shape((width, ch), BF16),
        shape((16, 128), F32),
    )
    v = pltpu.VMEM
    scratch = [
        v((tokens, width), BF16),
        v((tokens, width), BF16),
        v((width, ch), BF16),
        v((width, ch), BF16),
        v((nf, 16, 128), F32),
        v((rows, HALO, width), BF16),
        v((groups, rows * HALO, 128), F32),
        v((rows * HALO, width), BF16),
        v((2, stretch, ch), F32),
        v((groups, ext_rows, 128), F32),
        v(wide, F32),
        v(wide, F32),
        v(wide, BF16),
        v(wide, F32),
        v((tokens, ch), F32),
        v((tokens, ch), F32),
        v(wide, F32),
        v((beg_rows, 128), F32),
        v((tokens, 128), F32),
        v((tokens // 2, 128), F32),
        v((tokens // 2, 128), F32),
        v((chips, tokens // 2, 128), F32),
        v((tokens, 128), F32),
        v((tokens, 128), BF16),
        pltpu.SemaphoreType.DMA((sems,)),
        pltpu.SemaphoreType.DMA((sems,)),
        pltpu.SemaphoreType.DMA((nf,)),
        pltpu.SemaphoreType.DMA((nf,)),
        pltpu.SemaphoreType.DMA((2 * rd + 3,)),
        pltpu.SemaphoreType.DMA((14,)),
    ]
    return pl.pallas_call(
        functools.partial(front_kernel, nf, ns, rd, rank, nstate, sems),
        out_shape=out_shape,
        in_specs=[ANY] * 4 + [VMEM] * 4,
        out_specs=[ANY] * 14 + [VMEM],
        scratch_shapes=scratch,
        compiler_params=comm_params(0, 62 << 20),
        name="front",
    )(x, ct, w, sm, vecs, w_sel, w_step, w_out)


def carry_kernel(reach, ns, b, g, t, bf, gb, tf, tb, ssem, rsem):
    f, s = here()
    peers = []
    for j in range(1, reach + 1):
        peers.append((s + j < ns, (f, s + j)))
        peers.append((s - j >= 0, (f, s - j)))
    greet(peers)

    def copies(j):
        ahead, back = (f, s + j), (f, s - j)
        k = j - 1
        fwd = [
            remote(b, bf.at[k], ssem.at[0, k], rsem.at[0, k], ahead),
            remote(t, tf.at[k], ssem.at[1, k], rsem.at[1, k], ahead),
        ]
        bwd = [
            remote(g, gb.at[k], ssem.at[2, k], rsem.at[2, k], back),
            remote(t, tb.at[k], ssem.at[3, k], rsem.at[3, k], back),
        ]
        return fwd, bwd

    every = [copies(j) for j in range(1, reach + 1)]
    for j in range(1, reach + 1):
        fwd, bwd = every[j - 1]

        @pl.when(s + j < ns)
        def _():
            for cp in fwd:
                cp.start()

        @pl.when(s - j >= 0)
        def _():
            for cp in bwd:
                cp.start()

    for j in range(1, reach + 1):
        fwd, bwd = every[j - 1]

        @pl.when(s + j < ns)
        def _():
            for cp in fwd:
                cp.wait_send()
            for cp in bwd:
                cp.wait_recv()

        @pl.when(s - j >= 0)
        def _():
            for cp in bwd:
                cp.wait_send()
            for cp in fwd:
                cp.wait_recv()


def carry_over_seq(reach, ns, cid, b, g, t):
    shape = jax.ShapeDtypeStruct
    return pl.pallas_call(
        functools.partial(carry_kernel, reach, ns),
        out_shape=(
            shape((reach,) + b.shape, b.dtype),
            shape((reach,) + g.shape, g.dtype),
            shape((reach,) + t.shape, t.dtype),
            shape((reach,) + t.shape, t.dtype),
        ),
        in_specs=[VMEM] * 3,
        out_specs=[VMEM] * 4,
        scratch_shapes=[
            pltpu.SemaphoreType.DMA((4, reach)),
            pltpu.SemaphoreType.DMA((4, reach)),
        ],
        compiler_params=comm_params(cid, 32 << 20),
        name="carry_over_seq",
    )(b, g, t)


BLOCK_TOKENS = 1024


def at(t):
    return pl.ds(pl.multiple_of(t * 8, 8), 8)


def cut(d):
    return slice(d * 128, (d + 1) * 128)


def pieces(v, count):
    out = []
    for _ in range(count):
        top = v.astype(BF16)
        out.append(top)
        v = v - top.astype(F32)
    return out


def spread_coefs(packed, cscr, first, count, nstate):
    wide = 2 * count * 128
    source = lax.broadcasted_iota(jnp.int32, (128, wide), 0)
    block = lax.broadcasted_iota(jnp.int32, (128, wide), 1) // 128
    want = jnp.where(block < count, block, nstate - count + block) + first
    pick = jnp.where(
        jnp.logical_and(source % (2 * nstate) == want, source < 6 * nstate), 1.0, 0.0
    ).astype(BF16)
    cscr[...] = jnp.dot(packed[...], pick, preferred_element_type=F32)


ENDS_UNROLL = 4
SCAN_UNROLL = 4


def ends_kernel(count, groups, nstate, step, mix, dy, beg, packed, rate, b, p, g, cscr):
    j = pl.program_id(1)
    steps = step.shape[1] // 8
    spread_coefs(packed, cscr, j * count, count, nstate)
    keys = [(d, i) for d in range(groups) for i in range(count)]
    rates = [jnp.broadcast_to(rate[0, i : i + 1, cut(d)], (8, 128)) for d, i in keys]

    def one(t, carry):
        bs, ps, gs = carry
        nb, np_, ng = [], [], []
        reset = beg[rows_at(LEAD - 8 + t * 8, 8), :]
        enter = [cscr[at(t), cut(i)] for i in range(count)]
        read = [cscr[at(t), cut(count + i)] for i in range(count)]
        for d in range(groups):
            st, dt = step[d, at(t), :], dy[d, at(t), :]
            ut = st * mix[d, at(t), :]
            st = st + reset
            for i in range(count):
                k = d * count + i
                a = jnp.exp2(st * rates[k])
                prod = ps[k] * a
                nb.append(bs[k] * a + enter[i] * ut)
                np_.append(prod)
                ng.append(gs[k] + prod * (read[i] * dt))
        return tuple(nb), tuple(np_), tuple(ng)

    size = count * groups
    zero = jnp.zeros((8, 128), F32)
    init = ((zero,) * size, (zero + 1.0,) * size, (zero,) * size)
    bs, ps, gs = lax.fori_loop(0, steps, one, init, unroll=ENDS_UNROLL)
    for k, (d, i) in enumerate(keys):
        b[0, i, :, cut(d)] = bs[k]
        p[0, i, :, cut(d)] = ps[k]
        g[0, i, :, cut(d)] = gs[k]


def scan_specs(tokens, ch, nstate, count):
    blocks = tokens // BLOCK_TOKENS
    groups = ch // 128
    steps = BLOCK_TOKENS // 8
    tok = pl.BlockSpec((groups, BLOCK_TOKENS, 128), lambda n, j: (0, n, 0))
    narrow = pl.BlockSpec((BLOCK_TOKENS, 128), lambda n, j: (n, 0))
    marks = pl.BlockSpec((BLOCK_TOKENS + 16, 128), lambda n, j: (n, 0))
    rates = pl.BlockSpec((1, count, ch), lambda n, j: (j, 0, 0))
    state = pl.BlockSpec((1, count, 8, ch), lambda n, j: (n, j, 0, 0))
    flat = pl.BlockSpec((BLOCK_TOKENS, ch), lambda n, j: (n, 0))
    grid = (blocks, nstate // count)
    kept = pl.BlockSpec((1, steps, count * groups, 8, 128), lambda n, j: (n * grid[1] + j, 0, 0, 0, 0))
    kept_shape = jax.ShapeDtypeStruct((math.prod(grid), steps, count * groups, 8, 128), F32)
    return grid, groups, tok, narrow, marks, rates, state, flat, kept, kept_shape


def scan_ends(step, mix, dy, beg, packed, rate, count):
    groups, tokens, _ = step.shape
    nstate, ch = rate.shape
    grid, groups, tok, narrow, marks, rates, state, flat, kept, kept_shape = scan_specs(tokens, ch, nstate, count)
    shape = jax.ShapeDtypeStruct((grid[0], nstate, 8, ch), F32)
    work = tokens * nstate * ch
    return pl.pallas_call(
        functools.partial(ends_kernel, count, groups, nstate),
        out_shape=(shape,) * 3,
        grid=grid,
        in_specs=[tok, tok, tok, marks, narrow, rates],
        out_specs=[state] * 3,
        scratch_shapes=[pltpu.VMEM((BLOCK_TOKENS, 2 * count * 128), F32)],
        compiler_params=pltpu.CompilerParams(vmem_limit_bytes=40 << 20),
        cost_estimate=pl.CostEstimate(flops=8 * work, bytes_accessed=12 * tokens * ch, transcendentals=work),
        name="scan_ends",
    )(step, mix, dy, beg, packed, rate.reshape(nstate // count, count, ch))


def rates_of(rate, keys):
    return [jnp.broadcast_to(rate[0, i : i + 1, cut(d)], (8, 128)) for d, i in keys]


def lane_sums(seen, coef, count, first):
    wide = count * 128
    block = lax.broadcasted_iota(jnp.int32, (wide, 128), 0) // 128
    column = lax.broadcasted_iota(jnp.int32, (wide, 128), 1)
    ones = jnp.where(column == block + first, 1.0, 0.0).astype(BF16)
    for part in pieces(seen[...], 2):
        coef[...] += jnp.dot(part, ones, preferred_element_type=F32)


def forward_kernel(
    count, groups, rank, nstate, step, mix, dy, beg, packed, rate, hin, ga, dgs, vecs, gated, dgate, states, coef, cscr, seen_scr, y
):
    j = pl.program_id(1)
    steps = step.shape[1] // 8
    keys = [(d, i) for d in range(groups) for i in range(count)]
    rates = rates_of(rate, keys)
    spread_coefs(packed, cscr, j * count, count, nstate)

    @pl.when(j == 0)
    def _():
        coef[...] = jnp.zeros_like(coef)
        for d in range(groups):
            y[d] = mix[d] * vecs[d, 6:7, :]

    def forward(t, state):
        reset = beg[rows_at(16 + t * 8, 8), :]
        enter = [cscr[at(t), cut(i)] for i in range(count)]
        read = [cscr[at(t), cut(count + i)] for i in range(count)]
        new = []
        seen = [None] * count
        for d in range(groups):
            st, dt = step[d, at(t), :], dy[d, at(t), :]
            ut = st * mix[d, at(t), :]
            st = st + reset
            out = None
            for i in range(count):
                k = d * count + i
                a = jnp.exp2(st * rates[k])
                states[0, t, k] = state[k]
                h = state[k] * a + enter[i] * ut
                new.append(h)
                out = read[i] * h if out is None else out + read[i] * h
                term = h * dt
                seen[i] = term if seen[i] is None else seen[i] + term
            y[d, at(t), :] += out
        for i in range(count):
            seen_scr[at(t), cut(i)] = seen[i]
        return tuple(new)

    lax.fori_loop(0, steps, forward, tuple(hin[0, i, :, cut(d)] for d, i in keys), unroll=SCAN_UNROLL)
    lane_sums(seen_scr, coef, count, rank + nstate + j * count)

    @pl.when(j == pl.num_programs(1) - 1)
    def _():
        def some(idx, carry):
            where, i = split_at(idx, steps // 32)
            q, g = split_at(where, 2)
            for d in range(groups):
                v = y[d, pl.ds(q * 2 + g + i * 256, 32, stride=8), :]
                at_ = rows_at(where * steps + i * 32, 32, 16)
                gated[at_, cut(d)] = (v * ga[at_, cut(d)]).astype(BF16)
                dgate[at_, cut(d)] = (v * dgs[at_, cut(d)]).astype(BF16)
            return carry

        lax.fori_loop(0, 8 * (steps // 32), some, 0)


def backward_kernel(
    count, groups, rank, nstate, step, mix, dy, beg, packed, rate, lin, states, reads, pulled, gs, coef, tot, cscr, seen_scr
):
    j = pl.program_id(1)
    steps = step.shape[1] // 8
    size = count * groups
    keys = [(d, i) for d in range(groups) for i in range(count)]
    rates = rates_of(rate, keys)
    spread_coefs(packed, cscr, j * count, count, nstate)

    @pl.when(j == 0)
    def _():
        pulled[...] = jnp.zeros_like(pulled)
        gs[...] = jnp.zeros_like(gs)
        coef[...] = reads[...]

    def backward(k0, carry):
        t = steps - 1 - k0
        passed, sums = carry
        reset = beg[rows_at(16 + t * 8, 8), :]
        enter = [cscr[at(t), cut(i)] for i in range(count)]
        read = [cscr[at(t), cut(count + i)] for i in range(count)]
        new, news = [], []
        seen = [None] * count
        for d in range(groups):
            st, dt = step[d, at(t), :], dy[d, at(t), :]
            ut = st * mix[d, at(t), :]
            st = st + reset
            pull, slope_sum = None, None
            for i in range(count):
                k = d * count + i
                adj = passed[k] + read[i] * dt
                pull = adj * enter[i] if pull is None else pull + adj * enter[i]
                back = adj * jnp.exp2(st * rates[k])
                slope = back * states[0, t, k]
                slope_sum = slope * rates[k] if slope_sum is None else slope_sum + slope * rates[k]
                new.append(back)
                news.append(sums[k] + slope * st)
                term = adj * ut
                seen[i] = term if seen[i] is None else seen[i] + term
            pulled[d, at(t), :] += pull
            gs[d, at(t), :] += slope_sum
        for i in range(count):
            seen_scr[at(t), cut(i)] = seen[i]
        return tuple(new), tuple(news)

    zero = jnp.zeros((8, 128), F32)
    init = (tuple(lin[0, i, :, cut(d)] for d, i in keys), (zero,) * size)
    passed, sums = lax.fori_loop(0, steps, backward, init, unroll=SCAN_UNROLL)
    for n, (d, i) in enumerate(keys):
        line = jnp.sum(sums[n] * rates[n], axis=0, keepdims=True) * LN2
        at_ = pl.ds(j * count + i, 1)

        @pl.when(pl.program_id(0) == 0)
        def _():
            tot[d, at_, :] = line

        @pl.when(pl.program_id(0) > 0)
        def _():
            tot[d, at_, :] += line

    lane_sums(seen_scr, coef, count, rank + j * count)


def scan_forward(step, mix, dy, beg, packed, rate, hin, ga, dgs, vecs, rank, count):
    groups, tokens, _ = step.shape
    nstate, ch = rate.shape
    grid, groups, tok, narrow, marks, rates, state, flat, kept, kept_shape = scan_specs(tokens, ch, nstate, count)
    shape = jax.ShapeDtypeStruct
    work = tokens * nstate * ch
    vec = pl.BlockSpec(vecs.shape, lambda n, j: (0, 0, 0))
    return pl.pallas_call(
        functools.partial(forward_kernel, count, groups, rank, nstate),
        out_shape=(shape((tokens, ch), BF16), shape((tokens, ch), BF16), kept_shape, shape((tokens, 128), F32)),
        grid=grid,
        in_specs=[tok, tok, tok, marks, narrow, rates, state, flat, flat, vec],
        out_specs=[flat, flat, kept, narrow],
        scratch_shapes=[
            pltpu.VMEM((BLOCK_TOKENS, 2 * count * 128), F32),
            pltpu.VMEM((BLOCK_TOKENS, count * 128), F32),
            pltpu.VMEM((groups, BLOCK_TOKENS, 128), F32),
        ],
        compiler_params=pltpu.CompilerParams(vmem_limit_bytes=60 << 20),
        cost_estimate=pl.CostEstimate(flops=8 * work, bytes_accessed=4 * work, transcendentals=work),
        name="scan_forward",
    )(step, mix, dy, beg, packed, rate.reshape(nstate // count, count, ch), hin, ga, dgs, vecs)


def scan_backward(step, mix, dy, beg, packed, rate, lin, states, reads, rank, count):
    groups, tokens, _ = step.shape
    nstate, ch = rate.shape
    grid, groups, tok, narrow, marks, rates, state, flat, kept, kept_shape = scan_specs(tokens, ch, nstate, count)
    shape = jax.ShapeDtypeStruct
    work = tokens * nstate * ch
    return pl.pallas_call(
        functools.partial(backward_kernel, count, groups, rank, nstate),
        out_shape=(
            shape(step.shape, F32),
            shape(step.shape, F32),
            shape((tokens, 128), F32),
            shape((groups, nstate, 128), F32),
        ),
        grid=grid,
        in_specs=[tok, tok, tok, marks, narrow, rates, state, kept, narrow],
        out_specs=[tok, tok, narrow, pl.BlockSpec((groups, nstate, 128), lambda n, j: (0, 0, 0))],
        scratch_shapes=[
            pltpu.VMEM((BLOCK_TOKENS, 2 * count * 128), F32),
            pltpu.VMEM((BLOCK_TOKENS, count * 128), F32),
        ],
        compiler_params=pltpu.CompilerParams(vmem_limit_bytes=60 << 20),
        cost_estimate=pl.CostEstimate(flops=12 * work, bytes_accessed=4 * work, transcendentals=work),
        name="scan_backward",
    )(step, mix, dy, beg, packed, rate.reshape(nstate // count, count, ch), lin, states, reads)


class Stream:
    def __init__(self, wire, place, src, got_y, mid, got_z, red, fin, out):
        self.wire, self.place = wire, place
        self.src, self.got_y, self.mid, self.got_z = src, got_y, mid, got_z
        self.red, self.fin, self.out = red, fin, out

    def start(self):
        p = self.place
        self.y = self.wire.send(self.src.at[:, 1 - p.b], self.got_y, p.beside)

    def across(self):
        p = self.place
        self.y.wait_recv()
        self.mid[...] = (self.src[:, p.b].astype(F32) + self.got_y[...].astype(F32)).astype(self.mid.dtype)
        self.z = [
            self.wire.send(self.mid.at[:, lax.bitwise_xor(p.a, i)], self.got_z.at[i - 1], p.zdev(i))
            for i in range(1, p.na)
        ]

    def swap(self):
        p = self.place
        for cp in self.z:
            cp.wait_recv()
        acc = self.mid[:, p.a].astype(F32)
        for i in range(1, p.na):
            acc = acc + self.got_z[i - 1].astype(F32)
        self.red[...] = acc.astype(self.red.dtype)
        self.w = [
            self.wire.send(self.red.at[lax.bitwise_xor(p.f, i)], self.fin.at[p.f], p.fdev(i)) for i in range(1, p.nf)
        ]
        self.fin[p.f] = self.red[p.f]

    def spread(self):
        p = self.place
        for cp in self.w:
            cp.wait_recv()
        self.out[p.b, p.a] = self.fin[...]
        self.g = [(self.wire.send(self.fin, self.out.at[p.b, p.a], p.zdev(i)), i) for i in range(1, p.na)]
        self.h = [self.wire.send(self.fin, self.out.at[p.b, p.a], p.beside)]

    def forward(self):
        p = self.place
        for cp, i in self.g:
            cp.wait_recv()
            block = self.out.at[p.b, lax.bitwise_xor(p.a, i)]
            self.h.append(self.wire.send(block, block, p.beside))

    def finish(self):
        for cp in self.h:
            cp.wait_recv()


class Place:
    def __init__(self, nf, ns):
        self.f, self.s = here()
        self.nf, self.ns, self.na = nf, ns, ns // 2
        self.a, self.b = lax.div(self.s, 2), lax.rem(self.s, 2)
        self.core = lax.rem(self.f, 2)
        self.peer = (lax.bitwise_xor(self.f, 1), self.s)
        self.beside = (self.f, lax.bitwise_xor(self.s, 1))

    def fdev(self, i):
        return (lax.bitwise_xor(self.f, i), self.s)

    def zdev(self, i):
        return (self.f, lax.bitwise_xor(self.a, i) * 2 + self.b)


def small_layout(groups, rank, nstate, ns):
    select, step, decay, vectors = 0, 128, 128 + rank, 128 + rank + nstate
    group = vectors + 8
    piece = -(-group * groups // (8 * ns)) * 8
    return select, step, decay, vectors, group, piece


def post_kernel(nf, ns, nq, rd, rank, nstate, sems, *refs):
    (pulled_i, slopes_i, mix_i, step_i, dy_i, slope_i, ext_i, beg_i, normed_i, wi_i, wg_i, dgate_i) = refs[:12]
    (ce, proj, vecs, w_sel, w_step, table, x, ct, decay) = refs[12:21]
    gates = refs[21 : 21 + nq]
    refs = refs[21 + nq :]
    rout, gain_out, small_out = refs[:3]
    outs = refs[3 : 3 + 2 * nq]
    refs = refs[3 + 2 * nq :]
    (pulled, slopes, mix, step, dy, slope, ext, beg, normed, wi, wg, dgate) = refs[:12]
    (mixb, dlin, dproj, dib, part, got, mid, far, sums) = refs[12:21]
    dconv, dp = mix, normed
    (near_d, mid_d, far_d, gain_l, gain_f, gain_m, gain_y, gain_n, gain_z, small, small_y, small_m, small_z) = refs[21:34]
    (edge_o, edge_i) = refs[34:36]
    refs = refs[36:]
    inners = refs[:nq]
    refs = refs[nq:]
    bufs = [refs[n * 2 * nq : (n + 1) * 2 * nq] for n in range(5)]
    ssem, rsem, lsem, esem = refs[10 * nq :]

    place = Place(nf, ns)
    f, s, a, b, core = place.f, place.s, place.a, place.b, place.core
    na = place.na
    chips = list(range(2, nf, 2))
    groups, tokens, _ = pulled.shape
    ch = groups * 128
    stretch = tokens // (nf * rd)
    half = stretch // 2
    span_t = half * 8
    blocks = tokens // span_t
    width = normed.shape[1]
    off_select, off_step, off_decay, off_vec, group_rows, piece = small_layout(groups, rank, nstate, ns)
    has_up, has_down = s + 1 < ns, s >= 1
    greet(
        [(None, place.fdev(i)) for i in range(1, nf)]
        + [(None, place.beside)]
        + [(None, place.zdev(i)) for i in range(1, na)]
        + [(has_up, (f, s + 1)), (has_down, (f, s - 1))]
    )
    wire = Wire(ssem, rsem)
    streams = []
    for n in range(2 * nq):
        src = gates[n] if n < nq else inners[n - nq]
        streams.append(Stream(wire, place, src, *[v[n] for v in bufs], outs[n]))
    for n in range(nq):
        streams[n].start()

    loads = []

    def load(src, dst):
        cp = pltpu.make_async_copy(src, dst, lsem.at[len(loads)])
        loads.append(cp)
        cp.start()
        return cp

    hs = tokens // 2
    other, keep = (1 - core) * hs, core * hs
    first = [(pulled_i, pulled), (slopes_i, slopes), (mix_i, mix), (step_i, step), (dy_i, dy)]
    by_half = []
    for start in (other, keep):
        rows_ = rows_at(start, hs)
        by_half.append([load(src.at[:, rows_], dst.at[:, rows_]) for src, dst in first])
    conv_in = [load(slope_i, slope), load(ext_i, ext), load(beg_i, beg.at[pl.ds(0, beg_i.shape[0])])]
    late = [load(normed_i, normed), load(wi_i, wi), load(wg_i, wg), load(dgate_i, dgate)]
    for d in range(groups):
        small[d * group_rows + off_decay : d * group_rows + off_vec, :] = decay[d]
        small[d * group_rows + off_vec : (d + 1) * group_rows, :] = jnp.zeros((8, 128), F32)
    rest = small.shape[0] - groups * group_rows
    if rest:
        small[groups * group_rows :, :] = jnp.zeros((rest, 128), F32)
    beg[beg_i.shape[0] :, :] = jnp.zeros((24, 128), F32)

    chunk = 64

    def fold(v):
        out = v[0:8]
        for q in range(1, v.shape[0] // 8):
            out = out + v[q * 8 : (q + 1) * 8]
        return out

    def add_row(d, k, v):
        at_ = slice(d * group_rows + off_vec + k, d * group_rows + off_vec + k + 1)
        small[at_, :] += jnp.sum(v, axis=0, keepdims=True)

    zero = jnp.zeros((8, 128), F32)

    def step_half(start, cps):
        for cp in cps:
            cp.wait()
        for d in range(groups):

            def one(c, carry, d=d):
                at_ = rows_at(start + c * chunk, chunk)
                pu, m, st, dv = pulled[d, at_, :], mix[d, at_, :], step[d, at_, :], dy[d, at_, :]
                tiny = st * (1.0 - st * (0.5 - st * (1.0 / 6.0 - st * (1.0 / 24.0))))
                sig = jnp.where(st < 0.03, tiny, 1.0 - jnp.exp(-st))
                dpre = (m * pu + slopes[d, at_, :] * LN2) * sig
                low_at = rows_at(start + c * chunk, chunk, 16)
                dlin[d, low_at, :] = dpre.astype(BF16)
                mixb[d, low_at, :] = m.astype(BF16)
                pulled[d, at_, :] = st * pu + dv * vecs[d, 6:7, :]
                return carry[0] + fold(dpre), carry[1] + fold(dv * m)

            bias, skip = lax.fori_loop(0, hs // chunk, one, (zero, zero))
            add_row(d, 5, bias)
            add_row(d, 6, skip)
        at_ = rows_at(start, hs)
        total = None
        for d in range(groups):
            term = times_transposed(dlin[d, rows_at(start, hs, 16), :], w_step[:, cut(d)])
            total = term if total is None else total + term
        part[at_, :] = ce[at_, :]
        part[at_, :rank] += total

    step_half(other, by_half[0])
    one = wire.send(part.at[rows_at(other, hs)], got, place.peer)
    step_half(keep, by_half[1])
    one.wait_recv()
    mid[...] = part[rows_at(keep, hs), :] + got[...]
    two = [wire.send(mid, far.at[n], place.fdev(i)) for n, i in enumerate(chips)]

    for d in range(groups):
        low = proj[...][:, :rank].astype(BF16)
        small[d * group_rows + off_step : d * group_rows + off_decay, :] = rows_inner(low, dlin[d])
    for n in range(nq):
        streams[n].across()

    for cp in two:
        cp.wait_recv()
    acc = mid[...]
    for n in range(len(chips)):
        acc = acc + far[n]
    sums[rows_at(keep, hs), :] = acc
    three = wire.send(sums.at[rows_at(keep, hs)], sums.at[rows_at(keep, hs)], place.peer)
    for cp in conv_in:
        cp.wait()

    def mask_at(base, k):
        out = jnp.where(beg[rows_at(base + 16, chunk), :] > 0.0, 0.0, 1.0)
        if k <= 1:
            out = jnp.where(beg[rows_at(base + 8, chunk), :] > 0.0, 0.0, out)
        if k == 0:
            out = jnp.where(beg[rows_at(base, chunk), :] > 0.0, 0.0, out)
        return out

    def conv_half(start):
        at_all = rows_at(start, hs)
        low_all = rows_at(start, hs, 16)
        dproj[low_all, :] = sums[at_all, :].astype(BF16)
        for d in range(groups):
            slopes[d, at_all, :] = times_transposed(dproj[low_all, :], w_sel[d * 128 : (d + 1) * 128, :])

            def one(c, carry, d=d):
                row = start + c * chunk
                n, inside = split_at(row, span_t)
                at_ = rows_at(row, chunk)
                v = (pulled[d, at_, :] + slopes[d, at_, :]) * slope[d, at_, :]
                base = n * (span_t + LEAD)
                dconv[d, rows_at(base + inside, chunk), :] = v
                bb = n * (span_t + 16) + inside
                out = [carry[0] + fold(v)]
                for k in range(4):
                    tap = ext[d, rows_at(base + inside + k * 8, chunk), :]
                    w = v * tap if k == 3 else v * tap * mask_at(bb, k)
                    out.append(carry[1 + k] + fold(w))
                return tuple(out)

            totals = lax.fori_loop(0, hs // chunk, one, (zero,) * 5)
            add_row(d, 4, totals[0])
            for k in range(4):
                add_row(d, k, totals[1 + k])

    for n in range(blocks):
        for d in range(groups):
            dconv[d, n * (span_t + LEAD) + span_t : (n + 1) * (span_t + LEAD), :] = jnp.zeros((LEAD, 128), F32)
    conv_half(keep)
    three.wait_recv()
    conv_half(other)

    sub = lax.broadcasted_iota(jnp.int32, (8, 128), 0)
    for n in range(blocks):
        base = n * (span_t + LEAD)
        bb = n * (span_t + 16)
        hit = [jnp.where(beg[bb + q * 8 : bb + q * 8 + 8, :] > 0.0, 0.0, 1.0) for q in range(5)]
        for d in range(groups):
            tail = [zero] * 3
            for q in range(3):
                v = dconv[d, base + q * 8 : base + q * 8 + 8, :]
                keepers = [hit[q + 2] * hit[q + 1] * hit[q], hit[q + 2] * hit[q + 1], hit[q + 2]]
                for k in range(3 - q):
                    tail[q + k] = tail[q + k] + vecs[d, k : k + 1, :] * (v * keepers[k])
            for q in range(3):
                edge_o[d, n * 24 + q * 8 : n * 24 + q * 8 + 8, :] = tail[q]
    edge = remote(edge_o, edge_i, esem.at[0], esem.at[1], (f, s - 1))

    @pl.when(has_down)
    def _():
        edge.start()

    for n in range(nq):
        streams[n].swap()

    per = span_t // chunk

    def inner_chunk(idx, carry):
        nd, c = split_at(idx, per)
        n, d = split_at(nd, groups)
        base = n * (span_t + LEAD) + c * chunk
        bb = n * (span_t + 16) + c * chunk
        acc = vecs[d, 3:4, :] * dconv[d, rows_at(base, chunk), :]
        for k in range(3):
            ahead = (3 - k) * 8
            acc = acc + vecs[d, k : k + 1, :] * (dconv[d, rows_at(base + ahead, chunk), :] * mask_at(bb + ahead, k))
        pulled[d, rows_at(n * span_t + c * chunk, chunk), :] = acc
        return carry

    lax.fori_loop(0, blocks * groups * per, inner_chunk, 0)

    for d in range(groups):
        small[d * group_rows + off_select : d * group_rows + off_step, :] = rows_inner(mixb[d], dproj[...])
    small_half = na * piece
    small_ys = wire.send(small.at[rows_at((1 - b) * small_half, small_half)], small_y, place.beside)
    for n in range(nq):
        streams[n].spread()

    @pl.when(has_up)
    def _():
        edge.wait_recv()

    for n in range(blocks):
        for d in range(groups):
            for q in range(3):
                at_ = slice(n * 24 + q * 8, n * 24 + q * 8 + 8)
                inward = pltpu.roll(edge_o[d, at_, :], 7, 0)
                outer = jnp.where(has_up, pltpu.roll(edge_i[d, at_, :], 1, 0), 0.0)
                row = n * span_t + (half - 3 + q) * 8
                pulled[d, row : row + 8, :] += jnp.where(sub % 2 == 0, inward, outer)

    def to_rows(idx, carry):
        r_g, i = split_at(idx, half // 32)
        r, g = split_at(r_g, 2)
        n, q = split_at(r, 4)
        at_ = rows_at(r_g * half + i * 32, 32, 16)
        for d in range(groups):
            v = pulled[d, pl.ds(n * span_t + q * 2 + g + i * 256, 32, stride=8), :]
            dib[at_, cut(d)] = v.astype(BF16)
        return carry

    lax.fori_loop(0, 2 * nf * rd * (half // 32), to_rows, 0)

    for cp in late:
        cp.wait()
    drow = width // nf
    prow = drow // ns
    lanes = max(drow, 128)
    cq = ch // nq
    for q in range(nq):

        def grad_block(k, carry, q=q):
            v = rows_inner(normed[:, pl.ds(pl.multiple_of(k * lanes, 128), lanes)], dib[:, q * cq : (q + 1) * cq])
            for m in range(lanes // drow):
                for p in range(ns):
                    r = m * drow + p * prow
                    piece_v = v[r : r + prow].astype(inners[q].dtype)
                    inners[q][k * (lanes // drow) + m, p // na, p % na] = piece_v
            return carry

        lax.fori_loop(0, width // lanes, grad_block, 0)
        streams[nq + q].start()

    span = rd * stretch

    def dn_rows(flip):
        def one(n, carry):
            who = lax.bitwise_xor(lax.bitwise_xor(f, flip), 2 * n)
            for q in range(rd):
                at_ = rows_at(who * span + q * stretch, stretch, 16)
                v = times_transposed(dib[at_, :], wi[...]) + times_transposed(dgate[at_, :], wg[...])
                dp[at_, :] = v.astype(BF16)
            return carry

        lax.fori_loop(0, nf // 2, one, 0)

    def dp_rows(who):
        return rows_at(who * span, span, 16)

    dn_rows(1)
    near = [
        wire.send(dp.at[dp_rows(lax.bitwise_xor(lax.bitwise_xor(f, 1), i))], near_d.at[n], place.peer)
        for n, i in enumerate([0] + chips)
    ]
    dn_rows(0)
    fars = []
    for n, i in reversed(list(enumerate([0] + chips))):
        near[n].wait_recv()
        if i:
            dest = lax.bitwise_xor(f, i)
            mid_d[n - 1] = (dp[dp_rows(dest), :].astype(F32) + near_d[n].astype(F32)).astype(BF16)
            fars.append(wire.send(mid_d.at[n - 1], far_d.at[n - 1], place.fdev(i)))
    for n in range(nq):
        streams[n].forward()
    small_ys.wait_recv()
    small_m[...] = small[rows_at(b * small_half, small_half), :] + small_y[...]

    def owned(who):
        return rows_at(who * piece, piece)

    small_zs = [
        wire.send(small_m.at[owned(lax.bitwise_xor(a, i))], small_z.at[i - 1], place.zdev(i)) for i in range(1, na)
    ]
    for n in range(nq, 2 * nq):
        streams[n].across()

    gain = jnp.concatenate([table[q : q + 1, :] for q in range(width // 128)], axis=1)
    for cp in fars:
        cp.wait_recv()

    def own_rows(i, total):
        at_ = rows_at(i * 16, 16, 16)
        v = x[at_, :].astype(F32)
        scale = lax.rsqrt(jnp.sum(v * v, axis=1, keepdims=True) * (1.0 / width) + EPS)
        hat = v * scale
        dn = dp[rows_at(f * span + i * 16, 16, 16), :].astype(F32) + near_d[0, at_, :].astype(F32)
        for n in range(len(chips)):
            dn = dn + far_d[n, at_, :].astype(F32)
        dh = dn * gain
        inner = jnp.sum(dh * hat, axis=1, keepdims=True) * (1.0 / width)
        rout[at_, :] = ct[at_, :].astype(F32) + scale * (dh - hat * inner)
        return total + jnp.sum(dn * hat, axis=0, keepdims=True)

    gain_l[...] = lax.fori_loop(0, x.shape[0] // 16, own_rows, jnp.zeros((1, width), F32))
    gain_a = [wire.send(gain_l, gain_f.at[i - 1], place.fdev(i)) for i in range(1, nf)]
    for cp in small_zs:
        cp.wait_recv()
    acc = small_m[owned(a), :]
    for i in range(1, na):
        acc = acc + small_z[i - 1]
    mine = rows_at(b * small_half + a * piece, piece)
    small_out[mine, :] = acc
    small_g = [(wire.send(small_out.at[mine], small_out.at[mine], place.zdev(i)), i) for i in range(1, na)]
    small_h = [wire.send(small_out.at[mine], small_out.at[mine], place.beside)]
    for n in range(nq, 2 * nq):
        streams[n].swap()
    for cp in gain_a:
        cp.wait_recv()
    acc = gain_l[...]
    for i in range(1, nf):
        acc = acc + gain_f[i - 1]
    gain_m[...] = acc
    gain_b = wire.send(gain_m, gain_y, place.beside)
    for n in range(nq, 2 * nq):
        streams[n].spread()
    for cp, i in small_g:
        cp.wait_recv()
        theirs = rows_at(b * small_half + lax.bitwise_xor(a, i) * piece, piece)
        small_h.append(wire.send(small_out.at[theirs], small_out.at[theirs], place.beside))
    gain_b.wait_recv()
    gain_n[...] = gain_m[...] + gain_y[...]
    gain_c = [wire.send(gain_n, gain_z.at[i - 1], place.zdev(i)) for i in range(1, na)]
    for n in range(nq, 2 * nq):
        streams[n].forward()
    for cp in gain_c:
        cp.wait_recv()
    acc = gain_n[...]
    for i in range(1, na):
        acc = acc + gain_z[i - 1]
    gain_out[...] = acc
    for cp in small_h:
        cp.wait_recv()
    for st in streams:
        st.finish()
    wire.drain()

    @pl.when(has_down)
    def _():
        edge.wait_send()

    assert len(wire.copies) == sems


def post(nf, ns, nq, cid, rd, rank, nstate, big, little, gates):
    shape = jax.ShapeDtypeStruct
    v = pltpu.VMEM
    pulled, ext, beg, normed, wi = big[0], big[6], big[7], big[8], big[9]
    x = little[6]
    groups, tokens, _ = pulled.shape
    ch = groups * 128
    width = normed.shape[1]
    na = ns // 2
    chips = nf // 2 - 1
    block = x.shape
    piece_shape = gates[0].shape[3:]
    piece = small_layout(groups, rank, nstate, ns)[-1]
    total = piece * ns
    hs = tokens // 2
    blocks = tokens // BLOCK_TOKENS
    stream = 1 + (na - 1) + (nf - 1) + (na - 1) + 1 + (na - 1)
    sems = 2 * nq * stream
    sems += 2 + chips
    sems += 1 + 2 * chips
    sems += 1 + (na - 1) + (na - 1) + 1 + (na - 1)
    sems += (nf - 1) + 1 + (na - 1)
    outs = [shape(block, F32), shape((1, width), F32), shape((total, 128), F32)]
    kind = gates[0].dtype
    outs += [shape((2, na, nf) + piece_shape, kind)] * (2 * nq)
    scratch = [v(m.shape, m.dtype) for m in big]
    scratch[2] = v(ext.shape, F32)
    scratch[7] = v((beg.shape[0] + 24, 128), F32)
    scratch += [
        v(pulled.shape, BF16),
        v(pulled.shape, BF16),
        v((tokens, 128), BF16),
        v((tokens, ch), BF16),
        v((tokens, 128), F32),
        v((hs, 128), F32),
        v((hs, 128), F32),
        v((chips, hs, 128), F32),
        v((tokens, 128), F32),
        v((chips + 1,) + block, BF16),
        v((chips,) + block, BF16),
        v((chips,) + block, BF16),
        v((1, width), F32),
        v((nf - 1, 1, width), F32),
        v((1, width), F32),
        v((1, width), F32),
        v((1, width), F32),
        v((na - 1, 1, width), F32),
        v((total, 128), F32),
        v((na * piece, 128), F32),
        v((na * piece, 128), F32),
        v((na - 1, piece, 128), F32),
        v((groups, blocks * 24, 128), F32),
        v((groups, blocks * 24, 128), F32),
    ]
    scratch += [v(gates[0].shape, kind)] * nq
    scratch += [v((nf, na) + piece_shape, kind)] * (2 * nq)
    scratch += [v((nf, na) + piece_shape, kind)] * (2 * nq)
    scratch += [v((na - 1, nf) + piece_shape, kind)] * (2 * nq)
    scratch += [v((nf,) + piece_shape, kind)] * (2 * nq)
    scratch += [v((nf,) + piece_shape, kind)] * (2 * nq)
    scratch += [
        pltpu.SemaphoreType.DMA((sems,)),
        pltpu.SemaphoreType.DMA((sems,)),
        pltpu.SemaphoreType.DMA((17,)),
        pltpu.SemaphoreType.DMA((2,)),
    ]
    return pl.pallas_call(
        functools.partial(post_kernel, nf, ns, nq, rd, rank, nstate, sems),
        out_shape=outs,
        in_specs=[ANY] * 12 + [VMEM] * (9 + nq),
        out_specs=[VMEM] * len(outs),
        scratch_shapes=scratch,
        compiler_params=comm_params(cid, 63 << 20),
        name="post",
    )(*big, *little, *gates)


def rows_inner(left, right):
    return lax.dot_general(left, right, (((0,), (0,)), ((), ())), preferred_element_type=F32)


def times_transposed(left, right):
    return lax.dot_general(left, right, (((1,), (1,)), ((), ())), preferred_element_type=F32)


def silu_slope(value):
    sig = jax.nn.sigmoid(value)
    return sig * (1.0 + value * (1.0 - sig))


def shards(
    nf,
    ns,
    residual,
    out_cotangent,
    doc_lengths,
    norm_gain,
    input_proj,
    conv_kernel,
    conv_bias,
    select_proj,
    step_proj,
    step_bias,
    log_decay,
    skip_gain,
    output_proj,
):
    rd, stretch, width = residual.shape
    rows = nf * rd
    docs = doc_lengths.shape[1]
    ch = conv_bias.shape[0]
    rank = step_proj.shape[0]
    nstate = log_decay.shape[0]
    taps = conv_kernel.shape[0]
    edge = taps - 1
    tokens = rows * stretch
    half = stretch // 2
    blocks = rows // 4
    f, s = here()
    reach = -(-(stretch * ns // 2 - 1) // stretch)
    count = 4

    groups = ch // 128
    grows = norm_gain.shape[0]
    spot = lax.broadcasted_iota(jnp.int32, (width,), 0) // grows == f
    small = jnp.where(spot, jnp.tile(norm_gain.astype(F32), nf), 0.0).reshape(width // 128, 128)
    marks = jnp.pad(doc_lengths.astype(F32), ((0, 8 - rd), (0, 128 - docs)))
    small = jnp.concatenate([small, marks], axis=0)
    vecs = jnp.concatenate(
        [conv_kernel, conv_bias[None], step_bias[None], skip_gain[None], jnp.zeros((1, ch), BF16)], axis=0
    ).astype(F32)
    vecs = jnp.moveaxis(vecs.reshape(8, groups, 128), 1, 0)
    w_sel = jnp.pad(select_proj, ((0, 0), (0, 128 - select_proj.shape[1])))
    normed, cot, ext, slope, mix, dy, ga, dgs, step, beg, proj, packed, w_inner, w_gate, gain = front(
        nf, ns, residual, out_cotangent, input_proj, small, vecs, w_sel, step_proj, output_proj, rank, nstate
    )
    rate = -jnp.exp(log_decay.astype(F32))
    rate2 = rate * LOG2E

    def stacked(v):
        return v.reshape((blocks, half, 8) + v.shape[1:])

    b, p, g = scan_ends(step, mix, dy, beg, packed, rate2, count)
    resets = beg.reshape(blocks, half + 2, 8, 128)[:, 2:].max(axis=1)[:, :, :1]
    run = jnp.moveaxis(jnp.sum(step.reshape(groups, blocks, half, 8, 128), axis=2), 0, 2).reshape(blocks, 8, ch) + resets

    def halves(v):
        v = v.reshape(v.shape[:-2] + (4, 2, ch))
        return v[..., 0, :], v[..., 1, :]

    b0, b1 = halves(b)
    p0, p1 = halves(p)
    g0, g1 = halves(g)
    r0, r1 = halves(run)
    flat = (blocks * nstate * 4, ch)
    bf, gb, tf, tb = carry_over_seq(
        reach,
        ns,
        2,
        (p1 * b0 + b1).astype(BF16).reshape(flat),
        (g0 + p0 * g1).astype(BF16).reshape(flat),
        (r0 + r1).reshape(blocks * 4, ch),
    )
    state_shape = (blocks, nstate, 4, ch)

    def gathered(ends, sums, valid):
        state = jnp.zeros(state_shape, F32)
        for j in range(reach - 1, -1, -1):
            decay = jnp.exp2(rate2[None, :, None, :] * sums[j].reshape(blocks, 1, 4, ch))
            new = decay * state + ends[j].reshape(state_shape).astype(F32)
            state = jnp.where(valid(j + 1), new, 0.0)
        return state

    h_first = gathered(bf, tf, lambda j: s - j >= 0)
    l_last = gathered(gb, tb, lambda j: s + j < ns)
    hin = jnp.stack([h_first, p0 * h_first + b0], axis=3).reshape(blocks, nstate, 8, ch)
    lin = jnp.stack([g1 + p1 * l_last, l_last], axis=3).reshape(blocks, nstate, 8, ch)

    gated, d_gate, states, coef_read = scan_forward(step, mix, dy, beg, packed, rate2, hin, ga, dgs, vecs, rank, count)
    nq = 2 if ch % 256 == 0 else 1
    cq = ch // nq
    piece_rows = width // nf // ns
    kind = BF16
    output_grad = rows_inner(gated, cot).astype(BF16)
    out_part = jnp.dot(gated, output_proj, preferred_element_type=F32).astype(BF16)
    gate_grads = [
        rows_inner(normed, d_gate[:, q * cq : (q + 1) * cq]).astype(kind).reshape(nf, 2, ns // 2, piece_rows, cq)
        for q in range(nq)
    ]
    output_grad, out_part, lin, *gate_grads = lax.optimization_barrier((output_grad, out_part, lin, *gate_grads))
    output_grad = lax.psum(output_grad, "seq")
    out_sum = lax.psum_scatter(out_part, "fsdp", scatter_dimension=0, tiled=True)

    pulled, slopes, coefs, decay = scan_backward(step, mix, dy, beg, packed, rate2, lin, states, coef_read, rank, count)
    big = (pulled, slopes, mix, step, dy, slope, ext, beg, normed, w_inner, w_gate, d_gate)
    little = (
        coefs,
        proj,
        vecs,
        w_sel,
        step_proj,
        gain,
        residual.reshape(rd * stretch, width),
        out_cotangent.reshape(rd * stretch, width),
        decay,
    )
    residual_grad, gain_sum, small_sum, *sums = post(nf, ns, nq, 3, rd, rank, nstate, big, little, gate_grads)
    layer_output = (residual.reshape(rd * stretch, width).astype(F32) + out_sum.astype(F32)).astype(BF16)

    def side(parts):
        parts = [v.reshape(ns, nf, piece_rows, cq) for v in parts]
        return jnp.moveaxis(jnp.concatenate(parts, axis=3), 1, 2).reshape(width // nf, nf * ch)

    input_grad = jnp.concatenate([side(sums[nq:]), side(sums[:nq])], axis=1).astype(F32)
    off_select, off_step, off_decay, off_vec, group_rows, _ = small_layout(groups, rank, nstate, ns)
    small_sum = small_sum[: groups * group_rows].reshape(groups, group_rows, 128)

    def section(start, count_):
        return jnp.moveaxis(small_sum[:, start : start + count_], 0, 1).reshape(count_, ch)

    vectors = section(off_vec, 8)
    return (
        layer_output.reshape(rd, stretch, width),
        residual_grad.reshape(rd, stretch, width),
        lax.dynamic_slice(gain_sum[0], (f * grows,), (grows,)),
        input_grad,
        vectors[:4],
        vectors[4],
        small_sum[:, :off_step, : select_proj.shape[1]].reshape(ch, select_proj.shape[1]),
        section(off_step, rank),
        vectors[5],
        section(off_decay, nstate),
        vectors[6],
        output_grad.astype(F32),
    )


def solution(mesh):
    nf, ns = mesh.shape["fsdp"], mesh.shape["seq"]
    in_specs = (
        P("fsdp", "seq", None),
        P("fsdp", "seq", None),
        P("fsdp", None),
        P("fsdp"),
        P("fsdp", None),
        P(None, "fsdp"),
        P("fsdp"),
        P("fsdp", None),
        P(None, "fsdp"),
        P("fsdp"),
        P(None, "fsdp"),
        P("fsdp"),
        P("fsdp", None),
    )
    out_specs = (
        P("fsdp", "seq", None),
        P("fsdp", "seq", None),
        P("fsdp"),
        P("fsdp", None),
        P(None, "fsdp"),
        P("fsdp"),
        P("fsdp", None),
        P(None, "fsdp"),
        P("fsdp"),
        P(None, "fsdp"),
        P("fsdp"),
        P("fsdp", None),
    )
    return jax.shard_map(
        functools.partial(shards, nf, ns), mesh=mesh, in_specs=in_specs, out_specs=out_specs, check_vma=False
    )
```

time: 521 us -> 307 us (0.59)
  waiting for transfers between devices: 94.9 us -> 0.54 us
  blocking collectives: 41.9 us -> 0 us
  local copies, waits for them, and re-layouts: 60.3 us -> 21.7 us
  other arithmetic: 48 us -> 15.1 us
  matrix products: 37.8 us -> 10.4 us
  Pallas kernels: 217 us -> 242 us
    psum x2 -> x1, waiting for transfers between devices: 94.9 us -> 0.01 us  [shards(): output_grad = lax.psum(output_grad, 'seq')]
    psum x1 -> x0, blocking collectives: 35.7 us -> none  [shards(): lax.psum(gain_grad, 'seq')]
    pallas_call x10 -> x5, Pallas kernels: 200 us -> 226 us  [the longest x1 92.1 us: post(): pl.pallas_call(functools.partial(post_kernel, nf, ns, nq, rd, rank, nstat...]
    dot_general x11 -> x1, matrix products: 23.3 us -> 2.62 us  [shards(): jnp.dot(gated, output_proj, preferred_element_type=F32).astype(BF16)]
    convert_element_type x14 -> x3, other arithmetic: 24.4 us -> 6.07 us  [the longest x1 2.91 us: shards(): output_grad.astype(F32)]
    convert_element_type x4 -> x0, local copies, waits for them, and re-layouts: 16.8 us -> none  [the longest x2 11.9 us: norm(): v = v.astype(F32)]
    unnamed x92 -> x38, local copies, waits for them, and re-layouts: 19.9 us -> 8.13 us
    mul x7 -> x0, other arithmetic: 8.95 us -> none  [the longest x3 4.71 us: shards(): stacked(masked[k])[:, ahead:] * kern[k][None, None, None, :]]
  transfers between devices with their start and end apart: 2 -> 2, of which waited for: 2 -> 0; matrix products, arithmetic and copies ran while one was open for 6% -> 4% of each run, Pallas kernels for 7% -> 41%
where the time goes in v2:
time: 307 us; the launch traced here: 306 us
  Pallas kernels  242 us (79%)
  local copies, waits for them, and re-layouts  21.7 us (7%)
  between operations  16 us (5%)
  other arithmetic  15.1 us (5%)
  matrix products  10.4 us (3%)
    pallas_call x1, Pallas kernels, post(): pl.pallas_call(functools.partial(post_kernel, nf, ns, nq, rd, rank, nstat...  92.1 us
    pallas_call x1, Pallas kernels, front(): pl.pallas_call(functools.partial(front_kernel, nf, ns, rd, rank, nstate,...  56.3 us
    pallas_call x1, Pallas kernels, scan_backward(): pl.pallas_call(functools.partial(backward_kernel, count, groups, rank, ns...  32.9 us
    pallas_call x1, Pallas kernels, scan_forward(): pl.pallas_call(functools.partial(forward_kernel, count, groups, rank, nst...  29.6 us
    pallas_call x1, Pallas kernels, carry_over_seq(): pl.pallas_call(functools.partial(carry_kernel, reach, ns), out_shape=(sha...  15.9 us
    pallas_call x1, Pallas kernels, scan_ends(): pl.pallas_call(functools.partial(ends_kernel, count, groups, nstate), out...  15.2 us
    unnamed x38, local copies, waits for them, and re-layouts  8.13 us
    dot_general x3, matrix products, rows_inner(): lax.dot_general(left, right, (((0,), (0,)), ((), ())), preferred_element_...  7.76 us
  transfers between devices with their start and end apart: 2, of which 0 were waited for; matrix products, arithmetic and copies ran while one was open for 4% of the time, Pallas kernels for 41%

profile of v2, /device:TPU:0, one launch (start us, length us, event | category | flops | bytes accessed | tf_op | source)
XLA Modules:
  0.0 305.9 jit_solution(11190529474931508090)
XLA Ops:
  8.1 0.7 convert_element_type.195
  8.7 0.7 bitcast_convert_fusion
  9.4 0.7 copy.61
  10.1 0.7 copy.62
  10.7 0.7 copy.63
  11.4 0.7 concatenate.29
  12.1 0.6 convert_bitcast_fusion.refs_4_.vecs.refs_14_
  12.8 1.0 copy.64
  13.8 0.7 pad.9.refs_5_.refs_15_
  14.5 0.7 negate_multiply_fusion
  15.3 0.6 select_maximum_fusion.refs_3_
  15.9 56.3 %front.1 = (bf16[1024,1024]{1,0:T(8,128)(2,1)}, bf16[1024,1024]{1,0:T(8,128)(2,1)}, f32[4,1048,128]{2,1,0:T(8,128)}, f32[4,1024,128]{2,1,0:T(8,128)}, f32[4,1024...) custom-call(bf16[1,256,1024]{2,1,0:T(8,128)(2,1)} %refs_0_.1, ...), custom_call_target="tpu_custom_call" | custom-call | tf_op jit(solution)/shard_map/front/pallas_call | solution.py:501
  72.2 1.9 bitcast_reduce_fusion
  74.1 0.3 copy-done
  74.4 1.6 copy-done.1
  76.0 1.6 copy-done.2
  77.6 1.0 copy-done.3
  78.6 0.9 copy-done.5
  79.6 15.2 %scan_ends.1 = (f32[1,16,8,512]{3,2,1,0:T(8,128)S(1)}, f32[1,16,8,512]{3,2,1,0:T(8,128)S(1)}, f32[1,16,8,512]{3,2,1,0:T(8,128)S(1)}) custom-call(f32[4,1024,128]{2,1,0:T(8,128)S(1)} %copy-done, f32[4,1024,128]{2,1,0:T(8,128)S(1)} %copy-done.1, f32[4,1024,128]{2,1,0:T(8,128)S(1)} %copy-done.2, f32[1040,128]{1,0:T(8,128)S(1)} %copy-done.3, ...), custom_call_target="tpu_custom_call" | custom-call | flops 67108864 | bytes 6291456 | tf_op jit(solution)/shard_map/scan_ends/pallas_call | solution.py:679
  94.8 0.1 reshape.570
  95.0 0.2 fusion.12
  95.2 0.1 reshape.571
  95.3 0.2 fusion.13
  95.5 0.1 reshape.572
  95.7 0.2 fusion.11
  95.9 0.2 fusion.3
  96.2 0.1 slice_reduce_fusion
  96.3 0.1 slice_reduce_fusion.1
  96.4 0.1 add.207
  96.5 0.1 copy.72
  96.6 0.1 copy_add_fusion.2
  96.7 15.9 %carry_over_seq.1 = (bf16[4,64,512]{2,1,0:T(8,128)(2,1)S(1)}, bf16[4,64,512]{2,1,0:T(8,128)(2,1)S(1)}, f32[4,4,512]{2,1,0:T(4,128)S(1)}, f32[4,4,512]{2,1,0:T(4,128)S(1)}) custom-call(bf16[64,512]{1,0:T(8,128)(2,1)S(1)} %convert_element_type.198.b, bf16[64,512]{1,0:T(8,128)(2,1)S(1)} %convert_element_type.200.g, f32[4,512]{1,0:T(4,128)S(1)} %fusion.5.t), custom_call_target="tpu_custom_call" | custom-call | tf_op jit(solution)/shard_map/carry_over_seq/pallas_call | solution.py:567
  112.9 0.3 multiply_add_fusion.1
  113.3 0.2 copy.74
  113.5 0.9 reshape.576.hin
  114.4 29.6 %scan_forward.1 = (bf16[1024,512]{1,0:T(8,128)(2,1)}, bf16[1024,512]{1,0:T(8,128)(2,1)}, f32[4,128,16,8,128]{4,3,2,1,0:T(8,128)}, f32[1024,128]{1,0:T(8,128)}) custom-call(f32[4,1024,128]{2,1,0:T(8,128)} %get-tuple-element.54.step.refs_3_, f32[4,1024,128]{2,1,0:T(8,128)} %get-tuple-element.55.mix.refs_2_, f32[4,1024,128]{2,1,0:T(8,128)} %get-tuple-element.56.dy.refs_4_, ...), custom_call_target="tpu_custom_call" | custom-call | flops 67108864 | bytes 33554432 | tf_op jit(solution)/shard_map/scan_forward/pallas_call | solution.py:834
  144.0 2.7 convolution_convert_fusion.3
  146.7 1.6 convolution_convert_fusion.2
  148.3 2.6 convolution_convert_fusion
  150.9 3.5 %convolution_convert_fusion.1 = bf16[512,1024]{1,0:T(8,128)(2,1)} fusion(bf16[1024,512]{1,0:T(8,128)(2,1)} %get-tuple-element.66, bf16[1024,1024]{1,0:T(8,128)(2,1)S(1)} %copy-done.9), kind=kOutput, calls=%fused_computation.3 | convolution fusion | flops 1074266112 | bytes 4194304 | tf_op jit(solution)/shard_map/dot_general | solution.py:1410
  154.7 0.3 multiply_add_fusion
  155.0 0.1 pad_maximum_fusion.1
  155.0 0.2 copy.75
  155.2 0.9 reshape.577.lin
  156.2 0.5 reduce-scatter.2.cloned.1.call-update
  156.7 32.9 %scan_backward.1 = (f32[4,1024,128]{2,1,0:T(8,128)}, f32[4,1024,128]{2,1,0:T(8,128)}, f32[1024,128]{1,0:T(8,128)}, f32[4,16,128]{2,1,0:T(8,128)}) custom-call(f32[4,1024,128]{2,1,0:T(8,128)} %get-tuple-element.54.step.refs_3_, f32[4,1024,128]{2,1,0:T(8,128)} %get-tuple-element.55.mix.refs_2_, f32[4,1024,128]{2,1,0:T(8,128)} %get-tuple-element.56.dy.refs_4_, ...), custom_call_target="tpu_custom_call" | custom-call | flops 100663296 | bytes 33554432 | tf_op jit(solution)/shard_map/scan_backward/pallas_call | solution.py:857
  189.7 92.1 %post.1 = (f32[256,1024]{1,0:T(8,128)}, f32[1,1024]{1,0:T(1,128)}, f32[896,128]{1,0:T(8,128)}, bf16[2,4,4,32,256]{4,3,2,1,0:T(8,128)(2,1)}, bf16[2,4,4,32,256]{4...) custom-call(f32[4,1024,128]{2,1,0:T(8,128)} %get-tuple-element.76.refs_0_, ...), custom_call_target="tpu_custom_call" | custom-call | tf_op jit(solution)/shard_map/post/pallas_call | solution.py:1398
  281.8 1.3 maximum_bitcast_fusion.1
  283.1 0.8 copy.77
  283.9 0.3 copy.92
  284.2 0.1 copy-done.15
  284.3 0.1 maximum_bitcast_fusion
  284.4 0.8 copy.76
  285.2 0.3 copy.91
  285.6 0.8 copy.82
  286.4 1.2 constant_dynamic-slice_fusion
  287.6 0.6 fusion.14
  288.2 0.6 slice_bitcast_fusion.3
  288.8 0.6 copy_bitcast_fusion.1
  289.4 0.7 copy_bitcast_fusion
  290.1 2.5 maximum_convert_fusion
  292.6 2.9 convert_element_type.224
  295.5 2.0 fusion
  297.5 1.0 copy.112
  (57 shorter events, 0.8 us)
Async XLA Ops:
  8.0 284.6 %all-reduce.4.cloned.1.call-start = ((), (), s32[]{:S(2)}) async-start(), calls=%async_computation.2 | async-start | bytes 2097152 | tf_op jit(solution)/shard_map/psum | solution.py:1522
  15.2 58.8 %copy-start.6 = (f32[4,4,512]{2,1,0:T(4,128)}, f32[4,4,512]{2,1,0:T(4,128)S(1)}, u32[]{:S(2)}) copy-start(f32[4,4,512]{2,1,0:T(4,128)S(1)} %reshape.569.rate) | copy-start | bytes 98308
  72.2 2.2 copy-start
  74.4 1.6 copy-start.1
  76.0 1.6 copy-start.2
  77.6 1.0 copy-start.3
  78.6 0.9 copy-start.5
  94.8 1.4 copy-start.4
  114.4 29.6 %copy-start.8 = (bf16[1024,1024]{1,0:T(8,128)(2,1)S(1)}, bf16[1024,1024]{1,0:T(8,128)(2,1)}, u32[]{:S(2)}) copy-start(bf16[1024,1024]{1,0:T(8,128)(2,1)} %get-tuple-element.70.refs_8_) | copy-start | bytes 6291460
  144.0 2.7 copy-start.10
  146.7 1.6 copy-start.12
  146.7 1.6 copy-start.13
  148.3 2.6 copy-start.9
  156.1 139.3 %reduce-scatter.2.cloned.1.call-start = ((), (), s32[]{:S(2)}) async-start(), calls=%async_computation.1 | async-start | bytes 2621440 | tf_op jit(solution)/shard_map/reduce_scatter | solution.py:1523
  283.1 1.1 copy-start.14
  283.1 1.2 copy-start.15
  284.4 1.1 copy-start.16
  292.6 2.9 copy-start.7
  292.6 5.0 %copy-start.11 = (f32[256,1024]{1,0:T(8,128)S(1)}, f32[256,1024]{1,0:T(8,128)}, u32[]{:S(2)}) copy-start(f32[256,1024]{1,0:T(8,128)} %get-tuple-element.88) | copy-start | bytes 3145732
Sparse Core Ops, SparseCore 0:
  156.3 87.9 all-reduce.3
Sparse Core Ops, SparseCore 1:
  159.1 30.7 reduce-scatter.1

commit v3 on v2

--- a/solution.py
+++ b/solution.py
@@ -509,80 +509,6 @@
     )(x, ct, w, sm, vecs, w_sel, w_step, w_out)
 
 
-def carry_kernel(reach, ns, b, g, t, bf, gb, tf, tb, ssem, rsem):
-    f, s = here()
-    peers = []
-    for j in range(1, reach + 1):
-        peers.append((s + j < ns, (f, s + j)))
-        peers.append((s - j >= 0, (f, s - j)))
-    greet(peers)
-
-    def copies(j):
-        ahead, back = (f, s + j), (f, s - j)
-        k = j - 1
-        fwd = [
-            remote(b, bf.at[k], ssem.at[0, k], rsem.at[0, k], ahead),
-            remote(t, tf.at[k], ssem.at[1, k], rsem.at[1, k], ahead),
-        ]
-        bwd = [
-            remote(g, gb.at[k], ssem.at[2, k], rsem.at[2, k], back),
-            remote(t, tb.at[k], ssem.at[3, k], rsem.at[3, k], back),
-        ]
-        return fwd, bwd
-
-    every = [copies(j) for j in range(1, reach + 1)]
-    for j in range(1, reach + 1):
-        fwd, bwd = every[j - 1]
-
-        @pl.when(s + j < ns)
-        def _():
-            for cp in fwd:
-                cp.start()
-
-        @pl.when(s - j >= 0)
-        def _():
-            for cp in bwd:
-                cp.start()
-
-    for j in range(1, reach + 1):
-        fwd, bwd = every[j - 1]
-
-        @pl.when(s + j < ns)
-        def _():
-            for cp in fwd:
-                cp.wait_send()
-            for cp in bwd:
-                cp.wait_recv()
-
-        @pl.when(s - j >= 0)
-        def _():
-            for cp in bwd:
-                cp.wait_send()
-            for cp in fwd:
-                cp.wait_recv()
-
-
-def carry_over_seq(reach, ns, cid, b, g, t):
-    shape = jax.ShapeDtypeStruct
-    return pl.pallas_call(
-        functools.partial(carry_kernel, reach, ns),
-        out_shape=(
-            shape((reach,) + b.shape, b.dtype),
-            shape((reach,) + g.shape, g.dtype),
-            shape((reach,) + t.shape, t.dtype),
-            shape((reach,) + t.shape, t.dtype),
-        ),
-        in_specs=[VMEM] * 3,
-        out_specs=[VMEM] * 4,
-        scratch_shapes=[
-            pltpu.SemaphoreType.DMA((4, reach)),
-            pltpu.SemaphoreType.DMA((4, reach)),
-        ],
-        compiler_params=comm_params(cid, 32 << 20),
-        name="carry_over_seq",
-    )(b, g, t)
-
-
 BLOCK_TOKENS = 1024
 
 
@@ -611,47 +537,11 @@
     pick = jnp.where(
         jnp.logical_and(source % (2 * nstate) == want, source < 6 * nstate), 1.0, 0.0
     ).astype(BF16)
-    cscr[...] = jnp.dot(packed[...], pick, preferred_element_type=F32)
+    cscr[...] = jnp.dot(packed, pick, preferred_element_type=F32)
 
 
 ENDS_UNROLL = 4
 SCAN_UNROLL = 4
-
-
-def ends_kernel(count, groups, nstate, step, mix, dy, beg, packed, rate, b, p, g, cscr):
-    j = pl.program_id(1)
-    steps = step.shape[1] // 8
-    spread_coefs(packed, cscr, j * count, count, nstate)
-    keys = [(d, i) for d in range(groups) for i in range(count)]
-    rates = [jnp.broadcast_to(rate[0, i : i + 1, cut(d)], (8, 128)) for d, i in keys]
-
-    def one(t, carry):
-        bs, ps, gs = carry
-        nb, np_, ng = [], [], []
-        reset = beg[rows_at(LEAD - 8 + t * 8, 8), :]
-        enter = [cscr[at(t), cut(i)] for i in range(count)]
-        read = [cscr[at(t), cut(count + i)] for i in range(count)]
-        for d in range(groups):
-            st, dt = step[d, at(t), :], dy[d, at(t), :]
-            ut = st * mix[d, at(t), :]
-            st = st + reset
-            for i in range(count):
-                k = d * count + i
-                a = jnp.exp2(st * rates[k])
-                prod = ps[k] * a
-                nb.append(bs[k] * a + enter[i] * ut)
-                np_.append(prod)
-                ng.append(gs[k] + prod * (read[i] * dt))
-        return tuple(nb), tuple(np_), tuple(ng)
-
-    size = count * groups
-    zero = jnp.zeros((8, 128), F32)
-    init = ((zero,) * size, (zero + 1.0,) * size, (zero,) * size)
-    bs, ps, gs = lax.fori_loop(0, steps, one, init, unroll=ENDS_UNROLL)
-    for k, (d, i) in enumerate(keys):
-        b[0, i, :, cut(d)] = bs[k]
-        p[0, i, :, cut(d)] = ps[k]
-        g[0, i, :, cut(d)] = gs[k]
 
 
 def scan_specs(tokens, ch, nstate, count):
@@ -670,25 +560,6 @@
     return grid, groups, tok, narrow, marks, rates, state, flat, kept, kept_shape
 
 
-def scan_ends(step, mix, dy, beg, packed, rate, count):
-    groups, tokens, _ = step.shape
-    nstate, ch = rate.shape
-    grid, groups, tok, narrow, marks, rates, state, flat, kept, kept_shape = scan_specs(tokens, ch, nstate, count)
-    shape = jax.ShapeDtypeStruct((grid[0], nstate, 8, ch), F32)
-    work = tokens * nstate * ch
-    return pl.pallas_call(
-        functools.partial(ends_kernel, count, groups, nstate),
-        out_shape=(shape,) * 3,
-        grid=grid,
-        in_specs=[tok, tok, tok, marks, narrow, rates],
-        out_specs=[state] * 3,
-        scratch_shapes=[pltpu.VMEM((BLOCK_TOKENS, 2 * count * 128), F32)],
-        compiler_params=pltpu.CompilerParams(vmem_limit_bytes=40 << 20),
-        cost_estimate=pl.CostEstimate(flops=8 * work, bytes_accessed=12 * tokens * ch, transcendentals=work),
-        name="scan_ends",
-    )(step, mix, dy, beg, packed, rate.reshape(nstate // count, count, ch))
-
-
 def rates_of(rate, keys):
     return [jnp.broadcast_to(rate[0, i : i + 1, cut(d)], (8, 128)) for d, i in keys]
 
@@ -702,62 +573,277 @@
         coef[...] += jnp.dot(part, ones, preferred_element_type=F32)
 
 
-def forward_kernel(
-    count, groups, rank, nstate, step, mix, dy, beg, packed, rate, hin, ga, dgs, vecs, gated, dgate, states, coef, cscr, seen_scr, y
-):
-    j = pl.program_id(1)
-    steps = step.shape[1] // 8
+def mid_kernel(nf, ns, reach, count, rank, nstate, *refs):
+    (step, mix, dy, beg, packed, rate, vecs, ga_i, dgs_i) = refs[:9]
+    (gated, dgate, states_o, coef, lin_o) = refs[9:14]
+    (cscr, seen, y, keep, bsc, psc, gsc, run, b_out, g_out, b_in, g_in, t_out, t_up, t_down, ga, dgs) = refs[14:31]
+    ssem, rsem, tsem, tsem2, ksem, lsem = refs[31:]
+    f, s = here()
+    groups = step.shape[0]
+    blocks = step.shape[1] // BLOCK_TOKENS
+    steps = BLOCK_TOKENS // 8
+    parts = nstate // count
     keys = [(d, i) for d in range(groups) for i in range(count)]
-    rates = rates_of(rate, keys)
-    spread_coefs(packed, cscr, j * count, count, nstate)
-
-    @pl.when(j == 0)
-    def _():
-        coef[...] = jnp.zeros_like(coef)
+    size = len(keys)
+    sub = lax.broadcasted_iota(jnp.int32, (8, 128), 0)
+    odd = sub % 2 == 1
+    zero = jnp.zeros((8, 128), F32)
+    slots = parts if blocks == 1 else 1
+
+    peers = []
+    for q in range(1, reach + 1):
+        peers.append((s + q < ns, (f, s + q)))
+        peers.append((s - q >= 0, (f, s - q)))
+    greet(peers)
+    loads = [pltpu.make_async_copy(ga_i, ga, lsem.at[0]), pltpu.make_async_copy(dgs_i, dgs, lsem.at[1])]
+    for cp in loads:
+        cp.start()
+
+    def each_way(q, up, down):
+        @pl.when(s + q < ns)
+        def _():
+            up()
+
+        @pl.when(s - q >= 0)
+        def _():
+            down()
+
+    def starts(cps):
+        for cp in cps:
+            cp.start()
+
+    def rates(j):
+        return [jnp.broadcast_to(rate[d, j * count + i : j * count + i + 1, :], (8, 128)) for d, i in keys]
+
+    def tokens_of(n):
+        return slice(n * BLOCK_TOKENS, (n + 1) * BLOCK_TOKENS)
+
+    def row(n, t):
+        return rows_at(n * BLOCK_TOKENS + t * 8, 8)
+
+    def marks(n, t):
+        return beg[rows_at(n * (BLOCK_TOKENS + 16) + 16 + t * 8, 8), :]
+
+    def pair_up(values, side):
+        out = []
+        for k in range(0, len(values), 2):
+            one, two = values[k], values[k + 1]
+            if side:
+                out.append(jnp.where(odd, one, pltpu.roll(two, 7, 0)))
+            else:
+                out.append(jnp.where(odd, pltpu.roll(two, 1, 0), one))
+        return out
+
+    def both_rows(v, side):
+        return jnp.where(odd, v, pltpu.roll(v, 7, 0)) if side else jnp.where(odd, pltpu.roll(v, 1, 0), v)
+
+    carries = []
+    for n in range(blocks):
+        for j in range(parts):
+            slot = j if blocks == 1 else 0
+            spread_coefs(packed[tokens_of(n), :], cscr.at[slot], j * count, count, nstate)
+            rt = rates(j)
+
+            def one(t, carry, n=n, j=j, slot=slot, rt=rt):
+                bs, ps, gs, rs = carry
+                nb, np_, ng, nr = [], [], [], []
+                reset = marks(n, t)
+                enter = [cscr[slot, at(t), cut(i)] for i in range(count)]
+                read = [cscr[slot, at(t), cut(count + i)] for i in range(count)]
+                for d in range(groups):
+                    st, dt = step[d, row(n, t), :], dy[d, row(n, t), :]
+                    ut = st * mix[d, row(n, t), :]
+                    st = st + reset
+                    if j == 0:
+                        nr.append(rs[d] + st)
+                    for i in range(count):
+                        k = d * count + i
+                        a = jnp.exp2(st * rt[k])
+                        prod = ps[k] * a
+                        nb.append(bs[k] * a + enter[i] * ut)
+                        np_.append(prod)
+                        ng.append(gs[k] + prod * (read[i] * dt))
+                return tuple(nb), tuple(np_), tuple(ng), tuple(nr)
+
+            init = ((zero,) * size, (zero + 1.0,) * size, (zero,) * size, (zero,) * (groups if j == 0 else 0))
+            bs, ps, gs, rs = lax.fori_loop(0, steps, one, init, unroll=ENDS_UNROLL)
+            if j == 0:
+                for d in range(groups):
+                    both = rs[d] + jnp.where(odd, pltpu.roll(rs[d], 1, 0), pltpu.roll(rs[d], 7, 0))
+                    t_out[n, d] = both
+                cps = []
+                for q in range(1, reach + 1):
+                    cps.append(remote(t_out.at[n], t_up.at[n, q - 1], tsem.at[0, n, q - 1], tsem.at[1, n, q - 1], (f, s + q)))
+                    cps.append(remote(t_out.at[n], t_down.at[n, q - 1], tsem2.at[0, n, q - 1], tsem2.at[1, n, q - 1], (f, s - q)))
+                    each_way(q, cps[-2].start, cps[-1].start)
+                carries.append(cps)
+            bd, gd = [], []
+            for k in range(size):
+                bsc[n, j, k], psc[n, j, k], gsc[n, j, k] = bs[k], ps[k], gs[k]
+                bd.append(ps[k] * pltpu.roll(bs[k], 1, 0) + bs[k])
+                gd.append(gs[k] + ps[k] * pltpu.roll(gs[k], 7, 0))
+            bp, gp = pair_up(bd, True), pair_up(gd, False)
+            for k in range(0, size // 2, 2):
+                b_out[n, j, k * 8 : k * 8 + 16, :] = jnp.concatenate([bp[k], bp[k + 1]], axis=0).astype(BF16)
+                g_out[n, j, k * 8 : k * 8 + 16, :] = jnp.concatenate([gp[k], gp[k + 1]], axis=0).astype(BF16)
+            cps = []
+            for q in range(1, reach + 1):
+                cps.append(
+                    remote(b_out.at[n, j], b_in.at[n, j, q - 1], ssem.at[0, n, j, q - 1], rsem.at[0, n, j, q - 1], (f, s + q))
+                )
+                cps.append(
+                    remote(g_out.at[n, j], g_in.at[n, j, q - 1], ssem.at[1, n, j, q - 1], rsem.at[1, n, j, q - 1], (f, s - q))
+                )
+                each_way(q, cps[-2].start, cps[-1].start)
+            carries.append(cps)
+
+    for cp in loads:
+        cp.wait()
+    coef[...] = jnp.zeros_like(coef)
+    outs = []
+    order = 0
+    for n in range(blocks):
         for d in range(groups):
-            y[d] = mix[d] * vecs[d, 6:7, :]
-
-    def forward(t, state):
-        reset = beg[rows_at(16 + t * 8, 8), :]
-        enter = [cscr[at(t), cut(i)] for i in range(count)]
-        read = [cscr[at(t), cut(count + i)] for i in range(count)]
-        new = []
-        seen = [None] * count
-        for d in range(groups):
-            st, dt = step[d, at(t), :], dy[d, at(t), :]
-            ut = st * mix[d, at(t), :]
-            st = st + reset
-            out = None
-            for i in range(count):
-                k = d * count + i
-                a = jnp.exp2(st * rates[k])
-                states[0, t, k] = state[k]
-                h = state[k] * a + enter[i] * ut
-                new.append(h)
-                out = read[i] * h if out is None else out + read[i] * h
-                term = h * dt
-                seen[i] = term if seen[i] is None else seen[i] + term
-            y[d, at(t), :] += out
-        for i in range(count):
-            seen_scr[at(t), cut(i)] = seen[i]
-        return tuple(new)
-
-    lax.fori_loop(0, steps, forward, tuple(hin[0, i, :, cut(d)] for d, i in keys), unroll=SCAN_UNROLL)
-    lane_sums(seen_scr, coef, count, rank + nstate + j * count)
-
-    @pl.when(j == pl.num_programs(1) - 1)
-    def _():
-        def some(idx, carry):
+            y[d] = mix[d, tokens_of(n), :] * vecs[d, 6:7, :]
+        for j in range(parts):
+            slot = j if blocks == 1 else 0
+            if blocks > 1:
+                spread_coefs(packed[tokens_of(n), :], cscr.at[slot], j * count, count, nstate)
+            mine = [carries[n * (parts + 1) + 1 + j]] + ([carries[n * (parts + 1)]] if j == 0 else [])
+            for cps in mine:
+                for q in range(1, reach + 1):
+                    up, down = cps[2 * q - 2], cps[2 * q - 1]
+
+                    def ahead(up=up, down=down):
+                        up.wait_send()
+                        down.wait_recv()
+
+                    def behind(up=up, down=down):
+                        down.wait_send()
+                        up.wait_recv()
+
+                    each_way(q, ahead, behind)
+            rt = rates(j)
+            hin = [None] * size
+            for k in range(0, size, 2):
+                h, l = [zero, zero], [zero, zero]
+                for q in range(reach - 1, -1, -1):
+                    at_ = slice(k * 4, k * 4 + 8)
+                    bv, gv = b_in[n, j, q, at_, :].astype(F32), g_in[n, j, q, at_, :].astype(F32)
+                    for m in range(2):
+                        d = keys[k + m][0]
+                        nh = jnp.exp2(rt[k + m] * t_up[n, q, d]) * h[m] + both_rows(bv, m == 0)
+                        nl = jnp.exp2(rt[k + m] * t_down[n, q, d]) * l[m] + both_rows(gv, m == 1)
+                        h[m] = jnp.where(s - (q + 1) >= 0, nh, 0.0)
+                        l[m] = jnp.where(s + (q + 1) < ns, nl, 0.0)
+                for m in range(2):
+                    d, i = keys[k + m]
+                    pv, bv, gv = psc[n, j, k + m], bsc[n, j, k + m], gsc[n, j, k + m]
+                    hin[k + m] = jnp.where(odd, pltpu.roll(pv, 1, 0) * h[m] + pltpu.roll(bv, 1, 0), h[m])
+                    lin = jnp.where(odd, l[m], pltpu.roll(gv, 7, 0) + pltpu.roll(pv, 7, 0) * l[m])
+                    lin_o[n, j * count + i, :, cut(d)] = lin
+            kslot = order % 2
+            if order >= 2:
+                outs[order - 2].wait()
+
+            def forward(t, state, n=n, slot=slot, rt=rt, kslot=kslot):
+                reset = marks(n, t)
+                enter = [cscr[slot, at(t), cut(i)] for i in range(count)]
+                read = [cscr[slot, at(t), cut(count + i)] for i in range(count)]
+                new = []
+                total = [None] * count
+                for d in range(groups):
+                    st, dt = step[d, row(n, t), :], dy[d, row(n, t), :]
+                    ut = st * mix[d, row(n, t), :]
+                    st = st + reset
+                    out = None
+                    for i in range(count):
+                        k = d * count + i
+                        a = jnp.exp2(st * rt[k])
+                        keep[kslot, t, k] = state[k]
+                        h = state[k] * a + enter[i] * ut
+                        new.append(h)
+                        out = read[i] * h if out is None else out + read[i] * h
+                        term = h * dt
+                        total[i] = term if total[i] is None else total[i] + term
+                    y[d, at(t), :] += out
+                for i in range(count):
+                    seen[at(t), cut(i)] = total[i]
+                return tuple(new)
+
+            lax.fori_loop(0, steps, forward, tuple(hin), unroll=SCAN_UNROLL)
+            cp = pltpu.make_async_copy(keep.at[kslot], states_o.at[n * parts + j], ksem.at[order])
+            cp.start()
+            outs.append(cp)
+            order += 1
+            lane_sums(seen, coef.at[tokens_of(n)], count, rank + nstate + j * count)
+
+        def some(idx, carry, n=n):
             where, i = split_at(idx, steps // 32)
             q, g = split_at(where, 2)
             for d in range(groups):
                 v = y[d, pl.ds(q * 2 + g + i * 256, 32, stride=8), :]
-                at_ = rows_at(where * steps + i * 32, 32, 16)
+                at_ = rows_at(n * BLOCK_TOKENS + where * steps + i * 32, 32, 16)
                 gated[at_, cut(d)] = (v * ga[at_, cut(d)]).astype(BF16)
                 dgate[at_, cut(d)] = (v * dgs[at_, cut(d)]).astype(BF16)
             return carry
 
         lax.fori_loop(0, 8 * (steps // 32), some, 0)
+    for cp in outs[-2:]:
+        cp.wait()
+
+
+def middle(nf, ns, cid, reach, step, mix, dy, beg, packed, rate, vecs, ga, dgs, rank, count):
+    groups, tokens, _ = step.shape
+    nstate, ch = rate.shape[1], groups * 128
+    blocks = tokens // BLOCK_TOKENS
+    steps = BLOCK_TOKENS // 8
+    parts = nstate // count
+    size = count * groups
+    shape = jax.ShapeDtypeStruct
+    v = pltpu.VMEM
+    sem = pltpu.SemaphoreType.DMA
+    rows_ = size // 2 * 8
+    slots = parts if blocks == 1 else 1
+    return pl.pallas_call(
+        functools.partial(mid_kernel, nf, ns, reach, count, rank, nstate),
+        out_shape=(
+            shape((tokens, ch), BF16),
+            shape((tokens, ch), BF16),
+            shape((blocks * parts, steps, size, 8, 128), F32),
+            shape((tokens, 128), F32),
+            shape((blocks, nstate, 8, ch), F32),
+        ),
+        in_specs=[VMEM] * 7 + [ANY] * 2,
+        out_specs=[VMEM, VMEM, ANY, VMEM, VMEM],
+        scratch_shapes=[
+            v((slots, BLOCK_TOKENS, 2 * count * 128), F32),
+            v((BLOCK_TOKENS, count * 128), F32),
+            v((groups, BLOCK_TOKENS, 128), F32),
+            v((2, steps, size, 8, 128), F32),
+            v((blocks, parts, size, 8, 128), F32),
+            v((blocks, parts, size, 8, 128), F32),
+            v((blocks, parts, size, 8, 128), F32),
+            v((8, 128), F32),
+            v((blocks, parts, rows_, 128), BF16),
+            v((blocks, parts, rows_, 128), BF16),
+            v((blocks, parts, reach, rows_, 128), BF16),
+            v((blocks, parts, reach, rows_, 128), BF16),
+            v((blocks, groups, 8, 128), F32),
+            v((blocks, reach, groups, 8, 128), F32),
+            v((blocks, reach, groups, 8, 128), F32),
+            v((tokens, ch), F32),
+            v((tokens, ch), F32),
+            sem((2, blocks, parts, reach)),
+            sem((2, blocks, parts, reach)),
+            sem((2, blocks, reach)),
+            sem((2, blocks, reach)),
+            sem((blocks * parts,)),
+            sem((2,)),
+        ],
+        compiler_params=comm_params(cid, 63 << 20),
+        name="middle",
+    )(step, mix, dy, beg, packed, rate, vecs, ga, dgs)
 
 
 def backward_kernel(
@@ -768,7 +854,7 @@
     size = count * groups
     keys = [(d, i) for d in range(groups) for i in range(count)]
     rates = rates_of(rate, keys)
-    spread_coefs(packed, cscr, j * count, count, nstate)
+    spread_coefs(packed[...], cscr, j * count, count, nstate)
 
     @pl.when(j == 0)
     def _():
@@ -822,30 +908,6 @@
             tot[d, at_, :] += line
 
     lane_sums(seen_scr, coef, count, rank + j * count)
-
-
-def scan_forward(step, mix, dy, beg, packed, rate, hin, ga, dgs, vecs, rank, count):
-    groups, tokens, _ = step.shape
-    nstate, ch = rate.shape
-    grid, groups, tok, narrow, marks, rates, state, flat, kept, kept_shape = scan_specs(tokens, ch, nstate, count)
-    shape = jax.ShapeDtypeStruct
-    work = tokens * nstate * ch
-    vec = pl.BlockSpec(vecs.shape, lambda n, j: (0, 0, 0))
-    return pl.pallas_call(
-        functools.partial(forward_kernel, count, groups, rank, nstate),
-        out_shape=(shape((tokens, ch), BF16), shape((tokens, ch), BF16), kept_shape, shape((tokens, 128), F32)),
-        grid=grid,
-        in_specs=[tok, tok, tok, marks, narrow, rates, state, flat, flat, vec],
-        out_specs=[flat, flat, kept, narrow],
-        scratch_shapes=[
-            pltpu.VMEM((BLOCK_TOKENS, 2 * count * 128), F32),
-            pltpu.VMEM((BLOCK_TOKENS, count * 128), F32),
-            pltpu.VMEM((groups, BLOCK_TOKENS, 128), F32),
-        ],
-        compiler_params=pltpu.CompilerParams(vmem_limit_bytes=60 << 20),
-        cost_estimate=pl.CostEstimate(flops=8 * work, bytes_accessed=4 * work, transcendentals=work),
-        name="scan_forward",
-    )(step, mix, dy, beg, packed, rate.reshape(nstate // count, count, ch), hin, ga, dgs, vecs)
 
 
 def scan_backward(step, mix, dy, beg, packed, rate, lin, states, reads, rank, count):
@@ -1468,46 +1530,10 @@
     rate = -jnp.exp(log_decay.astype(F32))
     rate2 = rate * LOG2E
 
-    def stacked(v):
-        return v.reshape((blocks, half, 8) + v.shape[1:])
-
-    b, p, g = scan_ends(step, mix, dy, beg, packed, rate2, count)
-    resets = beg.reshape(blocks, half + 2, 8, 128)[:, 2:].max(axis=1)[:, :, :1]
-    run = jnp.moveaxis(jnp.sum(step.reshape(groups, blocks, half, 8, 128), axis=2), 0, 2).reshape(blocks, 8, ch) + resets
-
-    def halves(v):
-        v = v.reshape(v.shape[:-2] + (4, 2, ch))
-        return v[..., 0, :], v[..., 1, :]
-
-    b0, b1 = halves(b)
-    p0, p1 = halves(p)
-    g0, g1 = halves(g)
-    r0, r1 = halves(run)
-    flat = (blocks * nstate * 4, ch)
-    bf, gb, tf, tb = carry_over_seq(
-        reach,
-        ns,
-        2,
-        (p1 * b0 + b1).astype(BF16).reshape(flat),
-        (g0 + p0 * g1).astype(BF16).reshape(flat),
-        (r0 + r1).reshape(blocks * 4, ch),
+    rates = jnp.moveaxis(rate2.reshape(nstate, groups, 128), 1, 0)
+    gated, d_gate, states, coef_read, lin = middle(
+        nf, ns, 2, reach, step, mix, dy, beg, packed, rates, vecs, ga, dgs, rank, count
     )
-    state_shape = (blocks, nstate, 4, ch)
-
-    def gathered(ends, sums, valid):
-        state = jnp.zeros(state_shape, F32)
-        for j in range(reach - 1, -1, -1):
-            decay = jnp.exp2(rate2[None, :, None, :] * sums[j].reshape(blocks, 1, 4, ch))
-            new = decay * state + ends[j].reshape(state_shape).astype(F32)
-            state = jnp.where(valid(j + 1), new, 0.0)
-        return state
-
-    h_first = gathered(bf, tf, lambda j: s - j >= 0)
-    l_last = gathered(gb, tb, lambda j: s + j < ns)
-    hin = jnp.stack([h_first, p0 * h_first + b0], axis=3).reshape(blocks, nstate, 8, ch)
-    lin = jnp.stack([g1 + p1 * l_last, l_last], axis=3).reshape(blocks, nstate, 8, ch)
-
-    gated, d_gate, states, coef_read = scan_forward(step, mix, dy, beg, packed, rate2, hin, ga, dgs, vecs, rank, count)
     nq = 2 if ch % 256 == 0 else 1
     cq = ch // nq
     piece_rows = width // nf // ns

time: 307 us -> 281 us (0.915)
  Pallas kernels: 242 us -> 229 us
  local copies, waits for them, and re-layouts: 21.7 us -> 13.5 us
    pallas_call x3 -> x1, Pallas kernels: 60.8 us -> 46.3 us  [middle(): pl.pallas_call(functools.partial(mid_kernel, nf, ns, reach, count, rank,...]
    unnamed x38 -> x24, local copies, waits for them, and re-layouts: 8.13 us -> 2.62 us
  transfers between devices with their start and end apart: 2 -> 2, of which waited for: 0 -> 0; matrix products, arithmetic and copies ran while one was open for 4% -> 5% of each run, Pallas kernels for 41% -> 45%
where the time goes in v3:
time: 281 us; the launch traced here: 280 us
  Pallas kernels  229 us (81%)
  between operations  15.7 us (6%)
  local copies, waits for them, and re-layouts  13.5 us (5%)
  other arithmetic  12.1 us (4%)
  matrix products  9.81 us (3%)
    pallas_call x1, Pallas kernels, post(): pl.pallas_call(functools.partial(post_kernel, nf, ns, nq, rd, rank, nstat...  93 us
    pallas_call x1, Pallas kernels, front(): pl.pallas_call(functools.partial(front_kernel, nf, ns, rd, rank, nstate,...  56.3 us
    pallas_call x1, Pallas kernels, middle(): pl.pallas_call(functools.partial(mid_kernel, nf, ns, reach, count, rank,...  46.3 us
    pallas_call x1, Pallas kernels, scan_backward(): pl.pallas_call(functools.partial(backward_kernel, count, groups, rank, ns...  32.9 us
    dot_general x3, matrix products, rows_inner(): lax.dot_general(left, right, (((0,), (0,)), ((), ())), preferred_element_...  7.18 us
  transfers between devices with their start and end apart: 2, of which 0 were waited for; matrix products, arithmetic and copies ran while one was open for 5% of the time, Pallas kernels for 45%

profile of v3, /device:TPU:0, one launch (start us, length us, event | category | flops | bytes accessed | tf_op | source)
XLA Modules:
  0.0 280.1 jit_solution(6822374596978122064)
XLA Ops:
  8.0 0.0 all-reduce.4.cloned.1.call-start
  8.1 0.7 convert_element_type.41
  8.7 0.7 bitcast_convert_fusion
  9.4 0.7 copy.32
  10.1 0.7 copy.33
  10.7 0.7 copy.34
  11.4 0.7 concatenate.29
  12.1 0.6 convert_bitcast_fusion.refs_4_.refs_6_.refs_14_
  12.7 1.0 copy.35
  13.8 0.7 pad.9.refs_5_.refs_15_
  14.5 0.7 negate_multiply_fusion
  15.2 0.6 copy.52
  15.8 0.6 select_maximum_fusion.refs_3_
  16.4 56.3 %front.1 = (bf16[1024,1024]{1,0:T(8,128)(2,1)}, bf16[1024,1024]{1,0:T(8,128)(2,1)}, f32[4,1048,128]{2,1,0:T(8,128)}, f32[4,1024,128]{2,1,0:T(8,128)}, f32[4,1024...) custom-call(bf16[1,256,1024]{2,1,0:T(8,128)(2,1)} %refs_0_.1, ...), custom_call_target="tpu_custom_call" | custom-call | tf_op jit(solution)/shard_map/front/pallas_call | solution.py:501
  72.7 46.3 %middle.1 = (bf16[1024,512]{1,0:T(8,128)(2,1)}, bf16[1024,512]{1,0:T(8,128)(2,1)}, f32[4,128,16,8,128]{4,3,2,1,0:T(8,128)}, f32[1024,128]{1,0:T(8,128)}, f32[1,16,8,512]{3,2,1,0:T(8,128)}) custom-call(f32[4,1024,128]{2,1,0:T(8,128)} %get-tuple-element.48.refs_0_.step.refs_3_, f32[4,1024,128]{2,1,0:T(8,128)} %get-tuple-element.49.refs_1_.mix.refs_2_, ...), custom_call_target="tpu_custom_call" | custom-call | tf_op jit(solution)/shard_map/middle/pallas_call | solution.py:808
  119.0 0.0 copy-start.1
  119.0 0.0 copy-start.3
  119.0 3.4 %convolution_convert_fusion.3 = bf16[1024,256]{1,0:T(8,128)(2,1)} fusion(bf16[1024,1024]{1,0:T(8,128)(2,1)} %get-tuple-element.58.refs_8_, bf16[1024,512]{1,0:T(8,128)(2,1)} %get-tuple-element.59.refs_11_), kind=kOutput, calls=%fused_computation.4 | convolution fusion | flops 537133056 | bytes 3145728 | tf_op jit(solution)/shard_map/dot_general | solution.py:1472
  122.4 0.0 copy-done.1
  122.4 0.0 copy-done.3
  122.4 0.0 copy-start.5
  122.4 0.0 copy-start.6
  122.4 1.6 convolution_convert_fusion.2
  124.0 0.0 copy-done.5
  124.0 0.0 copy-done.6
  124.0 0.0 copy-start.2
  124.0 2.6 convolution_convert_fusion
  126.6 0.0 copy-done.2
  126.6 2.2 convolution_convert_fusion.1
  128.9 0.0 all-reduce.4.cloned.1.call-update
  128.9 0.0 reduce-scatter.2.cloned.1.call-start
  128.9 0.5 reduce-scatter.2.cloned.1.call-update
  129.5 0.6 reshape.116.rate
  130.1 32.9 %scan_backward.1 = (f32[4,1024,128]{2,1,0:T(8,128)}, f32[4,1024,128]{2,1,0:T(8,128)}, f32[1024,128]{1,0:T(8,128)}, f32[4,16,128]{2,1,0:T(8,128)}) custom-call(f32[4,1024,128]{2,1,0:T(8,128)} %get-tuple-element.48.refs_0_.step.refs_3_, f32[4,1024,128]{2,1,0:T(8,128)} %get-tuple-element.49.refs_1_.mix.refs_2_, ...), custom_call_target="tpu_custom_call" | custom-call | flops 100663296 | bytes 33554432 | tf_op jit(solution)/shard_map/scan_backward/pallas_call | solution.py:919
  163.0 93.0 %post.1 = (f32[256,1024]{1,0:T(8,128)}, f32[1,1024]{1,0:T(1,128)}, f32[896,128]{1,0:T(8,128)}, bf16[2,4,4,32,256]{4,3,2,1,0:T(8,128)(2,1)}, bf16[2,4,4,32,256]{4...) custom-call(f32[4,1024,128]{2,1,0:T(8,128)} %get-tuple-element.64.refs_0_, ...), custom_call_target="tpu_custom_call" | custom-call | tf_op jit(solution)/shard_map/post/pallas_call | solution.py:1460
  256.1 1.3 maximum_bitcast_fusion.1
  257.3 0.0 copy-start.7
  257.4 0.0 copy-start.8
  257.4 0.8 copy.38
  258.2 0.3 copy.48
  258.5 0.0 copy-done.7
  258.5 0.1 copy-done.8
  258.5 0.1 maximum_bitcast_fusion
  258.6 0.0 copy-start.9
  258.7 0.8 copy.37
  259.5 0.3 copy.47
  259.7 0.0 copy-done.9
  259.8 0.8 copy.43
  260.6 1.2 constant_dynamic-slice_fusion
  261.8 0.6 fusion.9
  262.4 0.6 slice_bitcast_fusion.3
  263.0 0.6 copy_bitcast_fusion.1
  263.6 0.7 copy_bitcast_fusion
  264.3 2.5 maximum_convert_fusion
  266.8 0.0 copy-start
  266.8 0.0 copy-start.4
  266.8 0.0 all-reduce.4.cloned.1.call-done
  266.8 2.9 %convert_element_type.50 = f32[512,1024]{1,0:T(8,128)} convert(bf16[512,1024]{1,0:T(8,128)(2,1)} %all-reduce.4.cloned.1.call-done) | non-fusion elementwise | flops 524288 | bytes 3145728 | tf_op jit(solution)/shard_map/convert_element_type | solution.py:1591
  269.7 0.0 reduce-scatter.2.cloned.1.call-done
  269.7 0.0 copy-done
  269.7 2.0 fusion
  271.7 0.0 copy-done.4
  271.7 1.0 copy.55
  (6 shorter events, 0.1 us)
Async XLA Ops:
  8.0 258.8 %all-reduce.4.cloned.1.call-start = ((), (), s32[]{:S(2)}) async-start(), calls=%async_computation.2 | async-start | bytes 2097152 | tf_op jit(solution)/shard_map/psum | solution.py:1548
  119.0 3.4 %copy-start.1 = (bf16[1024,1024]{1,0:T(8,128)(2,1)S(1)}, bf16[1024,1024]{1,0:T(8,128)(2,1)}, u32[]{:S(2)}) copy-start(bf16[1024,1024]{1,0:T(8,128)(2,1)} %get-tuple-element.58.refs_8_) | copy-start | bytes 6291460
  119.0 3.4 %copy-start.3 = (bf16[1024,512]{1,0:T(8,128)(2,1)S(1)}, bf16[1024,512]{1,0:T(8,128)(2,1)}, u32[]{:S(2)}) copy-start(bf16[1024,512]{1,0:T(8,128)(2,1)} %get-tuple-element.59.refs_11_) | copy-start | bytes 3145732
  122.4 1.6 copy-start.5
  122.4 1.6 copy-start.6
  124.0 2.6 copy-start.2
  128.9 140.8 %reduce-scatter.2.cloned.1.call-start = ((), (), s32[]{:S(2)}) async-start(), calls=%async_computation.1 | async-start | bytes 2621440 | tf_op jit(solution)/shard_map/reduce_scatter | solution.py:1549
  257.3 1.1 copy-start.7
  257.4 1.2 copy-start.8
  258.6 1.1 copy-start.9
  266.8 2.9 %copy-start = (bf16[1,256,1024]{2,1,0:T(8,128)(2,1)S(1)}, bf16[1,256,1024]{2,1,0:T(8,128)(2,1)}, u32[]{:S(2)}) copy-start(bf16[1,256,1024]{2,1,0:T(8,128)(2,1)} %refs_0_.1) | copy-start | bytes 1572868
  266.8 5.0 %copy-start.4 = (f32[256,1024]{1,0:T(8,128)S(1)}, f32[256,1024]{1,0:T(8,128)}, u32[]{:S(2)}) copy-start(f32[256,1024]{1,0:T(8,128)} %get-tuple-element.76) | copy-start | bytes 3145732
Sparse Core Ops, SparseCore 0:
  129.0 90.6 all-reduce.3
Sparse Core Ops, SparseCore 1:
  131.9 30.3 reduce-scatter.1

commit v4 on v3

--- a/solution.py
+++ b/solution.py
@@ -1468,6 +1468,77 @@
     )(*big, *little, *gates)
 
 
+def last_kernel(ns, nf, nq, ni, rank, nstate, nsel, nextra, *refs):
+    gates, inners = refs[:nq], refs[nq : nq + ni]
+    og, x, rout, small = refs[nq + ni : nq + ni + 4]
+    extras = refs[nq + ni + 4 : nq + ni + 4 + nextra]
+    outs = refs[nq + ni + 4 + nextra :]
+    layer, residual, grad_o, taps, select, step, decay, vectors, ogf, grad, sem = outs
+    groups = select.shape[0] // 128
+    ch = groups * 128
+    na = ns // 2
+    prow = gates[0].shape[3]
+    inner_all = nf * ch
+    copies = []
+    for p in range(ns):
+        at_ = slice(p * prow, (p + 1) * prow)
+        for parts, base in ((inners, 0), (gates, inner_all)):
+            cq = ch // len(parts)
+            for q, part in enumerate(parts):
+                for k in range(nf):
+                    start = base + k * ch + q * cq
+                    grad[at_, start : start + cq] = part[p // na, p % na, k].astype(F32)
+        if prow % 8 == 0:
+            copies.append(pltpu.make_async_copy(grad.at[at_], grad_o.at[at_], sem.at[p]))
+            copies[-1].start()
+    if prow % 8:
+        copies.append(pltpu.make_async_copy(grad, grad_o, sem.at[0]))
+        copies[-1].start()
+    ogf[...] = og[...].astype(F32)
+    residual[...] = rout[...]
+    total = x[...].astype(F32)
+    for e in extras:
+        total = total + e[...].astype(F32)
+    layer[...] = total.astype(BF16)
+    off_select, off_step, off_decay, off_vec, group_rows, _ = small_layout(groups, rank, nstate, ns)
+    for d in range(groups):
+        base = d * group_rows
+        select[d * 128 : (d + 1) * 128, :] = small[base + off_select : base + off_step, :].astype(F32)[:, :nsel]
+        step[:, cut(d)] = small[base + off_step : base + off_decay, :].astype(F32)
+        decay[:, cut(d)] = small[base + off_decay : base + off_vec, :].astype(F32)
+        line = small[base + off_vec : base + group_rows, :].astype(F32)
+        vectors[:, cut(d)] = line
+        taps[:, cut(d)] = line[:4]
+    for cp in copies:
+        cp.wait()
+
+
+def last(nf, ns, rank, nstate, nsel, gates, inners, og, x, rout, small, extras):
+    shape = jax.ShapeDtypeStruct
+    nq, ni = len(gates), len(inners)
+    ch = og.shape[0]
+    drow = gates[0].shape[3] * ns
+    return pl.pallas_call(
+        functools.partial(last_kernel, ns, nf, nq, ni, rank, nstate, nsel, len(extras)),
+        out_shape=(
+            shape(x.shape, BF16),
+            shape(rout.shape, F32),
+            shape((drow, 2 * nf * ch), F32),
+            shape((4, ch), F32),
+            shape((ch, nsel), F32),
+            shape((rank, ch), F32),
+            shape((nstate, ch), F32),
+            shape((8, ch), F32),
+            shape(og.shape, F32),
+        ),
+        in_specs=[VMEM] * (nq + ni + 4 + len(extras)),
+        out_specs=[VMEM, VMEM, ANY] + [VMEM] * 6,
+        scratch_shapes=[pltpu.VMEM((drow, 2 * nf * ch), F32), pltpu.SemaphoreType.DMA((ns,))],
+        compiler_params=pltpu.CompilerParams(vmem_limit_bytes=56 << 20),
+        name="last",
+    )(*gates, *inners, og, x, rout, small, *extras)
+
+
 def rows_inner(left, right):
     return lax.dot_general(left, right, (((0,), (0,)), ((), ())), preferred_element_type=F32)
 
@@ -1562,33 +1633,33 @@
         decay,
     )
     residual_grad, gain_sum, small_sum, *sums = post(nf, ns, nq, 3, rd, rank, nstate, big, little, gate_grads)
-    layer_output = (residual.reshape(rd * stretch, width).astype(F32) + out_sum.astype(F32)).astype(BF16)
-
-    def side(parts):
-        parts = [v.reshape(ns, nf, piece_rows, cq) for v in parts]
-        return jnp.moveaxis(jnp.concatenate(parts, axis=3), 1, 2).reshape(width // nf, nf * ch)
-
-    input_grad = jnp.concatenate([side(sums[nq:]), side(sums[:nq])], axis=1).astype(F32)
-    off_select, off_step, off_decay, off_vec, group_rows, _ = small_layout(groups, rank, nstate, ns)
-    small_sum = small_sum[: groups * group_rows].reshape(groups, group_rows, 128)
-
-    def section(start, count_):
-        return jnp.moveaxis(small_sum[:, start : start + count_], 0, 1).reshape(count_, ch)
-
-    vectors = section(off_vec, 8)
+    layer_output, residual_grad, input_grad, kernel_grad, select_grad, step_grad, decay_grad, vectors, output_grad = last(
+        nf,
+        ns,
+        rank,
+        nstate,
+        select_proj.shape[1],
+        sums[:nq],
+        sums[nq:],
+        output_grad,
+        residual.reshape(rd * stretch, width),
+        residual_grad,
+        small_sum,
+        [out_sum],
+    )
     return (
         layer_output.reshape(rd, stretch, width),
         residual_grad.reshape(rd, stretch, width),
         lax.dynamic_slice(gain_sum[0], (f * grows,), (grows,)),
         input_grad,
-        vectors[:4],
+        kernel_grad,
         vectors[4],
-        small_sum[:, :off_step, : select_proj.shape[1]].reshape(ch, select_proj.shape[1]),
-        section(off_step, rank),
+        select_grad,
+        step_grad,
         vectors[5],
-        section(off_decay, nstate),
+        decay_grad,
         vectors[6],
-        output_grad.astype(F32),
+        output_grad,
     )
 
 

time: 281 us -> 276 us (0.982)
  other arithmetic: 12.1 us -> 3.27 us
  Pallas kernels: 229 us -> 236 us
  local copies, waits for them, and re-layouts: 13.5 us -> 10.1 us
    pallas_call x0 -> x1, Pallas kernels: none -> 6.69 us  [last(): pl.pallas_call(functools.partial(last_kernel, ns, nf, nq, ni, rank, nstat...]
    convert_element_type x2 -> x0, other arithmetic: 5.41 us -> none  [the longest x1 2.91 us: shards(): output_grad.astype(F32)]
  transfers between devices with their start and end apart: 2 -> 2, of which waited for: 0 -> 0; matrix products, arithmetic and copies ran while one was open for 5% -> 1% of each run, Pallas kernels for 45% -> 46%
where the time goes in v4:
time: 276 us; the launch traced here: 275 us
  Pallas kernels  236 us (86%)
  between operations  15.6 us (6%)
  local copies, waits for them, and re-layouts  10.1 us (4%)
  matrix products  9.85 us (4%)
  other arithmetic  3.27 us (1%)
    pallas_call x1, Pallas kernels, post(): pl.pallas_call(functools.partial(post_kernel, nf, ns, nq, rd, rank, nstat...  93.5 us
    pallas_call x1, Pallas kernels, front(): pl.pallas_call(functools.partial(front_kernel, nf, ns, rd, rank, nstate,...  56.3 us
    pallas_call x1, Pallas kernels, middle(): pl.pallas_call(functools.partial(mid_kernel, nf, ns, reach, count, rank,...  46.2 us
    pallas_call x1, Pallas kernels, scan_backward(): pl.pallas_call(functools.partial(backward_kernel, count, groups, rank, ns...  32.9 us
    dot_general x3, matrix products, rows_inner(): lax.dot_general(left, right, (((0,), (0,)), ((), ())), preferred_element_...  7.2 us
    pallas_call x1, Pallas kernels, last(): pl.pallas_call(functools.partial(last_kernel, ns, nf, nq, ni, rank, nstat...  6.69 us
  transfers between devices with their start and end apart: 2, of which 0 were waited for; matrix products, arithmetic and copies ran while one was open for 1% of the time, Pallas kernels for 46%

profile of v4, /device:TPU:0, one launch (start us, length us, event | category | flops | bytes accessed | tf_op | source)
XLA Modules:
  0.0 275.1 jit_solution(11449804489666137550)
XLA Ops:
  8.0 0.0 all-reduce.4.cloned.1.call-start
  8.1 0.7 convert_element_type.25
  8.7 0.7 bitcast_convert_fusion
  9.4 0.7 copy.27
  10.1 0.7 copy.28
  10.7 0.7 copy.29
  11.4 0.7 concatenate.20
  12.1 0.6 convert_bitcast_fusion.refs_4_.refs_6_.refs_14_
  12.8 0.7 fusion.7
  13.5 0.6 copy.35
  14.1 1.0 copy.30
  15.1 0.7 pad.9.refs_5_.refs_15_
  15.8 0.6 select_maximum_fusion.refs_3_
  16.4 56.3 %front.1 = (bf16[1024,1024]{1,0:T(8,128)(2,1)}, bf16[1024,1024]{1,0:T(8,128)(2,1)}, f32[4,1048,128]{2,1,0:T(8,128)}, f32[4,1024,128]{2,1,0:T(8,128)}, f32[4,1024...) custom-call(bf16[1,256,1024]{2,1,0:T(8,128)(2,1)} %refs_0_.1, ...), custom_call_target="tpu_custom_call" | custom-call | tf_op jit(solution)/shard_map/front/pallas_call | solution.py:501
  72.7 46.2 %middle.1 = (bf16[1024,512]{1,0:T(8,128)(2,1)}, bf16[1024,512]{1,0:T(8,128)(2,1)}, f32[4,128,16,8,128]{4,3,2,1,0:T(8,128)}, f32[1024,128]{1,0:T(8,128)}, f32[1,16,8,512]{3,2,1,0:T(8,128)}) custom-call(f32[4,1024,128]{2,1,0:T(8,128)} %get-tuple-element.57.refs_0_.step.refs_3_, f32[4,1024,128]{2,1,0:T(8,128)} %get-tuple-element.58.refs_1_.mix.refs_2_, ...), custom_call_target="tpu_custom_call" | custom-call | tf_op jit(solution)/shard_map/middle/pallas_call | solution.py:808
  119.0 0.0 copy-start
  119.0 0.0 copy-start.2
  119.0 3.4 %convolution_convert_fusion.2 = bf16[1024,256]{1,0:T(8,128)(2,1)} fusion(bf16[1024,1024]{1,0:T(8,128)(2,1)} %get-tuple-element.67.refs_8_, bf16[1024,512]{1,0:T(8,128)(2,1)} %get-tuple-element.68.refs_11_), kind=kOutput, calls=%fused_computation.2 | convolution fusion | flops 537133056 | bytes 3145728 | tf_op jit(solution)/shard_map/dot_general | solution.py:1543
  122.4 0.0 copy-done
  122.4 0.0 copy-done.2
  122.4 0.0 copy-start.3
  122.4 0.0 copy-start.4
  122.4 1.6 convolution_convert_fusion.3
  124.0 0.0 copy-done.3
  124.0 0.0 copy-done.4
  124.0 0.0 copy-start.1
  124.0 2.6 convolution_convert_fusion
  126.6 0.0 copy-done.1
  126.6 2.2 convolution_convert_fusion.1
  128.9 0.0 all-reduce.4.cloned.1.call-update
  128.9 0.0 reduce-scatter.2.cloned.1.call-start
  129.0 0.5 reduce-scatter.2.cloned.1.call-update
  129.5 0.6 reshape.73.rate
  130.1 32.9 %scan_backward.1 = (f32[4,1024,128]{2,1,0:T(8,128)}, f32[4,1024,128]{2,1,0:T(8,128)}, f32[1024,128]{1,0:T(8,128)}, f32[4,16,128]{2,1,0:T(8,128)}) custom-call(f32[4,1024,128]{2,1,0:T(8,128)} %get-tuple-element.57.refs_0_.step.refs_3_, f32[4,1024,128]{2,1,0:T(8,128)} %get-tuple-element.58.refs_1_.mix.refs_2_, ...), custom_call_target="tpu_custom_call" | custom-call | flops 100663296 | bytes 33554432 | tf_op jit(solution)/shard_map/scan_backward/pallas_call | solution.py:919
  163.0 93.5 %post.1 = (f32[256,1024]{1,0:T(8,128)}, f32[1,1024]{1,0:T(1,128)}, f32[896,128]{1,0:T(8,128)}, bf16[2,4,4,32,256]{4,3,2,1,0:T(8,128)(2,1)}, bf16[2,4,4,32,256]{4...) custom-call(f32[4,1024,128]{2,1,0:T(8,128)} %get-tuple-element.72.refs_0_, ...), custom_call_target="tpu_custom_call" | custom-call | tf_op jit(solution)/shard_map/post/pallas_call | solution.py:1460
  256.5 1.2 constant_dynamic-slice_fusion
  257.7 0.0 all-reduce.4.cloned.1.call-done.refs_4_
  257.7 0.0 reduce-scatter.2.cloned.1.call-done.refs_8_
  257.7 6.7 %last.1 = (bf16[256,1024]{1,0:T(8,128)(2,1)}, f32[256,1024]{1,0:T(8,128)}, f32[256,4096]{1,0:T(8,128)}, f32[4,512]{1,0:T(4,128)}, f32[512,96]{1,0:T(8,128)}, /*i...) custom-call(bf16[2,4,4,32,256]{4,3,2,1,0:T(8,128)(2,1)} %get-tuple-element.84.refs_0_, ...), custom_call_target="tpu_custom_call" | custom-call | tf_op jit(solution)/shard_map/last/pallas_call | solution.py:1521
  264.4 1.4 fusion.8
  265.9 1.8 copy.32
  (3 shorter events, 0.0 us)
Async XLA Ops:
  8.0 249.7 %all-reduce.4.cloned.1.call-start = ((), (), s32[]{:S(2)}) async-start(), calls=%async_computation.1 | async-start | bytes 2097152 | tf_op jit(solution)/shard_map/psum | solution.py:1619
  119.0 3.4 %copy-start = (bf16[1024,1024]{1,0:T(8,128)(2,1)S(1)}, bf16[1024,1024]{1,0:T(8,128)(2,1)}, u32[]{:S(2)}) copy-start(bf16[1024,1024]{1,0:T(8,128)(2,1)} %get-tuple-element.67.refs_8_) | copy-start | bytes 6291460
  119.0 3.4 %copy-start.2 = (bf16[1024,512]{1,0:T(8,128)(2,1)S(1)}, bf16[1024,512]{1,0:T(8,128)(2,1)}, u32[]{:S(2)}) copy-start(bf16[1024,512]{1,0:T(8,128)(2,1)} %get-tuple-element.68.refs_11_) | copy-start | bytes 3145732
  122.4 1.6 copy-start.3
  122.4 1.6 copy-start.4
  124.0 2.6 copy-start.1
  128.9 128.8 %reduce-scatter.2.cloned.1.call-start = ((), (), s32[]{:S(2)}) async-start(), calls=%async_computation.2 | async-start | bytes 2621440 | tf_op jit(solution)/shard_map/reduce_scatter | solution.py:1620
Sparse Core Ops, SparseCore 0:
  129.0 90.5 all-reduce.3
Sparse Core Ops, SparseCore 1:
  132.1 30.4 reduce-scatter.1

commit v5 on v4

--- a/solution.py
+++ b/solution.py
@@ -327,7 +327,7 @@
     def project(start):
         total = None
         for d in range(groups):
-            term = jnp.dot(mixb[d, rows_at(start, hs, 16), :], w_sel[d * 128 : (d + 1) * 128, :], preferred_element_type=F32)
+            term = times_transposed(mixb[d, rows_at(start, hs, 16), :], w_sel[:, cut(d)])
             total = term if total is None else total + term
         part[rows_at(start, hs), :] = total
 
@@ -1161,7 +1161,7 @@
         low_all = rows_at(start, hs, 16)
         dproj[low_all, :] = sums[at_all, :].astype(BF16)
         for d in range(groups):
-            slopes[d, at_all, :] = times_transposed(dproj[low_all, :], w_sel[d * 128 : (d + 1) * 128, :])
+            slopes[d, at_all, :] = jnp.dot(dproj[low_all, :], w_sel[:, cut(d)], preferred_element_type=F32)
 
             def one(c, carry, d=d):
                 row = start + c * chunk
@@ -1470,11 +1470,11 @@
 
 def last_kernel(ns, nf, nq, ni, rank, nstate, nsel, nextra, *refs):
     gates, inners = refs[:nq], refs[nq : nq + ni]
-    og, x, rout, small = refs[nq + ni : nq + ni + 4]
-    extras = refs[nq + ni + 4 : nq + ni + 4 + nextra]
-    outs = refs[nq + ni + 4 + nextra :]
-    layer, residual, grad_o, taps, select, step, decay, vectors, ogf, grad, sem = outs
-    groups = select.shape[0] // 128
+    og, x, rout, small, gain = refs[nq + ni : nq + ni + 5]
+    extras = refs[nq + ni + 5 : nq + ni + 5 + nextra]
+    outs = refs[nq + ni + 5 + nextra :]
+    layer, residual, grad_o, taps, select, step, decay, ogf, one, two, three, gain_o, grad, sem = outs
+    groups = select.shape[1] // 128
     ch = groups * 128
     na = ns // 2
     prow = gates[0].shape[3]
@@ -1503,17 +1503,24 @@
     off_select, off_step, off_decay, off_vec, group_rows, _ = small_layout(groups, rank, nstate, ns)
     for d in range(groups):
         base = d * group_rows
-        select[d * 128 : (d + 1) * 128, :] = small[base + off_select : base + off_step, :].astype(F32)[:, :nsel]
+        select[:, cut(d)] = jnp.transpose(small[base + off_select : base + off_step, :])[:nsel]
         step[:, cut(d)] = small[base + off_step : base + off_decay, :].astype(F32)
         decay[:, cut(d)] = small[base + off_decay : base + off_vec, :].astype(F32)
         line = small[base + off_vec : base + group_rows, :].astype(F32)
-        vectors[:, cut(d)] = line
+        for row_, out in ((4, one), (5, two), (6, three)):
+            out[:, cut(d)] = line[row_ : row_ + 1]
         taps[:, cut(d)] = line[:4]
+    width = gain_o.shape[1]
+    if width % 128 == 0:
+        f, _ = here()
+        gain_o[...] = gain[:, pl.ds(pl.multiple_of(f * width, 128), width)]
+    else:
+        gain_o[...] = gain[:, :width]
     for cp in copies:
         cp.wait()
 
 
-def last(nf, ns, rank, nstate, nsel, gates, inners, og, x, rout, small, extras):
+def last(nf, ns, rank, nstate, nsel, gates, inners, og, x, rout, small, gain, extras):
     shape = jax.ShapeDtypeStruct
     nq, ni = len(gates), len(inners)
     ch = og.shape[0]
@@ -1525,18 +1532,21 @@
             shape(rout.shape, F32),
             shape((drow, 2 * nf * ch), F32),
             shape((4, ch), F32),
-            shape((ch, nsel), F32),
+            shape((nsel, ch), F32),
             shape((rank, ch), F32),
             shape((nstate, ch), F32),
-            shape((8, ch), F32),
             shape(og.shape, F32),
+            shape((1, ch), F32),
+            shape((1, ch), F32),
+            shape((1, ch), F32),
+            shape((1, gain.shape[1] // nf), F32),
         ),
-        in_specs=[VMEM] * (nq + ni + 4 + len(extras)),
-        out_specs=[VMEM, VMEM, ANY] + [VMEM] * 6,
+        in_specs=[VMEM] * (nq + ni + 5 + len(extras)),
+        out_specs=[VMEM, VMEM, ANY] + [VMEM] * 9,
         scratch_shapes=[pltpu.VMEM((drow, 2 * nf * ch), F32), pltpu.SemaphoreType.DMA((ns,))],
         compiler_params=pltpu.CompilerParams(vmem_limit_bytes=56 << 20),
         name="last",
-    )(*gates, *inners, og, x, rout, small, *extras)
+    )(*gates, *inners, og, x, rout, small, gain, *extras)
 
 
 def rows_inner(left, right):
@@ -1594,7 +1604,7 @@
         [conv_kernel, conv_bias[None], step_bias[None], skip_gain[None], jnp.zeros((1, ch), BF16)], axis=0
     ).astype(F32)
     vecs = jnp.moveaxis(vecs.reshape(8, groups, 128), 1, 0)
-    w_sel = jnp.pad(select_proj, ((0, 0), (0, 128 - select_proj.shape[1])))
+    w_sel = jnp.pad(select_proj.T, ((0, 128 - select_proj.shape[1]), (0, 0)))
     normed, cot, ext, slope, mix, dy, ga, dgs, step, beg, proj, packed, w_inner, w_gate, gain = front(
         nf, ns, residual, out_cotangent, input_proj, small, vecs, w_sel, step_proj, output_proj, rank, nstate
     )
@@ -1633,7 +1643,7 @@
         decay,
     )
     residual_grad, gain_sum, small_sum, *sums = post(nf, ns, nq, 3, rd, rank, nstate, big, little, gate_grads)
-    layer_output, residual_grad, input_grad, kernel_grad, select_grad, step_grad, decay_grad, vectors, output_grad = last(
+    (layer_output, residual_grad, input_grad, kernel_grad, select_grad, step_grad, decay_grad, output_grad, *vectors) = last(
         nf,
         ns,
         rank,
@@ -1645,20 +1655,21 @@
         residual.reshape(rd * stretch, width),
         residual_grad,
         small_sum,
+        gain_sum,
         [out_sum],
     )
     return (
         layer_output.reshape(rd, stretch, width),
         residual_grad.reshape(rd, stretch, width),
-        lax.dynamic_slice(gain_sum[0], (f * grows,), (grows,)),
+        vectors[3][0] if grows % 128 == 0 else lax.dynamic_slice(gain_sum[0], (f * grows,), (grows,)),
         input_grad,
         kernel_grad,
-        vectors[4],
-        select_grad,
+        vectors[0][0],
+        select_grad.T,
         step_grad,
-        vectors[5],
+        vectors[1][0],
         decay_grad,
-        vectors[6],
+        vectors[2][0],
         output_grad,
     )
 

time: 276 us -> 272 us (0.986)
  local copies, waits for them, and re-layouts: 10.1 us -> 5.6 us
  transfers between devices with their start and end apart: 2 -> 2, of which waited for: 0 -> 0; matrix products, arithmetic and copies ran while one was open for 1% -> 0% of each run, Pallas kernels for 46% -> 47%
where the time goes in v5:
time: 272 us; the launch traced here: 271 us
  Pallas kernels  236 us (87%)
  between operations  15.6 us (6%)
  matrix products  9.85 us (4%)
  local copies, waits for them, and re-layouts  5.6 us (2%)
  other arithmetic  3.27 us (1%)
    pallas_call x1, Pallas kernels, post(): pl.pallas_call(functools.partial(post_kernel, nf, ns, nq, rd, rank, nstat...  93.6 us
    pallas_call x1, Pallas kernels, front(): pl.pallas_call(functools.partial(front_kernel, nf, ns, rd, rank, nstate,...  56.3 us
    pallas_call x1, Pallas kernels, middle(): pl.pallas_call(functools.partial(mid_kernel, nf, ns, reach, count, rank,...  46.2 us
    pallas_call x1, Pallas kernels, scan_backward(): pl.pallas_call(functools.partial(backward_kernel, count, groups, rank, ns...  32.9 us
    dot_general x3, matrix products, rows_inner(): lax.dot_general(left, right, (((0,), (0,)), ((), ())), preferred_element_...  7.22 us
    pallas_call x1, Pallas kernels, last(): pl.pallas_call(functools.partial(last_kernel, ns, nf, nq, ni, rank, nstat...  7.16 us
  transfers between devices with their start and end apart: 2, of which 0 were waited for; matrix products, arithmetic and copies ran while one was open for 0% of the time, Pallas kernels for 47%

profile of v5, /device:TPU:0, one launch (start us, length us, event | category | flops | bytes accessed | tf_op | source)
XLA Modules:
  0.0 271.2 jit_solution(7614379170858195989)
XLA Ops:
  8.0 0.0 all-reduce.4.cloned.1.call-start
  8.1 0.7 convert_element_type.25
  8.7 0.7 bitcast_convert_fusion
  9.4 0.7 copy.25
  10.1 0.7 copy.26
  10.7 0.7 copy.27
  11.4 0.7 concatenate.20
  12.1 0.6 convert_bitcast_fusion.refs_4_.refs_6_.refs_14_
  12.7 0.7 fusion.7
  13.5 0.6 copy.31
  14.1 1.6 pad.9.refs_5_.refs_15_
  15.7 0.6 select_maximum_fusion.refs_3_
  16.3 56.3 %front.1 = (bf16[1024,1024]{1,0:T(8,128)(2,1)}, bf16[1024,1024]{1,0:T(8,128)(2,1)}, f32[4,1048,128]{2,1,0:T(8,128)}, f32[4,1024,128]{2,1,0:T(8,128)}, f32[4,1024...) custom-call(bf16[1,256,1024]{2,1,0:T(8,128)(2,1)} %refs_0_.1, ...), custom_call_target="tpu_custom_call" | custom-call | tf_op jit(solution)/shard_map/front/pallas_call | solution.py:501
  72.6 46.2 %middle.1 = (bf16[1024,512]{1,0:T(8,128)(2,1)}, bf16[1024,512]{1,0:T(8,128)(2,1)}, f32[4,128,16,8,128]{4,3,2,1,0:T(8,128)}, f32[1024,128]{1,0:T(8,128)}, f32[1,16,8,512]{3,2,1,0:T(8,128)}) custom-call(f32[4,1024,128]{2,1,0:T(8,128)} %get-tuple-element.60.refs_0_.step.refs_3_, f32[4,1024,128]{2,1,0:T(8,128)} %get-tuple-element.61.refs_1_.mix.refs_2_, ...), custom_call_target="tpu_custom_call" | custom-call | tf_op jit(solution)/shard_map/middle/pallas_call | solution.py:808
  118.8 0.0 copy-start
  118.8 0.0 copy-start.2
  118.8 3.4 %convolution_convert_fusion.2 = bf16[1024,256]{1,0:T(8,128)(2,1)} fusion(bf16[1024,1024]{1,0:T(8,128)(2,1)} %get-tuple-element.70.refs_8_, bf16[1024,512]{1,0:T(8,128)(2,1)} %get-tuple-element.71.refs_11_), kind=kOutput, calls=%fused_computation.2 | convolution fusion | flops 537133056 | bytes 3145728 | tf_op jit(solution)/shard_map/dot_general | solution.py:1553
  122.2 0.0 copy-done
  122.2 0.0 copy-done.2
  122.2 0.0 copy-start.3
  122.2 0.0 copy-start.4
  122.3 1.6 convolution_convert_fusion.3
  123.8 0.0 copy-done.3
  123.8 0.0 copy-done.4
  123.8 0.0 copy-start.1
  123.8 2.6 convolution_convert_fusion
  126.5 0.0 copy-done.1
  126.5 2.2 convolution_convert_fusion.1
  128.7 0.0 all-reduce.4.cloned.1.call-update
  128.7 0.0 reduce-scatter.2.cloned.1.call-start
  128.8 0.5 reduce-scatter.2.cloned.1.call-update
  129.3 0.6 reshape.72.rate
  129.9 32.9 %scan_backward.1 = (f32[4,1024,128]{2,1,0:T(8,128)}, f32[4,1024,128]{2,1,0:T(8,128)}, f32[1024,128]{1,0:T(8,128)}, f32[4,16,128]{2,1,0:T(8,128)}) custom-call(f32[4,1024,128]{2,1,0:T(8,128)} %get-tuple-element.60.refs_0_.step.refs_3_, f32[4,1024,128]{2,1,0:T(8,128)} %get-tuple-element.61.refs_1_.mix.refs_2_, ...), custom_call_target="tpu_custom_call" | custom-call | flops 100663296 | bytes 33554432 | tf_op jit(solution)/shard_map/scan_backward/pallas_call | solution.py:919
  162.9 93.6 %post.1 = (f32[256,1024]{1,0:T(8,128)}, f32[1,1024]{1,0:T(1,128)}, f32[896,128]{1,0:T(8,128)}, bf16[2,4,4,32,256]{4,3,2,1,0:T(8,128)(2,1)}, bf16[2,4,4,32,256]{4...) custom-call(f32[4,1024,128]{2,1,0:T(8,128)} %get-tuple-element.75.refs_0_, ...), custom_call_target="tpu_custom_call" | custom-call | tf_op jit(solution)/shard_map/post/pallas_call | solution.py:1460
  256.5 0.0 all-reduce.4.cloned.1.call-done.refs_4_
  256.5 0.0 reduce-scatter.2.cloned.1.call-done.refs_9_
  256.5 7.2 %last.1 = (bf16[256,1024]{1,0:T(8,128)(2,1)}, f32[256,1024]{1,0:T(8,128)}, f32[256,4096]{1,0:T(8,128)}, f32[4,512]{1,0:T(4,128)}, f32[96,512]{1,0:T(8,128)}, /*i...) custom-call(bf16[2,4,4,32,256]{4,3,2,1,0:T(8,128)(2,1)} %get-tuple-e, ...), custom_call_target="tpu_custom_call" | custom-call | tf_op jit(solution)/shard_map/last/pallas_call | solution.py:1528
  (3 shorter events, 0.0 us)
Async XLA Ops:
  8.0 248.5 %all-reduce.4.cloned.1.call-start = ((), (), s32[]{:S(2)}) async-start(), calls=%async_computation.1 | async-start | bytes 2097152 | tf_op jit(solution)/shard_map/psum | solution.py:1629
  118.8 3.4 %copy-start = (bf16[1024,1024]{1,0:T(8,128)(2,1)S(1)}, bf16[1024,1024]{1,0:T(8,128)(2,1)}, u32[]{:S(2)}) copy-start(bf16[1024,1024]{1,0:T(8,128)(2,1)} %get-tuple-element.70.refs_8_) | copy-start | bytes 6291460
  118.8 3.4 %copy-start.2 = (bf16[1024,512]{1,0:T(8,128)(2,1)S(1)}, bf16[1024,512]{1,0:T(8,128)(2,1)}, u32[]{:S(2)}) copy-start(bf16[1024,512]{1,0:T(8,128)(2,1)} %get-tuple-element.71.refs_11_) | copy-start | bytes 3145732
  122.2 1.6 copy-start.3
  122.2 1.6 copy-start.4
  123.8 2.6 copy-start.1
  128.7 127.8 %reduce-scatter.2.cloned.1.call-start = ((), (), s32[]{:S(2)}) async-start(), calls=%async_computation.2 | async-start | bytes 2621440 | tf_op jit(solution)/shard_map/reduce_scatter | solution.py:1630
Sparse Core Ops, SparseCore 0:
  128.8 89.2 all-reduce.3
Sparse Core Ops, SparseCore 1:
  131.9 30.4 reduce-scatter.1

commit v6 on v5

--- a/solution.py
+++ b/solution.py
@@ -542,6 +542,7 @@
 
 ENDS_UNROLL = 4
 SCAN_UNROLL = 4
+BACK_UNROLL = 8
 
 
 def scan_specs(tokens, ch, nstate, count):
@@ -894,7 +895,7 @@
 
     zero = jnp.zeros((8, 128), F32)
     init = (tuple(lin[0, i, :, cut(d)] for d, i in keys), (zero,) * size)
-    passed, sums = lax.fori_loop(0, steps, backward, init, unroll=SCAN_UNROLL)
+    passed, sums = lax.fori_loop(0, steps, backward, init, unroll=BACK_UNROLL)
     for n, (d, i) in enumerate(keys):
         line = jnp.sum(sums[n] * rates[n], axis=0, keepdims=True) * LN2
         at_ = pl.ds(j * count + i, 1)

time: 272 us -> 272 us (level)
  no operation moved by 1% of the time
where the time goes in v6:
time: 272 us; the launch traced here: 270 us
  Pallas kernels  235 us (86%)
  between operations  15.6 us (6%)
  matrix products  9.85 us (4%)
  local copies, waits for them, and re-layouts  5.6 us (2%)
  other arithmetic  3.27 us (1%)
    pallas_call x1, Pallas kernels, post(): pl.pallas_call(functools.partial(post_kernel, nf, ns, nq, rd, rank, nstat...  93.2 us
    pallas_call x1, Pallas kernels, front(): pl.pallas_call(functools.partial(front_kernel, nf, ns, rd, rank, nstate,...  56.3 us
    pallas_call x1, Pallas kernels, middle(): pl.pallas_call(functools.partial(mid_kernel, nf, ns, reach, count, rank,...  46.2 us
    pallas_call x1, Pallas kernels, scan_backward(): pl.pallas_call(functools.partial(backward_kernel, count, groups, rank, ns...  32.6 us
    dot_general x3, matrix products, rows_inner(): lax.dot_general(left, right, (((0,), (0,)), ((), ())), preferred_element_...  7.22 us
    pallas_call x1, Pallas kernels, last(): pl.pallas_call(functools.partial(last_kernel, ns, nf, nq, ni, rank, nstat...  7.16 us
  transfers between devices with their start and end apart: 2, of which 0 were waited for; matrix products, arithmetic and copies ran while one was open for 0% of the time, Pallas kernels for 47%

profile of v6, /device:TPU:0, one launch (start us, length us, event | category | flops | bytes accessed | tf_op | source)
XLA Modules:
  0.0 270.5 jit_solution(15907739380255244614)
XLA Ops:
  8.0 0.0 all-reduce.4.cloned.1.call-start
  8.1 0.7 convert_element_type.25
  8.7 0.7 bitcast_convert_fusion
  9.4 0.7 copy.25
  10.1 0.7 copy.26
  10.7 0.7 copy.27
  11.4 0.7 concatenate.20
  12.1 0.6 convert_bitcast_fusion.refs_4_.refs_6_.refs_14_
  12.7 0.7 fusion.7
  13.5 0.6 copy.31
  14.1 1.6 pad.9.refs_5_.refs_15_
  15.7 0.6 select_maximum_fusion.refs_3_
  16.3 56.3 %front.1 = (bf16[1024,1024]{1,0:T(8,128)(2,1)}, bf16[1024,1024]{1,0:T(8,128)(2,1)}, f32[4,1048,128]{2,1,0:T(8,128)}, f32[4,1024,128]{2,1,0:T(8,128)}, f32[4,1024...) custom-call(bf16[1,256,1024]{2,1,0:T(8,128)(2,1)} %refs_0_.1, ...), custom_call_target="tpu_custom_call" | custom-call | tf_op jit(solution)/shard_map/front/pallas_call | solution.py:501
  72.6 46.2 %middle.1 = (bf16[1024,512]{1,0:T(8,128)(2,1)}, bf16[1024,512]{1,0:T(8,128)(2,1)}, f32[4,128,16,8,128]{4,3,2,1,0:T(8,128)}, f32[1024,128]{1,0:T(8,128)}, f32[1,16,8,512]{3,2,1,0:T(8,128)}) custom-call(f32[4,1024,128]{2,1,0:T(8,128)} %get-tuple-element.60.refs_0_.step.refs_3_, f32[4,1024,128]{2,1,0:T(8,128)} %get-tuple-element.61.refs_1_.mix.refs_2_, ...), custom_call_target="tpu_custom_call" | custom-call | tf_op jit(solution)/shard_map/middle/pallas_call | solution.py:809
  118.8 0.0 copy-start
  118.8 0.0 copy-start.2
  118.8 3.4 %convolution_convert_fusion.2 = bf16[1024,256]{1,0:T(8,128)(2,1)} fusion(bf16[1024,1024]{1,0:T(8,128)(2,1)} %get-tuple-element.70.refs_8_, bf16[1024,512]{1,0:T(8,128)(2,1)} %get-tuple-element.71.refs_11_), kind=kOutput, calls=%fused_computation.2 | convolution fusion | flops 537133056 | bytes 3145728 | tf_op jit(solution)/shard_map/dot_general | solution.py:1554
  122.2 0.0 copy-done
  122.2 0.0 copy-done.2
  122.2 0.0 copy-start.3
  122.2 0.0 copy-start.4
  122.3 1.6 convolution_convert_fusion.3
  123.8 0.0 copy-done.3
  123.8 0.0 copy-done.4
  123.8 0.0 copy-start.1
  123.8 2.6 convolution_convert_fusion
  126.5 0.0 copy-done.1
  126.5 2.2 convolution_convert_fusion.1
  128.7 0.0 all-reduce.4.cloned.1.call-update
  128.7 0.0 reduce-scatter.2.cloned.1.call-start
  128.8 0.5 reduce-scatter.2.cloned.1.call-update
  129.3 0.6 reshape.72.rate
  129.9 32.6 %scan_backward.1 = (f32[4,1024,128]{2,1,0:T(8,128)}, f32[4,1024,128]{2,1,0:T(8,128)}, f32[1024,128]{1,0:T(8,128)}, f32[4,16,128]{2,1,0:T(8,128)}) custom-call(f32[4,1024,128]{2,1,0:T(8,128)} %get-tuple-element.60.refs_0_.step.refs_3_, f32[4,1024,128]{2,1,0:T(8,128)} %get-tuple-element.61.refs_1_.mix.refs_2_, ...), custom_call_target="tpu_custom_call" | custom-call | flops 100663296 | bytes 33554432 | tf_op jit(solution)/shard_map/scan_backward/pallas_call | solution.py:920
  162.6 93.2 %post.1 = (f32[256,1024]{1,0:T(8,128)}, f32[1,1024]{1,0:T(1,128)}, f32[896,128]{1,0:T(8,128)}, bf16[2,4,4,32,256]{4,3,2,1,0:T(8,128)(2,1)}, bf16[2,4,4,32,256]{4...) custom-call(f32[4,1024,128]{2,1,0:T(8,128)} %get-tuple-element.75.refs_0_, ...), custom_call_target="tpu_custom_call" | custom-call | tf_op jit(solution)/shard_map/post/pallas_call | solution.py:1461
  255.8 0.0 all-reduce.4.cloned.1.call-done.refs_4_
  255.8 0.0 reduce-scatter.2.cloned.1.call-done.refs_9_
  255.8 7.2 %last.1 = (bf16[256,1024]{1,0:T(8,128)(2,1)}, f32[256,1024]{1,0:T(8,128)}, f32[256,4096]{1,0:T(8,128)}, f32[4,512]{1,0:T(4,128)}, f32[96,512]{1,0:T(8,128)}, /*i...) custom-call(bf16[2,4,4,32,256]{4,3,2,1,0:T(8,128)(2,1)} %get-tuple-e, ...), custom_call_target="tpu_custom_call" | custom-call | tf_op jit(solution)/shard_map/last/pallas_call | solution.py:1529
  (3 shorter events, 0.0 us)
Async XLA Ops:
  8.0 247.8 %all-reduce.4.cloned.1.call-start = ((), (), s32[]{:S(2)}) async-start(), calls=%async_computation.1 | async-start | bytes 2097152 | tf_op jit(solution)/shard_map/psum | solution.py:1630
  118.8 3.4 %copy-start = (bf16[1024,1024]{1,0:T(8,128)(2,1)S(1)}, bf16[1024,1024]{1,0:T(8,128)(2,1)}, u32[]{:S(2)}) copy-start(bf16[1024,1024]{1,0:T(8,128)(2,1)} %get-tuple-element.70.refs_8_) | copy-start | bytes 6291460
  118.8 3.4 %copy-start.2 = (bf16[1024,512]{1,0:T(8,128)(2,1)S(1)}, bf16[1024,512]{1,0:T(8,128)(2,1)}, u32[]{:S(2)}) copy-start(bf16[1024,512]{1,0:T(8,128)(2,1)} %get-tuple-element.71.refs_11_) | copy-start | bytes 3145732
  122.2 1.6 copy-start.3
  122.2 1.6 copy-start.4
  123.8 2.6 copy-start.1
  128.7 127.1 %reduce-scatter.2.cloned.1.call-start = ((), (), s32[]{:S(2)}) async-start(), calls=%async_computation.2 | async-start | bytes 2621440 | tf_op jit(solution)/shard_map/reduce_scatter | solution.py:1631
Sparse Core Ops, SparseCore 0:
  128.8 91.6 all-reduce.3
Sparse Core Ops, SparseCore 1:
  131.9 30.4 reduce-scatter.1
